TPU v7x, 256 devices: a whole 4x4x8 slice. The times are simulated.
256 devices in a mesh: grp: 16 (over x_hi, z), brick: 16 (over y, x_lo, core).
Axes of the slice: x: 4 (x_hi: 2, x_lo: 2; x = x_hi * 2 + x_lo), y: 4, z: 8, core: 2. Of those that a mesh axis runs over, the one named last changes fastest.
Arguments:
- deformation_vector: float32 [3, 64, 256, 256], P(None, 'grp', 'brick'), may hold values from -4 to 4
- applied_traction: float32 [3, 64, 256, 256], P(None, 'grp', 'brick'), may hold values from 4 to 16
- heat_level: float32 [64, 256, 256], P('grp', 'brick'), may hold values from -6 to 6
- stiffness_main_terms: float32 [3, 64, 256, 256], P(None, 'grp', 'brick'), may hold values from 8 to 10
- stiffness_cross_terms: float32 [3, 64, 256, 256], P(None, 'grp', 'brick'), may hold values from -0.8 to 0.8
- normal_clearance: float32 [64, 256, 256], P('grp', 'brick'), may hold values from -0.5 to 1
- touching_flag: int32 [64, 256, 256], P('grp', 'brick'), may hold values 0 or 1
- clipped_normal_flag: int32 [64, 256, 256], P('grp', 'brick'), may hold values 0 or 1
Outputs:
- moved: float32 [3, 64, 256, 256], P(None, 'grp', 'brick')
- residual: float32 [3, 64, 256, 256], P(None, 'grp', 'brick')
All inputs are finite; a program needn't handle non-finite values. No bound on the sum of `touching_flag` or of `clipped_normal_flag` on one device may be relied on, other than what follows from the above.
Results may differ from a plain program's by a relative error of at most 0.00002.
Values sent between devices are 32-bit elements; how exact they have to be, the bound alone decides.
No kernel may reach another device: no remote copies, remote signals or barrier semaphores. Data moves between devices by JAX's collectives and lax.ppermute only.
A program may use at most 128 MiB of HBM per device.

v0:
```python
import jax
import jax.numpy as jnp
from jax import lax
from jax.sharding import PartitionSpec as P

OMEGA = 0.6
FREE = 1000.0


def padded(x, sides, width):
    edges = {}
    for axis, dim in sides:
        size, length = (lax.axis_size(axis), x.shape[dim])
        up = [(i, (i + 1) % size) for i in range(size - 1)]
        last = lax.slice_in_dim(x, length - width, length, axis=dim)
        first = lax.slice_in_dim(x, 0, width, axis=dim)
        edges[dim] = (
            lax.ppermute(last, axis, up),
            lax.ppermute(first, axis, [(b, a) for a, b in up]),
        )
    done = []
    for _, dim in sides:
        low, high = edges[dim]
        around = [(width, width) if d in done else (0, 0) for d in range(x.ndim)]
        x = jnp.concatenate([jnp.pad(low, around), x, jnp.pad(high, around)], axis=dim)
        done.append(dim)
    return x


def block_times(diag, off, field):
    a, b, c = (diag[0], diag[1], diag[2])
    d, e, f = (off[0], off[1], off[2])
    return jnp.stack(
        [
            a * field[0] + d * field[1] + f * field[2],
            d * field[0] + b * field[1] + e * field[2],
            f * field[0] + e * field[1] + c * field[2],
        ]
    )


def inverse_entries(diag, off):
    a, b, c = (diag[0], diag[1], diag[2])
    d, e, f = (off[0], off[1], off[2])
    i00 = b * c - e * e
    i11 = a * c - f * f
    i22 = a * b - d * d
    i01 = f * e - d * c
    i12 = d * f - a * e
    i02 = d * e - b * f
    scale = 1.0 / (a * i00 + d * i01 + f * i02)
    return jnp.stack([i00 * scale, i11 * scale, i22 * scale, i01 * scale, i12 * scale, i02 * scale])


def inverse_times(inv, rest):
    return jnp.stack(
        [
            inv[0] * rest[0] + inv[3] * rest[1] + inv[5] * rest[2],
            inv[3] * rest[0] + inv[1] * rest[1] + inv[4] * rest[2],
            inv[5] * rest[0] + inv[4] * rest[1] + inv[2] * rest[2],
        ]
    )


def operate_ext(ext, diag, off):
    inner = ext[:, 1:-1, 1:-1, :]
    deeper = jnp.pad(inner, ((0, 0), (0, 0), (0, 0), (1, 1)))
    beside = ext[:, 2:, 1:-1, :] + ext[:, :-2, 1:-1, :]
    beside = beside + ext[:, 1:-1, 2:, :] + ext[:, 1:-1, :-2, :]
    beside = beside + deeper[:, :, :, 2:] + deeper[:, :, :, :-2]
    return block_times(diag, off, inner) - beside


def project(field, obstacle):
    return jnp.concatenate([jnp.minimum(field[0], obstacle)[None], field[1:]], 0)


def sweep_ext(ext, force, diag, off, inv, obstacle):
    rest = force - operate_ext(ext, diag, off)
    return project(ext[:, 1:-1, 1:-1, :] + OMEGA * inverse_times(inv, rest), obstacle)


def first_sweep(force, inv, obstacle):
    return project(OMEGA * inverse_times(inv, force), obstacle)


def fine_edges(field):
    return padded(field, (("grp", 1), ("brick", 2)), 1)


def middle_edges(field):
    return padded(field, (("grp", 1), ("brick", 2)), 1)


def grouped(x):
    s = x.shape
    return x.reshape(s[:-3] + (s[-3] // 2, 2, s[-2] // 2, 2, s[-1] // 2, 2))


def group_sum(x):
    return jnp.sum(grouped(x), axis=(-5, -3, -1))


def group_min(x):
    return jnp.min(grouped(x), axis=(-5, -3, -1))


def spread(x):
    return jnp.repeat(jnp.repeat(jnp.repeat(x, 2, axis=-3), 2, axis=-2), 2, axis=-1)


def local(
    deformation_vector,
    applied_traction,
    heat_level,
    stiffness_main_terms,
    stiffness_cross_terms,
    normal_clearance,
    touching_flag,
    clipped_normal_flag,
):
    joined_tensors = jnp.concatenate([deformation_vector, heat_level[None]], 0)
    ext = padded(joined_tensors, (("grp", 1), ("brick", 2)), 1)
    heating_traction = ext[3]
    heat_deep = jnp.pad(heating_traction[1:-1, 1:-1, :], ((0, 0), (0, 0), (1, 1)))
    drift = jnp.stack(
        [
            heating_traction[2:, 1:-1, :] - heating_traction[:-2, 1:-1, :],
            heating_traction[1:-1, 2:, :] - heating_traction[1:-1, :-2, :],
            heat_deep[:, :, 2:] - heat_deep[:, :, :-2],
        ]
    )
    force = applied_traction - drift
    inv1 = inverse_entries(stiffness_main_terms, stiffness_cross_terms)
    obstacle1 = jnp.where(touching_flag == 1, normal_clearance, FREE)
    field = sweep_ext(ext[:3], force, stiffness_main_terms, stiffness_cross_terms, inv1, obstacle1)
    field = sweep_ext(
        fine_edges(field), force, stiffness_main_terms, stiffness_cross_terms, inv1, obstacle1
    )
    rest = force - operate_ext(fine_edges(field), stiffness_main_terms, stiffness_cross_terms)
    rest = jnp.concatenate([jnp.where(clipped_normal_flag == 1, 0.0, rest[0])[None], rest[1:]], 0)
    force2 = 0.25 * group_sum(rest)
    diag2 = 0.125 * group_sum(stiffness_main_terms)
    off2 = 0.125 * group_sum(stiffness_cross_terms)
    allowed = (touching_flag == 1) & (clipped_normal_flag == 0)
    obstacle2 = group_min(jnp.where(allowed, normal_clearance - field[0], FREE))
    inv2 = inverse_entries(diag2, off2)
    middle = first_sweep(force2, inv2, obstacle2)
    middle = sweep_ext(middle_edges(middle), force2, diag2, off2, inv2, obstacle2)
    force3 = 0.25 * group_sum(force2 - operate_ext(middle_edges(middle), diag2, off2))
    diag3 = 0.125 * group_sum(diag2)
    off3 = 0.125 * group_sum(off2)
    obstacle3 = group_min(obstacle2 - middle[0])
    inv3 = inverse_entries(diag3, off3)
    opening = first_sweep(force3, inv3, obstacle3)
    rim = padded(opening, (("grp", 1), ("brick", 2)), 1)
    lowest = sweep_ext(rim, force3, diag3, off3, inv3, obstacle3)
    middle = middle + spread(lowest)
    middle = sweep_ext(middle_edges(middle), force2, diag2, off2, inv2, obstacle2)
    middle = sweep_ext(middle_edges(middle), force2, diag2, off2, inv2, obstacle2)
    correction = spread(middle)
    correction = jnp.concatenate(
        [jnp.where(clipped_normal_flag == 1, 0.0, correction[0])[None], correction[1:]], 0
    )
    field = field + correction
    field = sweep_ext(
        fine_edges(field), force, stiffness_main_terms, stiffness_cross_terms, inv1, obstacle1
    )
    field = sweep_ext(
        fine_edges(field), force, stiffness_main_terms, stiffness_cross_terms, inv1, obstacle1
    )
    last = padded(field, (("grp", 1), ("brick", 2)), 1)
    residual = force - operate_ext(last, stiffness_main_terms, stiffness_cross_terms)
    return (field, residual)


def solution(mesh):
    return jax.shard_map(
        local,
        mesh=mesh,
        in_specs=(
            P(None, "grp", "brick", None),
            P(None, "grp", "brick", None),
            P("grp", "brick", None),
            P(None, "grp", "brick", None),
            P(None, "grp", "brick", None),
            P("grp", "brick", None),
            P("grp", "brick", None),
            P("grp", "brick", None),
        ),
        out_specs=(P(None, "grp", "brick", None), P(None, "grp", "brick", None)),
        check_vma=False,
    )
```

profile of v0, /device:TPU:248, one launch (start us, length us, event | category | flops | bytes accessed | tf_op | source)
XLA Modules:
  0.0 271.6 jit_solution(2094102740378730935)
XLA Ops:
  3.7 4.5 %collective-permute-start.3 = (f32[4,4,1,256]{3,1,2,0:T(4,128)S(1)}, f32[4,4,1,256]{3,1,2,0:T(4,128)S(1)}, u32[]{:S(2)}, u32[]{:S(2)}) collective-permute-start(f32[4,4,1,256]{3,1,2,0:T(4,128)S(1)} %copy.494), channel_id=1, source_target_pairs={{1,0},{2,1},{3,2},{4,3},{5,4},{6,5},{7,6},{8,7},{9,8},{10,9},{11,1... | collective-permute-start | bytes 49160 | tf_op jit(solution)/shard_map/ppermute | solution.py:19
  11.0 3.9 %collective-permute-start.2 = (f32[4,1,16,256]{3,2,1,0:T(8,128)S(1)}, f32[4,1,16,256]{3,2,1,0:T(8,128)S(1)}, u32[]{:S(2)}, u32[]{:S(2)}) collective-permute-start(f32[4,1,16,256]{3,2,1,0:T(8,128)S(1)} %get-tuple-element.89), channel_id=1, source_target_pairs={{16,0},{32,16},{48,32},{64,48},{80,64},{96,80},{112,96},{128,112},... | collective-permute-start | bytes 196616 | tf_op jit(solution)/shard_map/ppermute | solution.py:19
  15.0 14.8 %reshape.516 = f32[3,2,2,8,2,128,2]{6,5,4,3,2,1,0:T(8,128)} reshape(f32[3,4,16,256]{3,2,1,0:T(8,128)} %param.11) | data formatting | bytes 393216 | tf_op jit(solution)/shard_map/reshape | solution.py:97
  29.8 14.0 %reshape.517 = f32[3,2,2,8,2,128,2]{6,5,4,3,2,1,0:T(8,128)} reshape(f32[3,4,16,256]{3,2,1,0:T(8,128)S(1)} %copy-done) | data formatting | bytes 393216 | tf_op jit(solution)/shard_map/reshape | solution.py:97
  43.8 5.5 %reduce_sum.60 = f32[3,2,8,128]{3,2,1,0:T(8,128)S(1)} reduce(f32[3,2,2,8,2,128,2]{6,5,4,3,2,1,0:T(8,128)} %reshape.516, f32[]{:T(128)} %constant.10.clone.1), dimensions={2,4,6}, to_apply=%region_0.1 | reduce | flops 43008 | bytes 221188 | tf_op jit(solution)/shard_map/reduce_sum | solution.py:101
  49.4 5.5 %reduce_sum.61 = f32[3,2,8,128]{3,2,1,0:T(8,128)S(1)} reduce(f32[3,2,2,8,2,128,2]{6,5,4,3,2,1,0:T(8,128)} %reshape.517, f32[]{:T(128)} %constant.10.clone.1), dimensions={2,4,6}, to_apply=%region_1.2 | reduce | flops 43008 | bytes 221188 | tf_op jit(solution)/shard_map/reduce_sum | solution.py:101
  60.2 4.5 %collective-permute-start.6 = (f32[3,4,1,256]{3,1,2,0:T(4,128)S(1)}, f32[3,4,1,256]{3,1,2,0:T(4,128)S(1)}, u32[]{:S(2)}, u32[]{:S(2)}) collective-permute-start(f32[3,4,1,256]{3,1,2,0:T(4,128)S(1)} %copy.464), channel_id=1, source_target_pairs={{1,0},{2,1},{3,2},{4,3},{5,4},{6,5},{7,6},{8,7},{9,8},{10,9},{11,1... | collective-permute-start | bytes 36872 | tf_op jit(solution)/shard_map/ppermute | solution.py:19
  64.8 5.5 %collective-permute-start.5 = (f32[3,1,16,256]{3,2,1,0:T(8,128)S(1)}, f32[3,1,16,256]{3,2,1,0:T(8,128)S(1)}, u32[]{:S(2)}, u32[]{:S(2)}) collective-permute-start(f32[3,1,16,256]{3,2,1,0:T(8,128)S(1)} %get-tuple-element.108), channel_id=1, source_target_pairs={{0,16},{16,32},{32,48},{48,64},{64,80},{80,96},{96,112},{112,128},... | collective-permute-start | bytes 147464 | tf_op jit(solution)/shard_map/ppermute | solution.py:18
  72.3 7.6 %collective-permute-done.4 = f32[3,1,16,256]{3,2,1,0:T(8,128)S(1)} collective-permute-done((f32[3,1,16,256]{3,2,1,0:T(8,128)S(1)}, f32[3,1,16,256]{3,2,1,0:T(8,128)S(1)}, u32[]{:S(2)}, u32[]{:S(2)}) %collective-permute-start.4) | collective-permute-done | bytes 49184 | tf_op jit(solution)/shard_map/ppermute | solution.py:19
  80.4 1.9 collective-permute-start.11
  82.3 4.5 %collective-permute-start.10 = (f32[3,4,1,256]{3,1,2,0:T(4,128)S(1)}, f32[3,4,1,256]{3,1,2,0:T(4,128)S(1)}, u32[]{:S(2)}, u32[]{:S(2)}) collective-permute-start(f32[3,4,1,256]{3,1,2,0:T(4,128)S(1)} %copy.468), channel_id=1, source_target_pairs={{1,0},{2,1},{3,2},{4,3},{5,4},{6,5},{7,6},{8,7},{9,8},{10,9},{11,1... | collective-permute-start | bytes 36872 | tf_op jit(solution)/shard_map/ppermute | solution.py:19
  88.8 4.1 %collective-permute-start.8 = (f32[3,1,16,256]{3,2,1,0:T(8,128)S(1)}, f32[3,1,16,256]{3,2,1,0:T(8,128)S(1)}, u32[]{:S(2)}, u32[]{:S(2)}) collective-permute-start(f32[3,1,16,256]{3,2,1,0:T(8,128)S(1)} %get-tuple-element.105), channel_id=1, source_target_pairs={{16,0},{32,16},{48,32},{64,48},{80,64},{96,80},{112,96},{128,112},... | collective-permute-start | bytes 147464 | tf_op jit(solution)/shard_map/ppermute | solution.py:19
  93.0 5.4 %collective-permute-done.8 = f32[3,1,16,256]{3,2,1,0:T(8,128)S(1)} collective-permute-done((f32[3,1,16,256]{3,2,1,0:T(8,128)S(1)}, f32[3,1,16,256]{3,2,1,0:T(8,128)S(1)}, u32[]{:S(2)}, u32[]{:S(2)}) %collective-permute-start.8) | collective-permute-done | bytes 49184 | tf_op jit(solution)/shard_map/ppermute | solution.py:19
  98.6 5.6 %concatenate.259 = f32[1,2,2,8,2,128,2]{6,5,4,3,2,1,0:T(8,128)} reshape(f32[4,16,256]{2,1,0:T(8,128)S(1)} %get-tuple-element.44) | data formatting | bytes 131072 | tf_op jit(solution)/shard_map/concatenate | solution.py:141
  104.2 2.8 %copy.472 = f32[1,2,2,8,2,128,2]{5,3,6,4,2,1,0:T(8,128)S(1)} copy(f32[1,2,2,8,2,128,2]{6,5,4,3,2,1,0:T(8,128)} %concatenate.259) | data formatting | bytes 131072 | tf_op jit(solution)/shard_map/concatenate | solution.py:141
  107.1 5.7 %reshape.518 = f32[2,2,8,2,128,2]{5,4,3,2,1,0:T(8,128)} reshape(f32[4,16,256]{2,1,0:T(8,128)S(1)} %get-tuple-element.122) | data formatting | bytes 131072 | tf_op jit(solution)/shard_map/reshape | solution.py:97
  112.7 9.8 %concatenate.260 = f32[2,2,2,8,2,128,2]{6,5,4,3,2,1,0:T(8,128)} reshape(f32[2,4,16,256]{3,2,1,0:T(8,128)S(1)} %slice.1188) | data formatting | bytes 262144 | tf_op jit(solution)/shard_map/concatenate | solution.py:141
  122.5 5.2 %copy.473 = f32[2,2,2,8,2,128,2]{5,3,6,4,2,1,0:T(8,128)S(1)} copy(f32[2,2,2,8,2,128,2]{6,5,4,3,2,1,0:T(8,128)} %concatenate.260) | data formatting | bytes 262144 | tf_op jit(solution)/shard_map/concatenate | solution.py:141
  127.8 2.5 reduce_min.23
  132.4 2.4 collective-permute-start.15
  136.7 3.9 %collective-permute-start.12 = (f32[3,1,8,128]{3,2,1,0:T(8,128)S(1)}, f32[3,1,8,128]{3,2,1,0:T(8,128)S(1)}, u32[]{:S(2)}, u32[]{:S(2)}) collective-permute-start(f32[3,1,8,128]{3,2,1,0:T(8,128)S(1)} %get-tuple-element.153), channel_id=1, source_target_pairs={{16,0},{32,16},{48,32},{64,48},{80,64},{96,80},{112,96},{128,112},... | collective-permute-start | bytes 36872 | tf_op jit(solution)/shard_map/ppermute | solution.py:19
  140.7 5.2 %collective-permute-done.12 = f32[3,1,8,128]{3,2,1,0:T(8,128)S(1)} collective-permute-done((f32[3,1,8,128]{3,2,1,0:T(8,128)S(1)}, f32[3,1,8,128]{3,2,1,0:T(8,128)S(1)}, u32[]{:S(2)}, u32[]{:S(2)}) %collective-permute-start.12) | collective-permute-done | bytes 12320 | tf_op jit(solution)/shard_map/ppermute | solution.py:19
  146.1 2.9 %collective-permute-start.18 = (f32[3,2,1,128]{3,2,1,0:T(1,128)S(1)}, f32[3,2,1,128]{3,2,1,0:T(1,128)S(1)}, u32[]{:S(2)}, u32[]{:S(2)}) collective-permute-start(f32[3,2,1,128]{3,2,1,0:T(1,128)S(1)} %get-tuple-element.146), channel_id=1, source_target_pairs={{1,0},{2,1},{3,2},{4,3},{5,4},{6,5},{7,6},{8,7},{9,8},{10,9},{11,1... | collective-permute-start | bytes 9224 | tf_op jit(solution)/shard_map/ppermute | solution.py:19
  149.0 1.9 collective-permute-start.19
  151.0 2.5 collective-permute-start.17
  153.5 3.3 %collective-permute-start.16 = (f32[3,1,8,128]{3,2,1,0:T(8,128)S(1)}, f32[3,1,8,128]{3,2,1,0:T(8,128)S(1)}, u32[]{:S(2)}, u32[]{:S(2)}) collective-permute-start(f32[3,1,8,128]{3,2,1,0:T(8,128)S(1)} %get-tuple-element.149), channel_id=1, source_target_pairs={{16,0},{32,16},{48,32},{64,48},{80,64},{96,80},{112,96},{128,112},... | collective-permute-start | bytes 36872 | tf_op jit(solution)/shard_map/ppermute | solution.py:19
  157.2 5.5 %collective-permute-done.16 = f32[3,1,8,128]{3,2,1,0:T(8,128)S(1)} collective-permute-done((f32[3,1,8,128]{3,2,1,0:T(8,128)S(1)}, f32[3,1,8,128]{3,2,1,0:T(8,128)S(1)}, u32[]{:S(2)}, u32[]{:S(2)}) %collective-permute-start.16) | collective-permute-done | bytes 12320 | tf_op jit(solution)/shard_map/ppermute | solution.py:19
  165.8 3.9 %collective-permute-start.20 = (f32[3,1,4,64]{3,2,0,1:T(4,128)S(1)}, f32[3,1,4,64]{3,2,0,1:T(4,128)S(1)}, u32[]{:S(2)}, u32[]{:S(2)}) collective-permute-start(f32[3,1,4,64]{3,2,0,1:T(4,128)S(1)} %pad_maximum_fusion.108), channel_id=1, source_target_pairs={{16,0},{32,16},{48,32},{64,48},{80,64},{96,80},{112,96},{128,112},... | collective-permute-start | bytes 9224 | tf_op jit(solution)/shard_map/ppermute | solution.py:19
  169.7 2.2 collective-permute-start.22
  171.9 2.1 collective-permute-start.23
  174.1 3.6 %collective-permute-done.23 = f32[3,1,1,64]{3,2,0,1:T(1,128)S(1)} collective-permute-done((f32[3,1,1,64]{3,2,0,1:T(1,128)S(1)}, f32[3,1,1,64]{3,2,0,1:T(1,128)S(1)}, u32[]{:S(2)}, u32[]{:S(2)}) %collective-permute-start.23) | collective-permute-done | bytes 800 | tf_op jit(solution)/shard_map/ppermute | solution.py:18
  180.1 2.4 collective-permute-start.27
  182.6 6.4 %collective-permute-start.25 = (f32[3,1,8,128]{3,2,1,0:T(8,128)S(1)}, f32[3,1,8,128]{3,2,1,0:T(8,128)S(1)}, u32[]{:S(2)}, u32[]{:S(2)}) collective-permute-start(f32[3,1,8,128]{3,2,1,0:T(8,128)S(1)} %get-tuple-element.140), channel_id=1, source_target_pairs={{0,16},{16,32},{32,48},{48,64},{64,80},{80,96},{96,112},{112,128},... | collective-permute-start | bytes 36872 | tf_op jit(solution)/shard_map/ppermute | solution.py:18
  191.0 7.2 %collective-permute-done.24 = f32[3,1,8,128]{3,2,1,0:T(8,128)S(1)} collective-permute-done((f32[3,1,8,128]{3,2,1,0:T(8,128)S(1)}, f32[3,1,8,128]{3,2,1,0:T(8,128)S(1)}, u32[]{:S(2)}, u32[]{:S(2)}) %collective-permute-start.24) | collective-permute-done | bytes 12320 | tf_op jit(solution)/shard_map/ppermute | solution.py:19
  198.4 2.0 collective-permute-start.30
  200.4 2.3 collective-permute-start.31
  202.7 2.2 collective-permute-start.29
  204.9 3.7 %collective-permute-start.28 = (f32[3,1,8,128]{3,2,1,0:T(8,128)S(1)}, f32[3,1,8,128]{3,2,1,0:T(8,128)S(1)}, u32[]{:S(2)}, u32[]{:S(2)}) collective-permute-start(f32[3,1,8,128]{3,2,1,0:T(8,128)S(1)} %get-tuple-element.137), channel_id=1, source_target_pairs={{16,0},{32,16},{48,32},{64,48},{80,64},{96,80},{112,96},{128,112},... | collective-permute-start | bytes 36872 | tf_op jit(solution)/shard_map/ppermute | solution.py:19
  208.6 5.5 %collective-permute-done.28 = f32[3,1,8,128]{3,2,1,0:T(8,128)S(1)} collective-permute-done((f32[3,1,8,128]{3,2,1,0:T(8,128)S(1)}, f32[3,1,8,128]{3,2,1,0:T(8,128)S(1)}, u32[]{:S(2)}, u32[]{:S(2)}) %collective-permute-start.28) | collective-permute-done | bytes 12320 | tf_op jit(solution)/shard_map/ppermute | solution.py:19
  217.7 4.5 %collective-permute-start.34 = (f32[3,4,1,256]{3,1,2,0:T(4,128)S(1)}, f32[3,4,1,256]{3,1,2,0:T(4,128)S(1)}, u32[]{:S(2)}, u32[]{:S(2)}) collective-permute-start(f32[3,4,1,256]{3,1,2,0:T(4,128)S(1)} %copy.480), channel_id=1, source_target_pairs={{1,0},{2,1},{3,2},{4,3},{5,4},{6,5},{7,6},{8,7},{9,8},{10,9},{11,1... | collective-permute-start | bytes 36872 | tf_op jit(solution)/shard_map/ppermute | solution.py:19
  224.2 3.9 %collective-permute-start.32 = (f32[3,1,16,256]{3,2,1,0:T(8,128)S(1)}, f32[3,1,16,256]{3,2,1,0:T(8,128)S(1)}, u32[]{:S(2)}, u32[]{:S(2)}) collective-permute-start(f32[3,1,16,256]{3,2,1,0:T(8,128)S(1)} %get-tuple-element.101), channel_id=1, source_target_pairs={{16,0},{32,16},{48,32},{64,48},{80,64},{96,80},{112,96},{128,112},... | collective-permute-start | bytes 147464 | tf_op jit(solution)/shard_map/ppermute | solution.py:19
  228.2 5.5 %collective-permute-done.32 = f32[3,1,16,256]{3,2,1,0:T(8,128)S(1)} collective-permute-done((f32[3,1,16,256]{3,2,1,0:T(8,128)S(1)}, f32[3,1,16,256]{3,2,1,0:T(8,128)S(1)}, u32[]{:S(2)}, u32[]{:S(2)}) %collective-permute-start.32) | collective-permute-done | bytes 49184 | tf_op jit(solution)/shard_map/ppermute | solution.py:19
  236.2 4.5 %collective-permute-start.38 = (f32[3,4,1,256]{3,1,2,0:T(4,128)S(1)}, f32[3,4,1,256]{3,1,2,0:T(4,128)S(1)}, u32[]{:S(2)}, u32[]{:S(2)}) collective-permute-start(f32[3,4,1,256]{3,1,2,0:T(4,128)S(1)} %copy.484), channel_id=1, source_target_pairs={{1,0},{2,1},{3,2},{4,3},{5,4},{6,5},{7,6},{8,7},{9,8},{10,9},{11,1... | collective-permute-start | bytes 36872 | tf_op jit(solution)/shard_map/ppermute | solution.py:19
  242.7 3.9 %collective-permute-start.36 = (f32[3,1,16,256]{3,2,1,0:T(8,128)S(1)}, f32[3,1,16,256]{3,2,1,0:T(8,128)S(1)}, u32[]{:S(2)}, u32[]{:S(2)}) collective-permute-start(f32[3,1,16,256]{3,2,1,0:T(8,128)S(1)} %get-tuple-element.97), channel_id=1, source_target_pairs={{16,0},{32,16},{48,32},{64,48},{80,64},{96,80},{112,96},{128,112},... | collective-permute-start | bytes 147464 | tf_op jit(solution)/shard_map/ppermute | solution.py:19
  246.7 5.5 %collective-permute-done.36 = f32[3,1,16,256]{3,2,1,0:T(8,128)S(1)} collective-permute-done((f32[3,1,16,256]{3,2,1,0:T(8,128)S(1)}, f32[3,1,16,256]{3,2,1,0:T(8,128)S(1)}, u32[]{:S(2)}, u32[]{:S(2)}) %collective-permute-start.36) | collective-permute-done | bytes 49184 | tf_op jit(solution)/shard_map/ppermute | solution.py:19
  254.7 4.5 %collective-permute-start.42 = (f32[3,4,1,256]{3,1,2,0:T(4,128)S(1)}, f32[3,4,1,256]{3,1,2,0:T(4,128)S(1)}, u32[]{:S(2)}, u32[]{:S(2)}) collective-permute-start(f32[3,4,1,256]{3,1,2,0:T(4,128)S(1)} %copy.488), channel_id=1, source_target_pairs={{1,0},{2,1},{3,2},{4,3},{5,4},{6,5},{7,6},{8,7},{9,8},{10,9},{11,1... | collective-permute-start | bytes 36872 | tf_op jit(solution)/shard_map/ppermute | solution.py:19
  261.1 3.9 %collective-permute-start.40 = (f32[3,1,16,256]{3,2,1,0:T(8,128)S(1)}, f32[3,1,16,256]{3,2,1,0:T(8,128)S(1)}, u32[]{:S(2)}, u32[]{:S(2)}) collective-permute-start(f32[3,1,16,256]{3,2,1,0:T(8,128)S(1)} %get-tuple-element.93), channel_id=1, source_target_pairs={{16,0},{32,16},{48,32},{64,48},{80,64},{96,80},{112,96},{128,112},... | collective-permute-start | bytes 147464 | tf_op jit(solution)/shard_map/ppermute | solution.py:19
  265.2 5.5 %collective-permute-done.40 = f32[3,1,16,256]{3,2,1,0:T(8,128)S(1)} collective-permute-done((f32[3,1,16,256]{3,2,1,0:T(8,128)S(1)}, f32[3,1,16,256]{3,2,1,0:T(8,128)S(1)}, u32[]{:S(2)}, u32[]{:S(2)}) %collective-permute-start.40) | collective-permute-done | bytes 49184 | tf_op jit(solution)/shard_map/ppermute | solution.py:19
  (235 shorter events, 42.4 us)
Async XLA Ops:
  0.6 29.1 %copy-start.2 = (f32[3,4,16,256]{3,2,1,0:T(8,128)S(1)}, f32[3,4,16,256]{3,2,1,0:T(8,128)}, u32[]{:S(2)}) copy-start(f32[3,4,16,256]{3,2,1,0:T(8,128)} %param.8) | copy-start | bytes 589828
  0.6 29.1 %copy-start.1 = (f32[3,4,16,256]{3,2,1,0:T(8,128)S(1)}, f32[3,4,16,256]{3,2,1,0:T(8,128)}, u32[]{:S(2)}) copy-start(f32[3,4,16,256]{3,2,1,0:T(8,128)} %param.11) | copy-start | bytes 589828
  0.7 29.1 %copy-start = (f32[3,4,16,256]{3,2,1,0:T(8,128)S(1)}, f32[3,4,16,256]{3,2,1,0:T(8,128)}, u32[]{:S(2)}) copy-start(f32[3,4,16,256]{3,2,1,0:T(8,128)} %param.12) | copy-start | bytes 589828
  1.7 55.1 %collective-permute-start = (f32[4,4,1,256]{3,1,2,0:T(4,128)S(1)}, f32[4,4,1,256]{3,1,2,0:T(4,128)S(1)}, u32[]{:S(2)}, u32[]{:S(2)}) collective-permute-start(f32[4,4,1,256]{3,1,2,0:T(4,128)S(1)} %copy.493), channel_id=1, source_target_pairs={{0,1},{1,2},{2,3},{3,4},{4,5},{5,6},{6,7},{7,8},{8,9},{9,10},{10,1... | collective-permute-start | bytes 49160 | tf_op jit(solution)/shard_map/ppermute | solution.py:18
  3.7 53.2 %collective-permute-start.3 = (f32[4,4,1,256]{3,1,2,0:T(4,128)S(1)}, f32[4,4,1,256]{3,1,2,0:T(4,128)S(1)}, u32[]{:S(2)}, u32[]{:S(2)}) collective-permute-start(f32[4,4,1,256]{3,1,2,0:T(4,128)S(1)} %copy.494), channel_id=1, source_target_pairs={{1,0},{2,1},{3,2},{4,3},{5,4},{6,5},{7,6},{8,7},{9,8},{10,9},{11,1... | collective-permute-start | bytes 49160 | tf_op jit(solution)/shard_map/ppermute | solution.py:19
  9.1 47.9 %collective-permute-start.1 = (f32[4,1,16,256]{3,2,1,0:T(8,128)S(1)}, f32[4,1,16,256]{3,2,1,0:T(8,128)S(1)}, u32[]{:S(2)}, u32[]{:S(2)}) collective-permute-start(f32[4,1,16,256]{3,2,1,0:T(8,128)S(1)} %get-tuple-element.88), channel_id=1, source_target_pairs={{0,16},{16,32},{32,48},{48,64},{64,80},{80,96},{96,112},{112,128},... | collective-permute-start | bytes 196616 | tf_op jit(solution)/shard_map/ppermute | solution.py:18
  11.0 46.0 %collective-permute-start.2 = (f32[4,1,16,256]{3,2,1,0:T(8,128)S(1)}, f32[4,1,16,256]{3,2,1,0:T(8,128)S(1)}, u32[]{:S(2)}, u32[]{:S(2)}) collective-permute-start(f32[4,1,16,256]{3,2,1,0:T(8,128)S(1)} %get-tuple-element.89), channel_id=1, source_target_pairs={{16,0},{32,16},{48,32},{64,48},{80,64},{96,80},{112,96},{128,112},... | collective-permute-start | bytes 196616 | tf_op jit(solution)/shard_map/ppermute | solution.py:19
  56.9 41.7 %copy-start.7 = (s32[4,16,256]{2,1,0:T(8,128)S(1)}, s32[4,16,256]{2,1,0:T(8,128)}, u32[]{:S(2)}) copy-start(s32[4,16,256]{2,1,0:T(8,128)} %param.15) | copy-start | bytes 196612
  58.3 14.0 %collective-permute-start.7 = (f32[3,4,1,256]{3,1,2,0:T(4,128)S(1)}, f32[3,4,1,256]{3,1,2,0:T(4,128)S(1)}, u32[]{:S(2)}, u32[]{:S(2)}) collective-permute-start(f32[3,4,1,256]{3,1,2,0:T(4,128)S(1)} %copy.466), channel_id=1, source_target_pairs={{0,1},{1,2},{2,3},{3,4},{4,5},{5,6},{6,7},{7,8},{8,9},{9,10},{10,1... | collective-permute-start | bytes 36872 | tf_op jit(solution)/shard_map/ppermute | solution.py:18
  60.2 12.1 %collective-permute-start.6 = (f32[3,4,1,256]{3,1,2,0:T(4,128)S(1)}, f32[3,4,1,256]{3,1,2,0:T(4,128)S(1)}, u32[]{:S(2)}, u32[]{:S(2)}) collective-permute-start(f32[3,4,1,256]{3,1,2,0:T(4,128)S(1)} %copy.464), channel_id=1, source_target_pairs={{1,0},{2,1},{3,2},{4,3},{5,4},{6,5},{7,6},{8,7},{9,8},{10,9},{11,1... | collective-permute-start | bytes 36872 | tf_op jit(solution)/shard_map/ppermute | solution.py:19
  64.8 7.6 %collective-permute-start.5 = (f32[3,1,16,256]{3,2,1,0:T(8,128)S(1)}, f32[3,1,16,256]{3,2,1,0:T(8,128)S(1)}, u32[]{:S(2)}, u32[]{:S(2)}) collective-permute-start(f32[3,1,16,256]{3,2,1,0:T(8,128)S(1)} %get-tuple-element.108), channel_id=1, source_target_pairs={{0,16},{16,32},{32,48},{48,64},{64,80},{80,96},{96,112},{112,128},... | collective-permute-start | bytes 147464 | tf_op jit(solution)/shard_map/ppermute | solution.py:18
  70.3 9.6 %collective-permute-start.4 = (f32[3,1,16,256]{3,2,1,0:T(8,128)S(1)}, f32[3,1,16,256]{3,2,1,0:T(8,128)S(1)}, u32[]{:S(2)}, u32[]{:S(2)}) collective-permute-start(f32[3,1,16,256]{3,2,1,0:T(8,128)S(1)} %get-tuple-element.109), channel_id=1, source_target_pairs={{16,0},{32,16},{48,32},{64,48},{80,64},{96,80},{112,96},{128,112},... | collective-permute-start | bytes 147464 | tf_op jit(solution)/shard_map/ppermute | solution.py:19
  80.4 12.5 %collective-permute-start.11 = (f32[3,4,1,256]{3,1,2,0:T(4,128)S(1)}, f32[3,4,1,256]{3,1,2,0:T(4,128)S(1)}, u32[]{:S(2)}, u32[]{:S(2)}) collective-permute-start(f32[3,4,1,256]{3,1,2,0:T(4,128)S(1)} %copy.470), channel_id=1, source_target_pairs={{0,1},{1,2},{2,3},{3,4},{4,5},{5,6},{6,7},{7,8},{8,9},{9,10},{10,1... | collective-permute-start | bytes 36872 | tf_op jit(solution)/shard_map/ppermute | solution.py:18
  82.3 10.6 %collective-permute-start.10 = (f32[3,4,1,256]{3,1,2,0:T(4,128)S(1)}, f32[3,4,1,256]{3,1,2,0:T(4,128)S(1)}, u32[]{:S(2)}, u32[]{:S(2)}) collective-permute-start(f32[3,4,1,256]{3,1,2,0:T(4,128)S(1)} %copy.468), channel_id=1, source_target_pairs={{1,0},{2,1},{3,2},{4,3},{5,4},{6,5},{7,6},{8,7},{9,8},{10,9},{11,1... | collective-permute-start | bytes 36872 | tf_op jit(solution)/shard_map/ppermute | solution.py:19
  86.9 6.1 %collective-permute-start.9 = (f32[3,1,16,256]{3,2,1,0:T(8,128)S(1)}, f32[3,1,16,256]{3,2,1,0:T(8,128)S(1)}, u32[]{:S(2)}, u32[]{:S(2)}) collective-permute-start(f32[3,1,16,256]{3,2,1,0:T(8,128)S(1)} %get-tuple-element.104), channel_id=1, source_target_pairs={{0,16},{16,32},{32,48},{48,64},{64,80},{80,96},{96,112},{112,128},... | collective-permute-start | bytes 147464 | tf_op jit(solution)/shard_map/ppermute | solution.py:18
  88.8 9.6 %collective-permute-start.8 = (f32[3,1,16,256]{3,2,1,0:T(8,128)S(1)}, f32[3,1,16,256]{3,2,1,0:T(8,128)S(1)}, u32[]{:S(2)}, u32[]{:S(2)}) collective-permute-start(f32[3,1,16,256]{3,2,1,0:T(8,128)S(1)} %get-tuple-element.105), channel_id=1, source_target_pairs={{16,0},{32,16},{48,32},{64,48},{80,64},{96,80},{112,96},{128,112},... | collective-permute-start | bytes 147464 | tf_op jit(solution)/shard_map/ppermute | solution.py:19
  130.4 10.2 %collective-permute-start.14 = (f32[3,2,1,128]{3,2,1,0:T(1,128)S(1)}, f32[3,2,1,128]{3,2,1,0:T(1,128)S(1)}, u32[]{:S(2)}, u32[]{:S(2)}) collective-permute-start(f32[3,2,1,128]{3,2,1,0:T(1,128)S(1)} %get-tuple-element.150), channel_id=1, source_target_pairs={{1,0},{2,1},{3,2},{4,3},{5,4},{6,5},{7,6},{8,7},{9,8},{10,9},{11,1... | collective-permute-start | bytes 9224 | tf_op jit(solution)/shard_map/ppermute | solution.py:19
  132.4 8.3 %collective-permute-start.15 = (f32[3,2,1,128]{3,2,1,0:T(1,128)S(1)}, f32[3,2,1,128]{3,2,1,0:T(1,128)S(1)}, u32[]{:S(2)}, u32[]{:S(2)}) collective-permute-start(f32[3,2,1,128]{3,2,1,0:T(1,128)S(1)} %get-tuple-element.151), channel_id=1, source_target_pairs={{0,1},{1,2},{2,3},{3,4},{4,5},{5,6},{6,7},{7,8},{8,9},{9,10},{10,1... | collective-permute-start | bytes 9224 | tf_op jit(solution)/shard_map/ppermute | solution.py:18
  134.8 5.9 %collective-permute-start.13 = (f32[3,1,8,128]{3,2,1,0:T(8,128)S(1)}, f32[3,1,8,128]{3,2,1,0:T(8,128)S(1)}, u32[]{:S(2)}, u32[]{:S(2)}) collective-permute-start(f32[3,1,8,128]{3,2,1,0:T(8,128)S(1)} %get-tuple-element.152), channel_id=1, source_target_pairs={{0,16},{16,32},{32,48},{48,64},{64,80},{80,96},{96,112},{112,128},... | collective-permute-start | bytes 36872 | tf_op jit(solution)/shard_map/ppermute | solution.py:18
  136.7 9.2 %collective-permute-start.12 = (f32[3,1,8,128]{3,2,1,0:T(8,128)S(1)}, f32[3,1,8,128]{3,2,1,0:T(8,128)S(1)}, u32[]{:S(2)}, u32[]{:S(2)}) collective-permute-start(f32[3,1,8,128]{3,2,1,0:T(8,128)S(1)} %get-tuple-element.153), channel_id=1, source_target_pairs={{16,0},{32,16},{48,32},{64,48},{80,64},{96,80},{112,96},{128,112},... | collective-permute-start | bytes 36872 | tf_op jit(solution)/shard_map/ppermute | solution.py:19
  146.1 11.0 %collective-permute-start.18 = (f32[3,2,1,128]{3,2,1,0:T(1,128)S(1)}, f32[3,2,1,128]{3,2,1,0:T(1,128)S(1)}, u32[]{:S(2)}, u32[]{:S(2)}) collective-permute-start(f32[3,2,1,128]{3,2,1,0:T(1,128)S(1)} %get-tuple-element.146), channel_id=1, source_target_pairs={{1,0},{2,1},{3,2},{4,3},{5,4},{6,5},{7,6},{8,7},{9,8},{10,9},{11,1... | collective-permute-start | bytes 9224 | tf_op jit(solution)/shard_map/ppermute | solution.py:19
  149.0 8.1 %collective-permute-start.19 = (f32[3,2,1,128]{3,2,1,0:T(1,128)S(1)}, f32[3,2,1,128]{3,2,1,0:T(1,128)S(1)}, u32[]{:S(2)}, u32[]{:S(2)}) collective-permute-start(f32[3,2,1,128]{3,2,1,0:T(1,128)S(1)} %get-tuple-element.147), channel_id=1, source_target_pairs={{0,1},{1,2},{2,3},{3,4},{4,5},{5,6},{6,7},{7,8},{8,9},{9,10},{10,1... | collective-permute-start | bytes 9224 | tf_op jit(solution)/shard_map/ppermute | solution.py:18
  151.0 6.2 %collective-permute-start.17 = (f32[3,1,8,128]{3,2,1,0:T(8,128)S(1)}, f32[3,1,8,128]{3,2,1,0:T(8,128)S(1)}, u32[]{:S(2)}, u32[]{:S(2)}) collective-permute-start(f32[3,1,8,128]{3,2,1,0:T(8,128)S(1)} %get-tuple-element.148), channel_id=1, source_target_pairs={{0,16},{16,32},{32,48},{48,64},{64,80},{80,96},{96,112},{112,128},... | collective-permute-start | bytes 36872 | tf_op jit(solution)/shard_map/ppermute | solution.py:18
  153.5 9.2 %collective-permute-start.16 = (f32[3,1,8,128]{3,2,1,0:T(8,128)S(1)}, f32[3,1,8,128]{3,2,1,0:T(8,128)S(1)}, u32[]{:S(2)}, u32[]{:S(2)}) collective-permute-start(f32[3,1,8,128]{3,2,1,0:T(8,128)S(1)} %get-tuple-element.149), channel_id=1, source_target_pairs={{16,0},{32,16},{48,32},{64,48},{80,64},{96,80},{112,96},{128,112},... | collective-permute-start | bytes 36872 | tf_op jit(solution)/shard_map/ppermute | solution.py:19
  163.9 13.9 %collective-permute-start.21 = (f32[3,1,4,64]{3,2,0,1:T(4,128)S(1)}, f32[3,1,4,64]{3,2,0,1:T(4,128)S(1)}, u32[]{:S(2)}, u32[]{:S(2)}) collective-permute-start(f32[3,1,4,64]{3,2,0,1:T(4,128)S(1)} %pad_maximum_fusion.108), channel_id=1, source_target_pairs={{0,16},{16,32},{32,48},{48,64},{64,80},{80,96},{96,112},{112,128},... | collective-permute-start | bytes 9224 | tf_op jit(solution)/shard_map/ppermute | solution.py:18
  165.8 11.9 %collective-permute-start.20 = (f32[3,1,4,64]{3,2,0,1:T(4,128)S(1)}, f32[3,1,4,64]{3,2,0,1:T(4,128)S(1)}, u32[]{:S(2)}, u32[]{:S(2)}) collective-permute-start(f32[3,1,4,64]{3,2,0,1:T(4,128)S(1)} %pad_maximum_fusion.108), channel_id=1, source_target_pairs={{16,0},{32,16},{48,32},{64,48},{80,64},{96,80},{112,96},{128,112},... | collective-permute-start | bytes 9224 | tf_op jit(solution)/shard_map/ppermute | solution.py:19
  169.7 4.4 %collective-permute-start.22 = (f32[3,1,1,64]{3,2,0,1:T(1,128)S(1)}, f32[3,1,1,64]{3,2,0,1:T(1,128)S(1)}, u32[]{:S(2)}, u32[]{:S(2)}) collective-permute-start(f32[3,1,1,64]{3,2,0,1:T(1,128)S(1)} %get-tuple-element.159), channel_id=1, source_target_pairs={{1,0},{2,1},{3,2},{4,3},{5,4},{6,5},{7,6},{8,7},{9,8},{10,9},{11,1... | collective-permute-start | bytes 2312 | tf_op jit(solution)/shard_map/ppermute | solution.py:19
  171.9 5.8 %collective-permute-start.23 = (f32[3,1,1,64]{3,2,0,1:T(1,128)S(1)}, f32[3,1,1,64]{3,2,0,1:T(1,128)S(1)}, u32[]{:S(2)}, u32[]{:S(2)}) collective-permute-start(f32[3,1,1,64]{3,2,0,1:T(1,128)S(1)} %get-tuple-element.160), channel_id=1, source_target_pairs={{0,1},{1,2},{2,3},{3,4},{4,5},{5,6},{6,7},{7,8},{8,9},{9,10},{10,1... | collective-permute-start | bytes 2312 | tf_op jit(solution)/shard_map/ppermute | solution.py:18
  178.2 12.7 %collective-permute-start.26 = (f32[3,2,1,128]{3,2,1,0:T(1,128)S(1)}, f32[3,2,1,128]{3,2,1,0:T(1,128)S(1)}, u32[]{:S(2)}, u32[]{:S(2)}) collective-permute-start(f32[3,2,1,128]{3,2,1,0:T(1,128)S(1)} %get-tuple-element.138), channel_id=1, source_target_pairs={{1,0},{2,1},{3,2},{4,3},{5,4},{6,5},{7,6},{8,7},{9,8},{10,9},{11,1... | collective-permute-start | bytes 9224 | tf_op jit(solution)/shard_map/ppermute | solution.py:19
  180.1 10.8 %collective-permute-start.27 = (f32[3,2,1,128]{3,2,1,0:T(1,128)S(1)}, f32[3,2,1,128]{3,2,1,0:T(1,128)S(1)}, u32[]{:S(2)}, u32[]{:S(2)}) collective-permute-start(f32[3,2,1,128]{3,2,1,0:T(1,128)S(1)} %get-tuple-element.139), channel_id=1, source_target_pairs={{0,1},{1,2},{2,3},{3,4},{4,5},{5,6},{6,7},{7,8},{8,9},{9,10},{10,1... | collective-permute-start | bytes 9224 | tf_op jit(solution)/shard_map/ppermute | solution.py:18
  182.6 8.4 %collective-permute-start.25 = (f32[3,1,8,128]{3,2,1,0:T(8,128)S(1)}, f32[3,1,8,128]{3,2,1,0:T(8,128)S(1)}, u32[]{:S(2)}, u32[]{:S(2)}) collective-permute-start(f32[3,1,8,128]{3,2,1,0:T(8,128)S(1)} %get-tuple-element.140), channel_id=1, source_target_pairs={{0,16},{16,32},{32,48},{48,64},{64,80},{80,96},{96,112},{112,128},... | collective-permute-start | bytes 36872 | tf_op jit(solution)/shard_map/ppermute | solution.py:18
  189.0 9.2 %collective-permute-start.24 = (f32[3,1,8,128]{3,2,1,0:T(8,128)S(1)}, f32[3,1,8,128]{3,2,1,0:T(8,128)S(1)}, u32[]{:S(2)}, u32[]{:S(2)}) collective-permute-start(f32[3,1,8,128]{3,2,1,0:T(8,128)S(1)} %get-tuple-element.141), channel_id=1, source_target_pairs={{16,0},{32,16},{48,32},{64,48},{80,64},{96,80},{112,96},{128,112},... | collective-permute-start | bytes 36872 | tf_op jit(solution)/shard_map/ppermute | solution.py:19
  198.4 10.2 %collective-permute-start.30 = (f32[3,2,1,128]{3,2,1,0:T(1,128)S(1)}, f32[3,2,1,128]{3,2,1,0:T(1,128)S(1)}, u32[]{:S(2)}, u32[]{:S(2)}) collective-permute-start(f32[3,2,1,128]{3,2,1,0:T(1,128)S(1)} %get-tuple-element.134), channel_id=1, source_target_pairs={{1,0},{2,1},{3,2},{4,3},{5,4},{6,5},{7,6},{8,7},{9,8},{10,9},{11,1... | collective-permute-start | bytes 9224 | tf_op jit(solution)/shard_map/ppermute | solution.py:19
  200.4 8.2 %collective-permute-start.31 = (f32[3,2,1,128]{3,2,1,0:T(1,128)S(1)}, f32[3,2,1,128]{3,2,1,0:T(1,128)S(1)}, u32[]{:S(2)}, u32[]{:S(2)}) collective-permute-start(f32[3,2,1,128]{3,2,1,0:T(1,128)S(1)} %get-tuple-element.135), channel_id=1, source_target_pairs={{0,1},{1,2},{2,3},{3,4},{4,5},{5,6},{6,7},{7,8},{8,9},{9,10},{10,1... | collective-permute-start | bytes 9224 | tf_op jit(solution)/shard_map/ppermute | solution.py:18
  202.7 5.9 %collective-permute-start.29 = (f32[3,1,8,128]{3,2,1,0:T(8,128)S(1)}, f32[3,1,8,128]{3,2,1,0:T(8,128)S(1)}, u32[]{:S(2)}, u32[]{:S(2)}) collective-permute-start(f32[3,1,8,128]{3,2,1,0:T(8,128)S(1)} %get-tuple-element.136), channel_id=1, source_target_pairs={{0,16},{16,32},{32,48},{48,64},{64,80},{80,96},{96,112},{112,128},... | collective-permute-start | bytes 36872 | tf_op jit(solution)/shard_map/ppermute | solution.py:18
  204.9 9.2 %collective-permute-start.28 = (f32[3,1,8,128]{3,2,1,0:T(8,128)S(1)}, f32[3,1,8,128]{3,2,1,0:T(8,128)S(1)}, u32[]{:S(2)}, u32[]{:S(2)}) collective-permute-start(f32[3,1,8,128]{3,2,1,0:T(8,128)S(1)} %get-tuple-element.137), channel_id=1, source_target_pairs={{16,0},{32,16},{48,32},{64,48},{80,64},{96,80},{112,96},{128,112},... | collective-permute-start | bytes 36872 | tf_op jit(solution)/shard_map/ppermute | solution.py:19
  215.8 12.4 %collective-permute-start.35 = (f32[3,4,1,256]{3,1,2,0:T(4,128)S(1)}, f32[3,4,1,256]{3,1,2,0:T(4,128)S(1)}, u32[]{:S(2)}, u32[]{:S(2)}) collective-permute-start(f32[3,4,1,256]{3,1,2,0:T(4,128)S(1)} %copy.482), channel_id=1, source_target_pairs={{0,1},{1,2},{2,3},{3,4},{4,5},{5,6},{6,7},{7,8},{8,9},{9,10},{10,1... | collective-permute-start | bytes 36872 | tf_op jit(solution)/shard_map/ppermute | solution.py:18
  217.7 10.5 %collective-permute-start.34 = (f32[3,4,1,256]{3,1,2,0:T(4,128)S(1)}, f32[3,4,1,256]{3,1,2,0:T(4,128)S(1)}, u32[]{:S(2)}, u32[]{:S(2)}) collective-permute-start(f32[3,4,1,256]{3,1,2,0:T(4,128)S(1)} %copy.480), channel_id=1, source_target_pairs={{1,0},{2,1},{3,2},{4,3},{5,4},{6,5},{7,6},{8,7},{9,8},{10,9},{11,1... | collective-permute-start | bytes 36872 | tf_op jit(solution)/shard_map/ppermute | solution.py:19
  222.3 6.0 %collective-permute-start.33 = (f32[3,1,16,256]{3,2,1,0:T(8,128)S(1)}, f32[3,1,16,256]{3,2,1,0:T(8,128)S(1)}, u32[]{:S(2)}, u32[]{:S(2)}) collective-permute-start(f32[3,1,16,256]{3,2,1,0:T(8,128)S(1)} %get-tuple-element.100), channel_id=1, source_target_pairs={{0,16},{16,32},{32,48},{48,64},{64,80},{80,96},{96,112},{112,128},... | collective-permute-start | bytes 147464 | tf_op jit(solution)/shard_map/ppermute | solution.py:18
  224.2 9.6 %collective-permute-start.32 = (f32[3,1,16,256]{3,2,1,0:T(8,128)S(1)}, f32[3,1,16,256]{3,2,1,0:T(8,128)S(1)}, u32[]{:S(2)}, u32[]{:S(2)}) collective-permute-start(f32[3,1,16,256]{3,2,1,0:T(8,128)S(1)} %get-tuple-element.101), channel_id=1, source_target_pairs={{16,0},{32,16},{48,32},{64,48},{80,64},{96,80},{112,96},{128,112},... | collective-permute-start | bytes 147464 | tf_op jit(solution)/shard_map/ppermute | solution.py:19
  234.3 12.4 %collective-permute-start.39 = (f32[3,4,1,256]{3,1,2,0:T(4,128)S(1)}, f32[3,4,1,256]{3,1,2,0:T(4,128)S(1)}, u32[]{:S(2)}, u32[]{:S(2)}) collective-permute-start(f32[3,4,1,256]{3,1,2,0:T(4,128)S(1)} %copy.486), channel_id=1, source_target_pairs={{0,1},{1,2},{2,3},{3,4},{4,5},{5,6},{6,7},{7,8},{8,9},{9,10},{10,1... | collective-permute-start | bytes 36872 | tf_op jit(solution)/shard_map/ppermute | solution.py:18
  236.2 10.5 %collective-permute-start.38 = (f32[3,4,1,256]{3,1,2,0:T(4,128)S(1)}, f32[3,4,1,256]{3,1,2,0:T(4,128)S(1)}, u32[]{:S(2)}, u32[]{:S(2)}) collective-permute-start(f32[3,4,1,256]{3,1,2,0:T(4,128)S(1)} %copy.484), channel_id=1, source_target_pairs={{1,0},{2,1},{3,2},{4,3},{5,4},{6,5},{7,6},{8,7},{9,8},{10,9},{11,1... | collective-permute-start | bytes 36872 | tf_op jit(solution)/shard_map/ppermute | solution.py:19
  240.7 6.0 %collective-permute-start.37 = (f32[3,1,16,256]{3,2,1,0:T(8,128)S(1)}, f32[3,1,16,256]{3,2,1,0:T(8,128)S(1)}, u32[]{:S(2)}, u32[]{:S(2)}) collective-permute-start(f32[3,1,16,256]{3,2,1,0:T(8,128)S(1)} %get-tuple-element.96), channel_id=1, source_target_pairs={{0,16},{16,32},{32,48},{48,64},{64,80},{80,96},{96,112},{112,128},... | collective-permute-start | bytes 147464 | tf_op jit(solution)/shard_map/ppermute | solution.py:18
  242.7 9.6 %collective-permute-start.36 = (f32[3,1,16,256]{3,2,1,0:T(8,128)S(1)}, f32[3,1,16,256]{3,2,1,0:T(8,128)S(1)}, u32[]{:S(2)}, u32[]{:S(2)}) collective-permute-start(f32[3,1,16,256]{3,2,1,0:T(8,128)S(1)} %get-tuple-element.97), channel_id=1, source_target_pairs={{16,0},{32,16},{48,32},{64,48},{80,64},{96,80},{112,96},{128,112},... | collective-permute-start | bytes 147464 | tf_op jit(solution)/shard_map/ppermute | solution.py:19
  252.7 12.4 %collective-permute-start.43 = (f32[3,4,1,256]{3,1,2,0:T(4,128)S(1)}, f32[3,4,1,256]{3,1,2,0:T(4,128)S(1)}, u32[]{:S(2)}, u32[]{:S(2)}) collective-permute-start(f32[3,4,1,256]{3,1,2,0:T(4,128)S(1)} %copy.490), channel_id=1, source_target_pairs={{0,1},{1,2},{2,3},{3,4},{4,5},{5,6},{6,7},{7,8},{8,9},{9,10},{10,1... | collective-permute-start | bytes 36872 | tf_op jit(solution)/shard_map/ppermute | solution.py:18
  254.7 10.5 %collective-permute-start.42 = (f32[3,4,1,256]{3,1,2,0:T(4,128)S(1)}, f32[3,4,1,256]{3,1,2,0:T(4,128)S(1)}, u32[]{:S(2)}, u32[]{:S(2)}) collective-permute-start(f32[3,4,1,256]{3,1,2,0:T(4,128)S(1)} %copy.488), channel_id=1, source_target_pairs={{1,0},{2,1},{3,2},{4,3},{5,4},{6,5},{7,6},{8,7},{9,8},{10,9},{11,1... | collective-permute-start | bytes 36872 | tf_op jit(solution)/shard_map/ppermute | solution.py:19
  259.2 6.0 %collective-permute-start.41 = (f32[3,1,16,256]{3,2,1,0:T(8,128)S(1)}, f32[3,1,16,256]{3,2,1,0:T(8,128)S(1)}, u32[]{:S(2)}, u32[]{:S(2)}) collective-permute-start(f32[3,1,16,256]{3,2,1,0:T(8,128)S(1)} %get-tuple-element.92), channel_id=1, source_target_pairs={{0,16},{16,32},{32,48},{48,64},{64,80},{80,96},{96,112},{112,128},... | collective-permute-start | bytes 147464 | tf_op jit(solution)/shard_map/ppermute | solution.py:18
  261.1 9.6 %collective-permute-start.40 = (f32[3,1,16,256]{3,2,1,0:T(8,128)S(1)}, f32[3,1,16,256]{3,2,1,0:T(8,128)S(1)}, u32[]{:S(2)}, u32[]{:S(2)}) collective-permute-start(f32[3,1,16,256]{3,2,1,0:T(8,128)S(1)} %get-tuple-element.93), channel_id=1, source_target_pairs={{16,0},{32,16},{48,32},{64,48},{80,64},{96,80},{112,96},{128,112},... | collective-permute-start | bytes 147464 | tf_op jit(solution)/shard_map/ppermute | solution.py:19
  (5 other events, 28.9 us)
where the time goes:
time: 273 us; the launch traced here: 272 us
  starting transfers between devices  129 us (47%)
  local copies, waits for them, and re-layouts  62.6 us (23%)
  waiting for transfers between devices  56.8 us (21%)
  other arithmetic  20.3 us (7%)
    ppermute x22, starting transfers between devices, padded(): lax.ppermute(first, axis, [(b, a) for a, b in up])  76.7 us
    ppermute x22, waiting for transfers between devices, padded(): lax.ppermute(first, axis, [(b, a) for a, b in up])  53.1 us
    ppermute x22, starting transfers between devices, padded(): lax.ppermute(last, axis, up)  52.8 us
    reshape x3, local copies, waits for them, and re-layouts, grouped(): return x.reshape(s[:-3] + (s[-3] // 2, 2, s[-2] // 2, 2, s[-1] // 2, 2))  34.4 us
    concatenate x4, local copies, waits for them, and re-layouts, local(): jnp.concatenate([jnp.where(clipped_normal_flag == 1, 0.0, rest[0])[None],...  23.4 us
    reduce_sum x8, other arithmetic, group_sum(): return jnp.sum(grouped(x), axis=(-5, -3, -1))  11.7 us
  transfers between devices with their start and end apart: 44, of which 10 were waited for; matrix products, arithmetic and copies ran while one was open for 16% of the time, Pallas kernels for 0%

commit v1 on v0

v1 whole, which is shorter than its diff:
```python
import jax
import jax.numpy as jnp
from jax import lax
from jax.experimental import pallas as pl
from jax.experimental.pallas import tpu as pltpu
from jax.sharding import PartitionSpec as P

OMEGA = 0.6
KEEP = 0.4
FREE = 1000.0
F32 = jnp.float32
HIGH = lax.Precision.HIGHEST
EVEN_SLOTS = (4, 5, 3, 2, 6, 7, 1, 0)


def inverse(a, b, c, d, e, f):
    i00 = b * c - e * e
    i11 = a * c - f * f
    i22 = a * b - d * d
    i01 = f * e - d * c
    i12 = d * f - a * e
    i02 = d * e - b * f
    det = a * i00 + d * i01 + f * i02
    scale = jnp.where(det == 0.0, 0.0, 1.0 / jnp.where(det == 0.0, 1.0, det))
    return [i00 * scale, i11 * scale, i22 * scale, i01 * scale, i12 * scale, i02 * scale]


def symmetric_times(m, r):
    return [
        m[0] * r[0] + m[3] * r[1] + m[5] * r[2],
        m[3] * r[0] + m[1] * r[1] + m[4] * r[2],
        m[5] * r[0] + m[4] * r[1] + m[2] * r[2],
    ]


def lanes(shape):
    return lax.broadcasted_iota(jnp.int32, shape, 1)


def rows(shape):
    return lax.broadcasted_iota(jnp.int32, shape, 0)


def beside(x, step=1):
    n, m = x.shape
    lane = lanes(x.shape)
    left = jnp.where(lane < step, 0.0, pltpu.roll(x, step, axis=1))
    right = jnp.where(lane >= m - step, 0.0, pltpu.roll(x, m - step, axis=1))
    return (left + right) + (pltpu.roll(x, step, axis=0) + pltpu.roll(x, n - step, axis=0))


def sides(g):
    return (jnp.bitwise_and(g, 1) == 0), jnp.logical_and(g > 0, g < 15)


def pack_grp(pos, disp, trac, heat, main, cross, clear, touch, clip, me, mo, kinv, obst):
    par = jnp.bitwise_and(pos[0], 1)
    obst[...] = jnp.where(touch[...] == 1, clear[...], FREE)
    for p in range(4):
        inv = inverse(main[0, p], main[1, p], main[2, p], cross[0, p], cross[1, p], cross[2, p])
        for k in range(6):
            kinv[k, p] = inv[k]
    for msg, at in ((me, 1 - par), (mo, par)):
        for c in range(3):
            msg[3 * c : 3 * c + 3] = disp[c, pl.ds(at, 3)]
        msg[9:12] = heat[pl.ds(at, 3)]
        msg[12:15] = clip[pl.ds(at, 3)].astype(F32)
        for c in range(3):
            msg[15 + 2 * c : 17 + 2 * c] = trac[c, pl.ds(2 * at, 2)]
        for k in range(6):
            msg[21 + 2 * k : 23 + 2 * k] = kinv[k, pl.ds(2 * at, 2)]
        msg[33:35] = obst[pl.ds(2 * at, 2)]


def wide_plane(own, re, ro, even, inside, base, width, p):
    if p < width:
        return jnp.where(even, jnp.where(inside, ro[base + p], 0.0), re[base + p])
    if p < width + 4:
        return own(p - width)
    q = base + p - width - 4
    return jnp.where(even, re[q], jnp.where(inside, ro[q], 0.0))


def fields(disp, heat, clip, trac, kinv, obst):
    wide = [lambda p, c=c: disp[c, p] for c in range(3)]
    wide += [lambda p: heat[p], lambda p: clip[p].astype(F32)]
    near = [lambda p, c=c: trac[c, p] for c in range(3)]
    near += [lambda p, k=k: kinv[k, p] for k in range(6)]
    near += [lambda p: obst[p]]
    return wide, near


def put(msg, t, r, x):
    n = x.shape[0]
    msg[t, r : r + n, :] = x[:, :128]
    msg[t, r + 4 : r + 4 + n, :] = x[:, 128:]


def pack_brick(pos, disp, heat, clip, trac, kinv, obst, re, ro, be, bo):
    even, inside = sides(pos[0])
    up = jnp.bitwise_and(pos[1], 1) == 0
    wide, near = fields(disp, heat, clip, trac, kinv, obst)
    for f in range(5):
        for p in range(10):
            x = wide_plane(wide[f], re, ro, even, inside, 3 * f, 3, p)
            low, high = x[0:3], x[13:16]
            put(be, f * 10 + p, 0, jnp.where(up, high, low))
            put(bo, f * 10 + p, 0, jnp.where(up, low, high))
    for f in range(10):
        for p in range(8):
            x = wide_plane(near[f], re, ro, even, inside, 15 + 2 * f, 2, p)
            low, high = x[0:2], x[14:16]
            put(be, 50 + f * 4 + p // 2, 2 * (p % 2), jnp.where(up, high, low))
            put(bo, 50 + f * 4 + p // 2, 2 * (p % 2), jnp.where(up, low, high))


def brick_rows(be, bo, up, inside, t, r, n):
    e = jnp.concatenate([be[t, r : r + n, :], be[t, r + 4 : r + 4 + n, :]], 1)
    o = jnp.concatenate([bo[t, r : r + n, :], bo[t, r + 4 : r + 4 + n, :]], 1)
    o = jnp.where(inside, o, 0.0)
    return jnp.where(up, o, e), jnp.where(up, e, o)


def smooth(v0, force, kinv, obst, v1, v2):
    def one(src, dst, shift, planes):
        def body(p, carry):
            rest = []
            for c in range(3):
                near = src[c, p] + src[c, p + 2] + beside(src[c, p + 1])
                rest.append(force[c, p + shift] + near)
            inv = [kinv[k, p + shift] for k in range(6)]
            step = symmetric_times(inv, rest)
            new = [KEEP * src[c, p + 1] + OMEGA * step[c] for c in range(3)]
            dst[0, p] = jnp.minimum(new[0], obst[p + shift])
            dst[1, p] = new[1]
            dst[2, p] = new[2]
            return carry

        lax.fori_loop(0, planes, body, 0)

    one(v0, v1, 0, 8)
    one(v1, v2, 1, 6)


def residual_plane(v2, force, main, cross, p):
    own = [v2[c, p + 1][8:24] for c in range(3)]
    mat = [main[c, p] for c in range(3)] + [cross[c, p] for c in range(3)]
    kv = symmetric_times(mat, own)
    out = []
    for c in range(3):
        near = v2[c, p, 8:24, :] + v2[c, p + 2, 8:24, :] + beside(v2[c, p + 1])[8:24]
        out.append(force[c, p + 2, 8:24, :] - (kv[c] - near))
    return out


def presmooth(
    pos, disp, heat, clip, trac, kinv, obst, main, cross, clear, touch, re, ro, be, bo,
    force_x, kinv_x, obst_x, clip_x, pre, em, om,
    v0, heat_x, v1, v2, rest, gath,
):
    even, inside = sides(pos[0])
    up, inner = sides(pos[1])
    par = jnp.bitwise_and(pos[0], 1)
    wide, near = fields(disp, heat, clip, trac, kinv, obst)
    wide_to = [lambda p, c=c: v0.at[c, p] for c in range(3)]
    wide_to += [lambda p: heat_x.at[p], lambda p: clip_x.at[p]]
    near_to = [lambda p, c=c: force_x.at[c, p] for c in range(3)]
    near_to += [lambda p, k=k: kinv_x.at[k, p] for k in range(6)]
    near_to += [lambda p: obst_x.at[p]]
    for f in range(5):
        for p in range(10):
            to = wide_to[f](p)
            to[8:24, :] = wide_plane(wide[f], re, ro, even, inside, 3 * f, 3, p)
            low, high = brick_rows(be, bo, up, inner, f * 10 + p, 0, 3)
            to[5:8, :] = low
            to[24:27, :] = high
    for f in range(10):
        for p in range(8):
            to = near_to[f](p)
            to[8:24, :] = wide_plane(near[f], re, ro, even, inside, 15 + 2 * f, 2, p)
            low, high = brick_rows(be, bo, up, inner, 50 + f * 4 + p // 2, 2 * (p % 2), 2)
            to[6:8, :] = low
            to[24:26, :] = high

    def drift(p, carry):
        h = heat_x[p + 1]
        lane = lanes(h.shape)
        right = jnp.where(lane == 255, 0.0, pltpu.roll(h, 255, axis=1))
        left = jnp.where(lane == 0, 0.0, pltpu.roll(h, 1, axis=1))
        force_x[0, p] = force_x[0, p] - (heat_x[p + 2] - heat_x[p])
        force_x[1, p] = force_x[1, p] - (pltpu.roll(h, 31, axis=0) - pltpu.roll(h, 1, axis=0))
        force_x[2, p] = force_x[2, p] - (right - left)
        return carry

    lax.fori_loop(0, 8, drift, 0)
    smooth(v0, force_x, kinv_x, obst_x, v1, v2)

    shape = (16, 256)
    first = jnp.bitwise_and(lanes(shape), 1) == 0
    for q in range(2):
        low = None
        for p in (2 * q, 2 * q + 1):
            out = residual_plane(v2, force_x, main, cross, p)
            cut = clip[p] == 1
            out[0] = jnp.where(cut, 0.0, out[0])
            gap = jnp.logical_and(touch[p] == 1, clip[p] != 1)
            room = jnp.where(gap, clear[p] - v2[0, p + 1, 8:24, :], FREE)
            part = out + [room] + [main[c, p] for c in range(3)] + [cross[c, p] for c in range(3)]
            if low is None:
                low = part
            else:
                low = [jnp.minimum(x, y) if i == 3 else x + y for i, (x, y) in enumerate(zip(low, part))]
        for i in range(10):
            x = low[i]
            if i < 3:
                x = 0.25 * x
            elif i > 3:
                x = 0.125 * x
            for h in range(2):
                rest[i, h] = x[:, 128 * h : 128 * h + 128]
            halves = []
            for h in range(2):
                a, b = rest[i, h, pl.ds(0, 8, 2), :], rest[i, h, pl.ds(1, 8, 2), :]
                halves.append(jnp.minimum(a, b) if i == 3 else a + b)
            x = jnp.concatenate(halves, 1)
            if i == 3:
                x = jnp.minimum(x, pltpu.roll(x, 255, axis=1))
                x = jnp.where(first[0:8], x, 0.0)
            gath[(2 * i + q) * 8 : (2 * i + q) * 8 + 8, :] = x
    i, j = rows((256, 128)), lanes((256, 128))
    pick = jnp.where(lax.shift_right_logical(i, 1) == j, 1.0, 0.0)
    small = jnp.dot(gath[...], pick, precision=HIGH, preferred_element_type=F32)
    small = small.reshape(20, 8, 128)
    em[0:20] = small
    om[0:20] = small
    for p in range(4):
        for c in range(3):
            pre[c, p] = v2[c, p + 1, 8:24, :]
    for msg, at in ((em, 1 - par), (om, par)):
        for c in range(3):
            for k in range(3):
                t = 20 + (c * 3 + k) * 4
                x = v2[c, at + k + 1, 8:24, :]
                msg[t] = x[:8, :128]
                msg[t + 1] = x[:8, 128:]
                msg[t + 2] = x[8:, :128]
                msg[t + 3] = x[8:, 128:]


def pre_plane(pre, e, o, even, inside, c, p):
    def tile(msg, base, k):
        t = base + (c * 3 + k) * 4
        left = jnp.concatenate([msg[t], msg[t + 2]], 0)
        right = jnp.concatenate([msg[t + 1], msg[t + 3]], 0)
        return jnp.concatenate([left, right], 1)

    if p < 3:
        return jnp.where(even, jnp.where(inside, tile(o, 40, p), 0.0), tile(e, 20, p))
    if p < 7:
        return pre[c, p - 3]
    return jnp.where(even, tile(e, 20, p - 7), jnp.where(inside, tile(o, 40, p - 7), 0.0))


def pack_coarse(pos, pre, em, e, o, e2, o2, be, bo):
    even, inside = sides(pos[0])
    up = jnp.bitwise_and(pos[1], 1) == 0
    for msg in (be, bo):
        msg[0:20] = em[0:20]
        msg[20:40] = e[0:20]
        msg[40:80] = o[0:40]
        msg[80:120] = e2[...]
        msg[120:160] = o2[...]
    for c in range(3):
        for p in range(10):
            x = pre_plane(pre, e, o, even, inside, c, p)
            low, high = x[0:3], x[13:16]
            put(be, 160 + c * 10 + p, 0, jnp.where(up, high, low))
            put(bo, 160 + c * 10 + p, 0, jnp.where(up, low, high))


def pair_spread(x, op):
    n, m = x.shape
    even = jnp.bitwise_and(lanes(x.shape), 1) == 0
    x = op(x, jnp.where(even, pltpu.roll(x, m - 1, axis=1), pltpu.roll(x, 1, axis=1)))
    even = jnp.bitwise_and(rows(x.shape), 1) == 0
    return op(x, jnp.where(even, pltpu.roll(x, n - 1, axis=0), pltpu.roll(x, 1, axis=0)))


def coarse(pos, sent, be, bo, mid2, own, g, ki, va, vb, f3, k3, o3, l3):
    par = jnp.bitwise_and(pos[0], 1)
    up, inner = sides(pos[1])
    grp = pos[0]
    for s in range(8):
        place = jnp.where(par == 0, EVEN_SLOTS[s], 7 - EVEN_SLOTS[s])
        where = grp + place - jnp.where(par == 0, 4, 3)
        real = jnp.logical_and(where >= 0, where < 16)
        for f in range(10):
            for q in range(2):
                t = s * 20 + f * 2 + q
                a = jnp.where(real, be[t], 0.0)
                b = jnp.where(jnp.logical_and(real, inner), bo[t], 0.0)
                to = g.at[f, 2 * place + q]
                to[0:8, :] = jnp.where(up, b, a)
                to[8:16, :] = jnp.where(real, sent[t], 0.0)
                to[16:24, :] = jnp.where(up, a, b)

    def start(p, carry):
        inv = inverse(*[g[4 + k, p] for k in range(6)])
        for k in range(6):
            ki[k, p] = inv[k]
        v = symmetric_times(inv, [OMEGA * g[c, p] for c in range(3)])
        va[0, p] = jnp.minimum(v[0], g[3, p])
        va[1, p] = v[1]
        va[2, p] = v[2]
        return carry

    lax.fori_loop(0, 16, start, 0)

    def sweep(src, dst):
        def body(p, carry):
            rest = []
            for c in range(3):
                near = src[c, p - 1] + src[c, p + 1] + beside(src[c, p])
                rest.append(g[c, p] + near)
            step = symmetric_times([ki[k, p] for k in range(6)], rest)
            new = [KEEP * src[c, p] + OMEGA * step[c] for c in range(3)]
            dst[0, p] = jnp.minimum(new[0], g[3, p])
            dst[1, p] = new[1]
            dst[2, p] = new[2]
            return carry

        return body

    lax.fori_loop(1, 15, sweep(va, vb), 0)

    def third(q, carry):
        total = None
        for p in (2 * q, 2 * q + 1):
            mat = [g[4 + k, p] for k in range(6)]
            kv = symmetric_times(mat, [vb[c, p] for c in range(3)])
            part = []
            for c in range(3):
                near = vb[c, p - 1] + vb[c, p + 1] + beside(vb[c, p])
                part.append(g[c, p] - (kv[c] - near))
            part += mat + [g[3, p] - vb[0, p]]
            if total is None:
                total = part
            else:
                total = [jnp.minimum(x, y) if i == 9 else x + y for i, (x, y) in enumerate(zip(total, part))]
        force = [0.25 * pair_spread(total[c], jnp.add) for c in range(3)]
        mat = [0.125 * pair_spread(total[3 + k], jnp.add) for k in range(6)]
        room = pair_spread(total[9], jnp.minimum)
        inv = inverse(*mat)
        v = symmetric_times(inv, [OMEGA * x for x in force])
        v[0] = jnp.minimum(v[0], room)
        for c in range(3):
            f3[c, q] = force[c]
            l3[c, q] = v[c]
        for k in range(6):
            k3[k, q] = inv[k]
        o3[q] = room
        return carry

    lax.fori_loop(1, 7, third, 0)

    def lowest(q, carry):
        rest = []
        for c in range(3):
            near = l3[c, q - 1] + l3[c, q + 1] + beside(l3[c, q], 2)
            rest.append(f3[c, q] + near)
        step = symmetric_times([k3[k, q] for k in range(6)], rest)
        new = [KEEP * l3[c, q] + OMEGA * step[c] for c in range(3)]
        new[0] = jnp.minimum(new[0], o3[q])
        for c in range(3):
            for p in (2 * q, 2 * q + 1):
                va[c, p] = vb[c, p] + new[c]
        return carry

    lax.fori_loop(2, 6, lowest, 0)
    lax.fori_loop(5, 11, sweep(va, vb), 0)
    lax.fori_loop(6, 10, sweep(vb, va), 0)
    for c in range(3):
        for k in range(4):
            mid2[c, k] = va[c, 6 + k][4:20]
        for k in range(2):
            own[c, k] = va[c, 8 - 2 * par + k][4:20]


def finish(
    pos, pre, e, o, be, bo, mid2, other, force_x, kinv_x, obst_x, clip_x, main, cross,
    moved, residual, v0, v1, v2, mid_x, fine,
):
    par = jnp.bitwise_and(pos[0], 1)
    even, inside = sides(pos[0])
    up, inner = sides(pos[1])
    for c in range(3):
        for p in range(10):
            to = v0.at[c, p]
            to[8:24, :] = pre_plane(pre, e, o, even, inside, c, p)
            low, high = brick_rows(be, bo, up, inner, 160 + c * 10 + p, 0, 3)
            to[5:8, :] = low
            to[24:27, :] = high
    i, j = rows((128, 256)), lanes((128, 256))
    copy = jnp.where(lax.shift_right_logical(j, 1) == i, 1.0, 0.0)
    for c in range(3):
        mid_x[c, pl.ds(2 * par, 4)] = mid2[c]
        mid_x[c, pl.ds(4 * (1 - par), 2)] = other[c]
    wide = jnp.dot(
        mid_x[...].reshape(3 * 6 * 16, 128), copy, precision=HIGH, preferred_element_type=F32
    )
    for c in range(3):
        for k in range(6):
            x = wide[(c * 6 + k) * 16 : (c * 6 + k) * 16 + 16]
            for h in range(2):
                y = x[:, 128 * h : 128 * h + 128]
                fine[h, pl.ds(0, 16, 2), :] = y
                fine[h, pl.ds(1, 16, 2), :] = y
            up2 = jnp.concatenate([fine[0], fine[1]], 1)
            for p in range(10):
                if (p + 1) // 2 == k:
                    add = jnp.where(clip_x[p] == 1.0, 0.0, up2) if c == 0 else up2
                    v0[c, p] = v0[c, p] + add
    smooth(v0, force_x, kinv_x, obst_x, v1, v2)
    for p in range(4):
        out = residual_plane(v2, force_x, main, cross, p)
        for c in range(3):
            residual[c, p] = out[c]
            moved[c, p] = v2[c, p + 1, 8:24, :]


def call(kernel, outs, scratch, *args):
    vm = pl.BlockSpec(memory_space=pltpu.VMEM)
    return pl.pallas_call(
        kernel,
        out_shape=[jax.ShapeDtypeStruct(s, F32) for s in outs],
        in_specs=[pl.BlockSpec(memory_space=pltpu.SMEM)] + [vm] * (len(args) - 1),
        out_specs=[vm] * len(outs),
        scratch_shapes=[pltpu.VMEM(s, F32) for s in scratch],
        compiler_params=pltpu.CompilerParams(vmem_limit_bytes=32 * 1024 * 1024),
    )(*args)


EVEN = [(i, i ^ 1) for i in range(16)]
ODD = [(i, (((i + 1) ^ 1) - 1) % 16) for i in range(16)]


def swap_even(x, axis):
    return lax.ppermute(x, axis, EVEN)


def swap_odd(x, axis):
    return lax.ppermute(x, axis, ODD)


def local(disp, trac, heat, main, cross, clear, touch, clip):
    pos = jnp.stack([lax.axis_index("grp"), lax.axis_index("brick")]).astype(jnp.int32)
    own = (4, 16, 256)
    me, mo, kinv, obst = call(
        pack_grp, [(35, 16, 256), (35, 16, 256), (6,) + own, own], [],
        pos, disp, trac, heat, main, cross, clear, touch, clip,
    )
    re, ro = swap_even(me, "grp"), swap_odd(mo, "grp")
    be, bo = call(
        pack_brick, [(90, 8, 128)] * 2, [],
        pos, disp, heat, clip, trac, kinv, obst, re, ro,
    )
    re_b, ro_b = swap_even(be, "brick"), swap_odd(bo, "brick")
    force_x, kinv_x, obst_x, clip_x, pre, em, om = call(
        presmooth,
        [(3, 8, 32, 256), (6, 8, 32, 256), (8, 32, 256), (10, 32, 256), (3,) + own,
         (56, 8, 128), (56, 8, 128)],
        [(3, 10, 32, 256), (10, 32, 256), (3, 8, 32, 256), (3, 6, 32, 256),
         (10, 2, 16, 128), (160, 256)],
        pos, disp, heat, clip, trac, kinv, obst, main, cross, clear, touch, re, ro, re_b, ro_b,
    )
    e = swap_even(em, "grp")
    o = swap_odd(jnp.concatenate([om[:20], e[:20], om[20:]], 0), "grp")
    e2 = swap_even(o[:40], "grp")
    o2 = swap_odd(e2, "grp")
    ce, co = call(pack_coarse, [(190, 8, 128)] * 2, [], pos, pre, em, e, o, e2, o2)
    re_c, ro_c = swap_even(ce, "brick"), swap_odd(co, "brick")
    field = (3, 16, 24, 128)
    third = (3, 8, 24, 128)
    mid2, mine = call(
        coarse,
        [(3, 4, 16, 128), (3, 2, 16, 128)],
        [(10, 16, 24, 128), (6, 16, 24, 128), field, field, third, (6, 8, 24, 128),
         (8, 24, 128), third],
        pos, ce, re_c, ro_c,
    )
    other = swap_even(mine, "grp")
    return tuple(
        call(
            finish,
            [(3,) + own, (3,) + own],
            [(3, 10, 32, 256), (3, 8, 32, 256), (3, 6, 32, 256), (3, 6, 16, 128), (2, 32, 128)],
            pos, pre, e, o, re_c, ro_c, mid2, other, force_x, kinv_x, obst_x, clip_x, main, cross,
        )
    )


def solution(mesh):
    vector, scalar = P(None, "grp", "brick", None), P("grp", "brick", None)
    return jax.shard_map(
        local,
        mesh=mesh,
        in_specs=(vector, vector, scalar, vector, vector, scalar, scalar, scalar),
        out_specs=(vector, vector),
        check_vma=False,
    )
```

time: 273 us -> 115 us (0.42)
  the two profiles are of different devices: /device:TPU:248 before, /device:TPU:0 now
where the time goes in v1:
time: 115 us; the launch traced here: 114 us
  waiting for transfers between devices  66.1 us (57%)
  starting transfers between devices  24.6 us (21%)
  Pallas kernels  15.6 us (14%)
  local copies, waits for them, and re-layouts  7.11 us (6%)
    ppermute x5, waiting for transfers between devices, swap_odd(): return lax.ppermute(x, axis, ODD)  44.5 us
    ppermute x6, waiting for transfers between devices, swap_even(): return lax.ppermute(x, axis, EVEN)  21.6 us
    ppermute x5, starting transfers between devices, swap_odd(): return lax.ppermute(x, axis, ODD)  21.4 us
    pallas_call x6, Pallas kernels, call(): pl.pallas_call(kernel, out_shape=[jax.ShapeDtypeStruct(s, F32) for s in o...  15.6 us
    unnamed x20, local copies, waits for them, and re-layouts  7.07 us
    ppermute x6, starting transfers between devices, swap_even(): return lax.ppermute(x, axis, EVEN)  3.14 us
  transfers between devices with their start and end apart: 11, of which 9 were waited for; matrix products, arithmetic and copies ran while one was open for 0% of the time, Pallas kernels for 0%

profile of v1, /device:TPU:0, one launch (start us, length us, event | category | flops | bytes accessed | tf_op | source)
XLA Modules:
  0.0 114.2 jit_solution(1618004141208218114)
XLA Ops:
  0.6 0.1 pad_add_fusion.pos
  0.7 0.0 copy-start
  0.7 0.9 copy-done
  1.6 0.0 copy-start.2
  1.6 0.9 copy-done.2
  2.6 0.0 copy-start.4
  2.6 0.9 copy-done.4
  3.5 0.0 copy-start.5
  3.5 0.9 copy-done.5
  4.4 0.0 copy-start.6
  4.4 0.8 copy-done.6
  5.3 0.0 copy-start.7
  5.3 0.8 copy-done.7
  6.1 0.0 copy-start.8
  6.1 0.8 copy-done.8
  6.9 0.0 copy-start.9
  6.9 0.8 copy-done.9
  7.8 0.0 copy-start.1
  7.8 0.7 shard_map.95
  8.5 0.3 collective-permute-start
  8.7 7.4 %collective-permute-start.1 = (f32[35,16,256]{2,1,0:T(8,128)S(1)}, f32[35,16,256]{2,1,0:T(8,128)S(1)}, u32[]{:S(2)}, u32[]{:S(2)}) collective-permute-start(f32[35,16,256]{2,1,0:T(8,128)S(1)} %get-tuple-element.22), channel_id=1, source_target_pairs={{0,240},{16,32},{32,16},{48,64},{64,48},{80,96},{96,80},{112,128},... | collective-permute-start | bytes 1720328 | tf_op jit(solution)/shard_map/ppermute | solution.py:452
  16.2 5.6 %collective-permute-done.re = f32[35,16,256]{2,1,0:T(8,128)S(1)} collective-permute-done((f32[35,16,256]{2,1,0:T(8,128)S(1)}, f32[35,16,256]{2,1,0:T(8,128)S(1)}, u32[]{:S(2)}, u32[]{:S(2)}) %collective-permute-start) | collective-permute-done | bytes 573472 | tf_op jit(solution)/shard_map/ppermute | solution.py:448
  21.7 7.1 %collective-permute-done.1.ro = f32[35,16,256]{2,1,0:T(8,128)S(1)} collective-permute-done((f32[35,16,256]{2,1,0:T(8,128)S(1)}, f32[35,16,256]{2,1,0:T(8,128)S(1)}, u32[]{:S(2)}, u32[]{:S(2)}) %collective-permute-start.1) | collective-permute-done | bytes 573472 | tf_op jit(solution)/shard_map/ppermute | solution.py:452
  28.8 0.7 shard_map.96
  29.6 0.1 collective-permute-start.2
  29.7 3.1 %collective-permute-start.3 = (f32[90,8,128]{2,1,0:T(8,128)S(1)}, f32[90,8,128]{2,1,0:T(8,128)S(1)}, u32[]{:S(2)}, u32[]{:S(2)}) collective-permute-start(f32[90,8,128]{2,1,0:T(8,128)S(1)} %get-tuple-element.24), channel_id=1, source_target_pairs={{0,15},{1,2},{2,1},{3,4},{4,3},{5,6},{6,5},{7,8},{8,7},{9,10},{10,... | collective-permute-start | bytes 1105928 | tf_op jit(solution)/shard_map/ppermute | solution.py:452
  32.8 0.0 collective-permute-done.2.be
  32.8 9.0 %collective-permute-done.3.bo = f32[90,8,128]{2,1,0:T(8,128)S(1)} collective-permute-done((f32[90,8,128]{2,1,0:T(8,128)S(1)}, f32[90,8,128]{2,1,0:T(8,128)S(1)}, u32[]{:S(2)}, u32[]{:S(2)}) %collective-permute-start.3) | collective-permute-done | bytes 368672 | tf_op jit(solution)/shard_map/ppermute | solution.py:452
  41.9 0.0 copy-done.1
  41.9 0.0 copy-done.3
  41.9 4.2 %shard_map.97 = (f32[3,8,32,256]{3,2,1,0:T(8,128)S(1)}, f32[6,8,32,256]{3,2,1,0:T(8,128)S(1)}, f32[8,32,256]{2,1,0:T(8,128)S(1)}, f32[10,32,256]{2,1,0:T(8,128)S...) custom-call(s32[2]{0:T(128)S(1)} %pad_add_fusion.pos, ...), custom_call_target="tpu_custom_call" | custom-call | tf_op jit(solution)/shard_map/pallas_call | solution.py:433
  46.1 0.1 collective-permute-start.4
  46.2 6.6 %collective-permute-done.4.e = f32[56,8,128]{2,1,0:T(8,128)S(1)} collective-permute-done((f32[56,8,128]{2,1,0:T(8,128)S(1)}, f32[56,8,128]{2,1,0:T(8,128)S(1)}, u32[]{:S(2)}, u32[]{:S(2)}) %collective-permute-start.4) | collective-permute-done | bytes 229408 | tf_op jit(solution)/shard_map/ppermute | solution.py:448
  52.9 5.4 %collective-permute-start.5 = (f32[76,8,128]{2,1,0:T(8,128)S(1)}, f32[76,8,128]{2,1,0:T(8,128)S(1)}, u32[]{:S(2)}, u32[]{:S(2)}) collective-permute-start(f32[76,8,128]{2,1,0:T(8,128)S(1)} %pad_maximum_fusion), channel_id=1, source_target_pairs={{0,240},{16,32},{32,16},{48,64},{64,48},{80,96},{96,80},{112,128},... | collective-permute-start | bytes 933896 | tf_op jit(solution)/shard_map/ppermute | solution.py:452
  58.3 5.8 %collective-permute-done.5.o = f32[76,8,128]{2,1,0:T(8,128)S(1)} collective-permute-done((f32[76,8,128]{2,1,0:T(8,128)S(1)}, f32[76,8,128]{2,1,0:T(8,128)S(1)}, u32[]{:S(2)}, u32[]{:S(2)}) %collective-permute-start.5) | collective-permute-done | bytes 311328 | tf_op jit(solution)/shard_map/ppermute | solution.py:452
  64.1 0.1 collective-permute-start.6
  64.2 5.3 %collective-permute-done.6.e2 = f32[40,8,128]{2,1,0:T(8,128)S(1)} collective-permute-done((f32[40,8,128]{2,1,0:T(8,128)S(1)}, f32[40,8,128]{2,1,0:T(8,128)S(1)}, u32[]{:S(2)}, u32[]{:S(2)}) %collective-permute-start.6) | collective-permute-done | bytes 163872 | tf_op jit(solution)/shard_map/ppermute | solution.py:448
  69.5 5.4 %collective-permute-start.7 = (f32[40,8,128]{2,1,0:T(8,128)S(1)}, f32[40,8,128]{2,1,0:T(8,128)S(1)}, u32[]{:S(2)}, u32[]{:S(2)}) collective-permute-start(f32[40,8,128]{2,1,0:T(8,128)S(1)} %collective-permute-done.6.e2), channel_id=1, source_target_pairs={{0,240},{16,32},{32,16},{48,64},{64,48},{80,96},{96,80},{112,128},... | collective-permute-start | bytes 491528 | tf_op jit(solution)/shard_map/ppermute | solution.py:452
  74.9 3.6 %collective-permute-done.7.o2 = f32[40,8,128]{2,1,0:T(8,128)S(1)} collective-permute-done((f32[40,8,128]{2,1,0:T(8,128)S(1)}, f32[40,8,128]{2,1,0:T(8,128)S(1)}, u32[]{:S(2)}, u32[]{:S(2)}) %collective-permute-start.7) | collective-permute-done | bytes 163872 | tf_op jit(solution)/shard_map/ppermute | solution.py:452
  78.5 0.7 shard_map.98
  79.1 0.1 collective-permute-start.9
  79.2 2.5 %collective-permute-start.8 = (f32[190,8,128]{2,1,0:T(8,128)S(1)}, f32[190,8,128]{2,1,0:T(8,128)S(1)}, u32[]{:S(2)}, u32[]{:S(2)}) collective-permute-start(f32[190,8,128]{2,1,0:T(8,128)S(1)} %get-tuple-element.28.sent), channel_id=1, source_target_pairs={{0,1},{1,0},{2,3},{3,2},{4,5},{5,4},{6,7},{7,6},{8,9},{9,8},{10,11... | collective-permute-start | bytes 2334728 | tf_op jit(solution)/shard_map/ppermute | solution.py:448
  81.7 19.0 %collective-permute-done.9.bo = f32[190,8,128]{2,1,0:T(8,128)S(1)} collective-permute-done((f32[190,8,128]{2,1,0:T(8,128)S(1)}, f32[190,8,128]{2,1,0:T(8,128)S(1)}, u32[]{:S(2)}, u32[]{:S(2)}) %collective-permute-start.9) | collective-permute-done | bytes 778272 | tf_op jit(solution)/shard_map/ppermute | solution.py:452
  100.8 0.0 collective-permute-done.8.be
  100.8 5.3 %shard_map.99 = (f32[3,4,16,128]{3,2,1,0:T(8,128)S(1)}, f32[3,2,16,128]{3,2,1,0:T(8,128)S(1)}) custom-call(s32[2]{0:T(128)S(1)} %pad_add_fusion.pos, f32[190,8,128]{2,1,0:T(8,128)S(1)} %get-tuple-element.28.sent, f32[190,8,128]{2,1,0:T(8,128)S(1)} %collective-permute-done.8.be, f32[190,8,128]{2,1,0:T(8,128)S(1)} %collective-permute-done.9.bo), custom_call_target="tpu_custom_call" | custom-call | tf_op jit(solution)/shard_map/pallas_call | solution.py:433
  106.0 0.1 collective-permute-start.10
  106.1 4.1 %collective-permute-done.10.other = f32[3,2,16,128]{3,2,1,0:T(8,128)S(1)} collective-permute-done((f32[3,2,16,128]{3,2,1,0:T(8,128)S(1)}, f32[3,2,16,128]{3,2,1,0:T(8,128)S(1)}, u32[]{:S(2)}, u32[]{:S(2)}) %collective-permute-start.10) | collective-permute-done | bytes 49184 | tf_op jit(solution)/shard_map/ppermute | solution.py:448
  110.2 4.0 %shard_map.100 = (f32[3,4,16,256]{3,2,1,0:T(8,128)}, f32[3,4,16,256]{3,2,1,0:T(8,128)}) custom-call(s32[2]{0:T(128)S(1)} %pad_add_fusion.pos, f32[3,4,16,256]{3,2,1,0:T(8,128)S(1)} %get-tuple-element.25.pre, f32[56,8,128]{2,1,0:T(8,128)S(1)} %collective-permute-done.4.e, f32[76,8,128]{2,1,0:T(8,128)S(1)} %collective-permute-done.5.o, ...), custom_call_target="tpu_custom_call" | custom-call | tf_op jit(solution)/shard_map/pallas_call | solution.py:433
  (6 shorter events, 0.1 us)
Async XLA Ops:
  0.7 0.9 copy-start
  1.6 0.9 copy-start.2
  2.6 0.9 copy-start.4
  3.5 0.9 copy-start.5
  4.4 0.8 copy-start.6
  5.3 0.8 copy-start.7
  6.1 0.8 copy-start.8
  6.9 0.8 copy-start.9
  7.8 34.1 %copy-start.1 = (f32[3,4,16,256]{3,2,1,0:T(8,128)S(1)}, f32[3,4,16,256]{3,2,1,0:T(8,128)}, u32[]{:S(2)}) copy-start(f32[3,4,16,256]{3,2,1,0:T(8,128)} %main.5) | copy-start | bytes 589828
  7.8 34.1 %copy-start.3 = (f32[3,4,16,256]{3,2,1,0:T(8,128)S(1)}, f32[3,4,16,256]{3,2,1,0:T(8,128)}, u32[]{:S(2)}) copy-start(f32[3,4,16,256]{3,2,1,0:T(8,128)} %cross.5) | copy-start | bytes 589828
  8.5 13.2 %collective-permute-start = (f32[35,16,256]{2,1,0:T(8,128)S(1)}, f32[35,16,256]{2,1,0:T(8,128)S(1)}, u32[]{:S(2)}, u32[]{:S(2)}) collective-permute-start(f32[35,16,256]{2,1,0:T(8,128)S(1)} %get-tuple-element.21), channel_id=1, source_target_pairs={{0,16},{16,0},{32,48},{48,32},{64,80},{80,64},{96,112},{112,96},{1... | collective-permute-start | bytes 1720328 | tf_op jit(solution)/shard_map/ppermute | solution.py:448
  8.7 20.1 %collective-permute-start.1 = (f32[35,16,256]{2,1,0:T(8,128)S(1)}, f32[35,16,256]{2,1,0:T(8,128)S(1)}, u32[]{:S(2)}, u32[]{:S(2)}) collective-permute-start(f32[35,16,256]{2,1,0:T(8,128)S(1)} %get-tuple-element.22), channel_id=1, source_target_pairs={{0,240},{16,32},{32,16},{48,64},{64,48},{80,96},{96,80},{112,128},... | collective-permute-start | bytes 1720328 | tf_op jit(solution)/shard_map/ppermute | solution.py:452
  29.6 3.2 %collective-permute-start.2 = (f32[90,8,128]{2,1,0:T(8,128)S(1)}, f32[90,8,128]{2,1,0:T(8,128)S(1)}, u32[]{:S(2)}, u32[]{:S(2)}) collective-permute-start(f32[90,8,128]{2,1,0:T(8,128)S(1)} %get-tuple-element.23), channel_id=1, source_target_pairs={{0,1},{1,0},{2,3},{3,2},{4,5},{5,4},{6,7},{7,6},{8,9},{9,8},{10,11... | collective-permute-start | bytes 1105928 | tf_op jit(solution)/shard_map/ppermute | solution.py:448
  29.7 12.2 %collective-permute-start.3 = (f32[90,8,128]{2,1,0:T(8,128)S(1)}, f32[90,8,128]{2,1,0:T(8,128)S(1)}, u32[]{:S(2)}, u32[]{:S(2)}) collective-permute-start(f32[90,8,128]{2,1,0:T(8,128)S(1)} %get-tuple-element.24), channel_id=1, source_target_pairs={{0,15},{1,2},{2,1},{3,4},{4,3},{5,6},{6,5},{7,8},{8,7},{9,10},{10,... | collective-permute-start | bytes 1105928 | tf_op jit(solution)/shard_map/ppermute | solution.py:452
  46.1 6.8 %collective-permute-start.4 = (f32[56,8,128]{2,1,0:T(8,128)S(1)}, f32[56,8,128]{2,1,0:T(8,128)S(1)}, u32[]{:S(2)}, u32[]{:S(2)}) collective-permute-start(f32[56,8,128]{2,1,0:T(8,128)S(1)} %get-tuple-element.26.em), channel_id=1, source_target_pairs={{0,16},{16,0},{32,48},{48,32},{64,80},{80,64},{96,112},{112,96},{1... | collective-permute-start | bytes 688136 | tf_op jit(solution)/shard_map/ppermute | solution.py:448
  52.9 11.2 %collective-permute-start.5 = (f32[76,8,128]{2,1,0:T(8,128)S(1)}, f32[76,8,128]{2,1,0:T(8,128)S(1)}, u32[]{:S(2)}, u32[]{:S(2)}) collective-permute-start(f32[76,8,128]{2,1,0:T(8,128)S(1)} %pad_maximum_fusion), channel_id=1, source_target_pairs={{0,240},{16,32},{32,16},{48,64},{64,48},{80,96},{96,80},{112,128},... | collective-permute-start | bytes 933896 | tf_op jit(solution)/shard_map/ppermute | solution.py:452
  64.1 5.4 %collective-permute-start.6 = (f32[40,8,128]{2,1,0:T(8,128)S(1)}, f32[40,8,128]{2,1,0:T(8,128)S(1)}, u32[]{:S(2)}, u32[]{:S(2)}) collective-permute-start(f32[40,8,128]{2,1,0:T(8,128)S(1)} %slice.17), channel_id=1, source_target_pairs={{0,16},{16,0},{32,48},{48,32},{64,80},{80,64},{96,112},{112,96},{1... | collective-permute-start | bytes 491528 | tf_op jit(solution)/shard_map/ppermute | solution.py:448
  69.5 8.9 %collective-permute-start.7 = (f32[40,8,128]{2,1,0:T(8,128)S(1)}, f32[40,8,128]{2,1,0:T(8,128)S(1)}, u32[]{:S(2)}, u32[]{:S(2)}) collective-permute-start(f32[40,8,128]{2,1,0:T(8,128)S(1)} %collective-permute-done.6.e2), channel_id=1, source_target_pairs={{0,240},{16,32},{32,16},{48,64},{64,48},{80,96},{96,80},{112,128},... | collective-permute-start | bytes 491528 | tf_op jit(solution)/shard_map/ppermute | solution.py:452
  79.1 21.6 %collective-permute-start.9 = (f32[190,8,128]{2,1,0:T(8,128)S(1)}, f32[190,8,128]{2,1,0:T(8,128)S(1)}, u32[]{:S(2)}, u32[]{:S(2)}) collective-permute-start(f32[190,8,128]{2,1,0:T(8,128)S(1)} %get-tuple-element.29), channel_id=1, source_target_pairs={{0,15},{1,2},{2,1},{3,4},{4,3},{5,6},{6,5},{7,8},{8,7},{9,10},{10,... | collective-permute-start | bytes 2334728 | tf_op jit(solution)/shard_map/ppermute | solution.py:452
  79.2 21.5 %collective-permute-start.8 = (f32[190,8,128]{2,1,0:T(8,128)S(1)}, f32[190,8,128]{2,1,0:T(8,128)S(1)}, u32[]{:S(2)}, u32[]{:S(2)}) collective-permute-start(f32[190,8,128]{2,1,0:T(8,128)S(1)} %get-tuple-element.28.sent), channel_id=1, source_target_pairs={{0,1},{1,0},{2,3},{3,2},{4,5},{5,4},{6,7},{7,6},{8,9},{9,8},{10,11... | collective-permute-start | bytes 2334728 | tf_op jit(solution)/shard_map/ppermute | solution.py:448
  106.0 4.2 %collective-permute-start.10 = (f32[3,2,16,128]{3,2,1,0:T(8,128)S(1)}, f32[3,2,16,128]{3,2,1,0:T(8,128)S(1)}, u32[]{:S(2)}, u32[]{:S(2)}) collective-permute-start(f32[3,2,16,128]{3,2,1,0:T(8,128)S(1)} %get-tuple-element.31), channel_id=1, source_target_pairs={{0,16},{16,0},{32,48},{48,32},{64,80},{80,64},{96,112},{112,96},{1... | collective-permute-start | bytes 147464 | tf_op jit(solution)/shard_map/ppermute | solution.py:448

commit v2 on v1

--- a/solution.py
+++ b/solution.py
@@ -53,72 +53,102 @@
     return (jnp.bitwise_and(g, 1) == 0), jnp.logical_and(g > 0, g < 15)
 
 
-def pack_grp(pos, disp, trac, heat, main, cross, clear, touch, clip, me, mo, kinv, obst):
-    par = jnp.bitwise_and(pos[0], 1)
-    obst[...] = jnp.where(touch[...] == 1, clear[...], FREE)
-    for p in range(4):
-        inv = inverse(main[0, p], main[1, p], main[2, p], cross[0, p], cross[1, p], cross[2, p])
-        for k in range(6):
-            kinv[k, p] = inv[k]
-    for msg, at in ((me, 1 - par), (mo, par)):
-        for c in range(3):
-            msg[3 * c : 3 * c + 3] = disp[c, pl.ds(at, 3)]
-        msg[9:12] = heat[pl.ds(at, 3)]
-        msg[12:15] = clip[pl.ds(at, 3)].astype(F32)
-        for c in range(3):
-            msg[15 + 2 * c : 17 + 2 * c] = trac[c, pl.ds(2 * at, 2)]
-        for k in range(6):
-            msg[21 + 2 * k : 23 + 2 * k] = kinv[k, pl.ds(2 * at, 2)]
-        msg[33:35] = obst[pl.ds(2 * at, 2)]
-
-
-def wide_plane(own, re, ro, even, inside, base, width, p):
-    if p < width:
-        return jnp.where(even, jnp.where(inside, ro[base + p], 0.0), re[base + p])
-    if p < width + 4:
-        return own(p - width)
-    q = base + p - width - 4
-    return jnp.where(even, re[q], jnp.where(inside, ro[q], 0.0))
-
-
-def fields(disp, heat, clip, trac, kinv, obst):
+def put(msg, t, r, x):
+    n = x.shape[0]
+    msg[t, r : r + n, :] = x[:, :128]
+    msg[t, r + 4 : r + 4 + n, :] = x[:, 128:]
+
+
+def put_rows(be, bo, up, t, r, x, n, skip=0):
+    low, high = x[skip : skip + n], x[16 - skip - n : 16 - skip]
+    put(be, t, r, jnp.where(up, high, low))
+    put(bo, t, r, jnp.where(up, low, high))
+
+
+def get_rows(be, bo, up, inside, t, r, n):
+    e = jnp.concatenate([be[t, r : r + n, :], be[t, r + 4 : r + 4 + n, :]], 1)
+    o = jnp.concatenate([bo[t, r : r + n, :], bo[t, r + 4 : r + 4 + n, :]], 1)
+    o = jnp.where(inside, o, 0.0)
+    return jnp.where(up, o, e), jnp.where(up, e, o)
+
+
+def fields(disp, heat, trac, kinv, obst):
     wide = [lambda p, c=c: disp[c, p] for c in range(3)]
-    wide += [lambda p: heat[p], lambda p: clip[p].astype(F32)]
+    wide += [lambda p: heat[p]]
     near = [lambda p, c=c: trac[c, p] for c in range(3)]
     near += [lambda p, k=k: kinv[k, p] for k in range(6)]
     near += [lambda p: obst[p]]
     return wide, near
 
 
-def put(msg, t, r, x):
-    n = x.shape[0]
-    msg[t, r : r + n, :] = x[:, :128]
-    msg[t, r + 4 : r + 4 + n, :] = x[:, 128:]
-
-
-def pack_brick(pos, disp, heat, clip, trac, kinv, obst, re, ro, be, bo):
+def load_pack(
+    pos, disp_h, trac_h, heat_h, main_h, cross_h, clear_h, touch_h,
+    kinv, obst, me, mo, be, bo,
+    disp, trac, heat, main, cross, clear, touch, sem,
+):
+    pairs = [
+        (main_h, main), (cross_h, cross), (clear_h, clear), (touch_h, touch),
+        (disp_h, disp), (trac_h, trac), (heat_h, heat),
+    ]
+    copies = [pltpu.make_async_copy(x, y, sem.at[i]) for i, (x, y) in enumerate(pairs)]
+    for c in copies:
+        c.start()
+    par = jnp.bitwise_and(pos[0], 1)
+    up = jnp.bitwise_and(pos[1], 1) == 0
+    copies[0].wait()
+    copies[1].wait()
+
+    def invert(p, carry):
+        inv = inverse(main[0, p], main[1, p], main[2, p], cross[0, p], cross[1, p], cross[2, p])
+        for k in range(6):
+            kinv[k, p] = inv[k]
+        return carry
+
+    lax.fori_loop(0, 4, invert, 0)
+    copies[2].wait()
+    copies[3].wait()
+    obst[...] = jnp.where(touch[...] == 1, clear[...], FREE)
+    for c in copies[4:]:
+        c.wait()
+    for msg, at in ((me, 1 - par), (mo, par)):
+        for c in range(3):
+            msg[3 * c : 3 * c + 3] = disp[c, pl.ds(at, 3)]
+        msg[9:12] = heat[pl.ds(at, 3)]
+        for c in range(3):
+            msg[12 + 2 * c : 14 + 2 * c] = trac[c, pl.ds(2 * at, 2)]
+        for k in range(6):
+            msg[18 + 2 * k : 20 + 2 * k] = kinv[k, pl.ds(2 * at, 2)]
+        msg[30:32] = obst[pl.ds(2 * at, 2)]
+    wide, near = fields(disp, heat, trac, kinv, obst)
+    for f in range(4):
+        for p in range(4):
+            put_rows(be, bo, up, f * 4 + p, 0, wide[f](p), 3)
+    for f in range(10):
+        for p in range(4):
+            put_rows(be, bo, up, 16 + f * 2 + p // 2, 2 * (p % 2), near[f](p), 2)
+
+
+def halo_plane(re, ro, even, inside, low, k):
+    e, o = re[k], jnp.where(inside, ro[k], 0.0)
+    return jnp.where(even, o, e) if low else jnp.where(even, e, o)
+
+
+def pack_corner(pos, re, ro, be, bo):
     even, inside = sides(pos[0])
     up = jnp.bitwise_and(pos[1], 1) == 0
-    wide, near = fields(disp, heat, clip, trac, kinv, obst)
-    for f in range(5):
-        for p in range(10):
-            x = wide_plane(wide[f], re, ro, even, inside, 3 * f, 3, p)
-            low, high = x[0:3], x[13:16]
-            put(be, f * 10 + p, 0, jnp.where(up, high, low))
-            put(bo, f * 10 + p, 0, jnp.where(up, low, high))
+    for f in range(4):
+        for side in range(2):
+            low = side == 0
+            x = halo_plane(re, ro, even, inside, low, 3 * f + (2 if low else 0))
+            put_rows(be, bo, up, f * 2 + side, 0, x, 2)
+            x = halo_plane(re, ro, even, inside, low, 3 * f + 1)
+            put_rows(be, bo, up, f * 2 + side, 2, x, 1)
     for f in range(10):
-        for p in range(8):
-            x = wide_plane(near[f], re, ro, even, inside, 15 + 2 * f, 2, p)
-            low, high = x[0:2], x[14:16]
-            put(be, 50 + f * 4 + p // 2, 2 * (p % 2), jnp.where(up, high, low))
-            put(bo, 50 + f * 4 + p // 2, 2 * (p % 2), jnp.where(up, low, high))
-
-
-def brick_rows(be, bo, up, inside, t, r, n):
-    e = jnp.concatenate([be[t, r : r + n, :], be[t, r + 4 : r + 4 + n, :]], 1)
-    o = jnp.concatenate([bo[t, r : r + n, :], bo[t, r + 4 : r + 4 + n, :]], 1)
-    o = jnp.where(inside, o, 0.0)
-    return jnp.where(up, o, e), jnp.where(up, e, o)
+        for side in range(2):
+            low = side == 0
+            n = f * 2 + side
+            x = halo_plane(re, ro, even, inside, low, 12 + 2 * f + (1 if low else 0))
+            put_rows(be, bo, up, 8 + n // 4, n % 4, x, 1)
 
 
 def smooth(v0, force, kinv, obst, v1, v2):
@@ -154,33 +184,46 @@
 
 
 def presmooth(
-    pos, disp, heat, clip, trac, kinv, obst, main, cross, clear, touch, re, ro, be, bo,
-    force_x, kinv_x, obst_x, clip_x, pre, em, om,
-    v0, heat_x, v1, v2, rest, gath,
+    pos, disp, heat, clip, trac, kinv, obst, main, cross, clear, touch,
+    re, ro, be, bo, ce, co,
+    force_x, kinv_x, obst_x, v2, small_out, planes_out, pe, po,
+    v0, heat_x, v1, rest, gath,
 ):
     even, inside = sides(pos[0])
     up, inner = sides(pos[1])
-    par = jnp.bitwise_and(pos[0], 1)
-    wide, near = fields(disp, heat, clip, trac, kinv, obst)
+    wide, near = fields(disp, heat, trac, kinv, obst)
     wide_to = [lambda p, c=c: v0.at[c, p] for c in range(3)]
-    wide_to += [lambda p: heat_x.at[p], lambda p: clip_x.at[p]]
+    wide_to += [lambda p: heat_x.at[p]]
     near_to = [lambda p, c=c: force_x.at[c, p] for c in range(3)]
     near_to += [lambda p, k=k: kinv_x.at[k, p] for k in range(6)]
     near_to += [lambda p: obst_x.at[p]]
-    for f in range(5):
-        for p in range(10):
-            to = wide_to[f](p)
-            to[8:24, :] = wide_plane(wide[f], re, ro, even, inside, 3 * f, 3, p)
-            low, high = brick_rows(be, bo, up, inner, f * 10 + p, 0, 3)
-            to[5:8, :] = low
-            to[24:27, :] = high
+    for f in range(4):
+        for p in range(4):
+            to = wide_to[f](p + 3)
+            to[8:24, :] = wide[f](p)
+            to[5:8, :], to[24:27, :] = get_rows(be, bo, up, inner, f * 4 + p, 0, 3)
+        for side in range(2):
+            low = side == 0
+            for k in range(3):
+                to = wide_to[f](k if low else 7 + k)
+                to[8:24, :] = halo_plane(re, ro, even, inside, low, 3 * f + k)
+            to = wide_to[f](2 if low else 7)
+            to[6:8, :], to[24:26, :] = get_rows(ce, co, up, inner, f * 2 + side, 0, 2)
+            to = wide_to[f](1 if low else 8)
+            to[7:8, :], to[24:25, :] = get_rows(ce, co, up, inner, f * 2 + side, 2, 1)
     for f in range(10):
-        for p in range(8):
-            to = near_to[f](p)
-            to[8:24, :] = wide_plane(near[f], re, ro, even, inside, 15 + 2 * f, 2, p)
-            low, high = brick_rows(be, bo, up, inner, 50 + f * 4 + p // 2, 2 * (p % 2), 2)
-            to[6:8, :] = low
-            to[24:26, :] = high
+        for p in range(4):
+            to = near_to[f](p + 2)
+            to[8:24, :] = near[f](p)
+            to[6:8, :], to[24:26, :] = get_rows(be, bo, up, inner, 16 + f * 2 + p // 2, 2 * (p % 2), 2)
+        for side in range(2):
+            low = side == 0
+            for k in range(2):
+                to = near_to[f](k if low else 6 + k)
+                to[8:24, :] = halo_plane(re, ro, even, inside, low, 12 + 2 * f + k)
+            n = f * 2 + side
+            to = near_to[f](1 if low else 6)
+            to[7:8, :], to[24:25, :] = get_rows(ce, co, up, inner, 8 + n // 4, n % 4, 1)
 
     def drift(p, carry):
         h = heat_x[p + 1]
@@ -230,52 +273,34 @@
     i, j = rows((256, 128)), lanes((256, 128))
     pick = jnp.where(lax.shift_right_logical(i, 1) == j, 1.0, 0.0)
     small = jnp.dot(gath[...], pick, precision=HIGH, preferred_element_type=F32)
-    small = small.reshape(20, 8, 128)
-    em[0:20] = small
-    om[0:20] = small
+    small_out[...] = small.reshape(20, 8, 128)
+    for c in range(3):
+        for k in range(2):
+            planes_out[2 * c + k] = v2[c, k + 2, 8:24, :]
     for p in range(4):
-        for c in range(3):
-            pre[c, p] = v2[c, p + 1, 8:24, :]
-    for msg, at in ((em, 1 - par), (om, par)):
-        for c in range(3):
-            for k in range(3):
-                t = 20 + (c * 3 + k) * 4
-                x = v2[c, at + k + 1, 8:24, :]
-                msg[t] = x[:8, :128]
-                msg[t + 1] = x[:8, 128:]
-                msg[t + 2] = x[8:, :128]
-                msg[t + 3] = x[8:, 128:]
-
-
-def pre_plane(pre, e, o, even, inside, c, p):
-    def tile(msg, base, k):
-        t = base + (c * 3 + k) * 4
-        left = jnp.concatenate([msg[t], msg[t + 2]], 0)
-        right = jnp.concatenate([msg[t + 1], msg[t + 3]], 0)
-        return jnp.concatenate([left, right], 1)
-
-    if p < 3:
-        return jnp.where(even, jnp.where(inside, tile(o, 40, p), 0.0), tile(e, 20, p))
-    if p < 7:
-        return pre[c, p - 3]
-    return jnp.where(even, tile(e, 20, p - 7), jnp.where(inside, tile(o, 40, p - 7), 0.0))
-
-
-def pack_coarse(pos, pre, em, e, o, e2, o2, be, bo):
+        planes_out[6 + p] = clip[p].astype(F32)
+    for c in range(3):
+        for p in range(4):
+            put_rows(pe, po, up, c * 2 + p // 2, 2 * (p % 2), v2[c, p + 1, 8:24, :], 2, 1)
+        for side in range(2):
+            n = 2 * c + side
+            put_rows(pe, po, up, 10 + n // 2, 2 * (n % 2), v2[c, 5 * side, 8:24, :], 2)
+    for p in range(4):
+        put_rows(pe, po, up, 6 + p, 0, clip[p].astype(F32), 3)
+
+
+def pack_late(pos, ge, go, be, bo):
     even, inside = sides(pos[0])
     up = jnp.bitwise_and(pos[1], 1) == 0
-    for msg in (be, bo):
-        msg[0:20] = em[0:20]
-        msg[20:40] = e[0:20]
-        msg[40:80] = o[0:40]
-        msg[80:120] = e2[...]
-        msg[120:160] = o2[...]
-    for c in range(3):
-        for p in range(10):
-            x = pre_plane(pre, e, o, even, inside, c, p)
-            low, high = x[0:3], x[13:16]
-            put(be, 160 + c * 10 + p, 0, jnp.where(up, high, low))
-            put(bo, 160 + c * 10 + p, 0, jnp.where(up, low, high))
+    for side in range(2):
+        low = side == 0
+        for c in range(3):
+            x = halo_plane(ge, go, even, inside, low, 2 * c + (1 if low else 0))
+            put_rows(be, bo, up, side, c, x, 1)
+        x = halo_plane(ge, go, even, inside, low, 6 + (3 if low else 0))
+        put_rows(be, bo, up, 2 + side, 0, x, 2)
+        x = halo_plane(ge, go, even, inside, low, 6 + (2 if low else 1))
+        put_rows(be, bo, up, 2 + side, 2, x, 1)
 
 
 def pair_spread(x, op):
@@ -286,23 +311,34 @@
     return op(x, jnp.where(even, pltpu.roll(x, n - 1, axis=0), pltpu.roll(x, 1, axis=0)))
 
 
-def coarse(pos, sent, be, bo, mid2, own, g, ki, va, vb, f3, k3, o3, l3):
+def coarse(
+    pos, b0, b1, b2, b3, b4, r1e, r1o, r2e, r2o, r3e, r3o,
+    mid2, own, g, ki, va, vb, f3, k3, o3, l3,
+):
     par = jnp.bitwise_and(pos[0], 1)
     up, inner = sides(pos[1])
     grp = pos[0]
-    for s in range(8):
+    slots = [
+        (b0, 0, r1e, r1o, 0), (b1, 0, r1e, r1o, 20), (b2, 0, r2e, r2o, 0), (b2, 20, r2e, r2o, 20),
+        (b3, 0, r2e, r2o, 40), (b3, 20, r2e, r2o, 60), (b4, 0, r3e, r3o, 0), (b4, 20, r3e, r3o, 20),
+    ]
+    for s, (mine, m, re, ro, r) in enumerate(slots):
         place = jnp.where(par == 0, EVEN_SLOTS[s], 7 - EVEN_SLOTS[s])
         where = grp + place - jnp.where(par == 0, 4, 3)
         real = jnp.logical_and(where >= 0, where < 16)
-        for f in range(10):
+
+        def fill(f, carry):
             for q in range(2):
-                t = s * 20 + f * 2 + q
-                a = jnp.where(real, be[t], 0.0)
-                b = jnp.where(jnp.logical_and(real, inner), bo[t], 0.0)
+                t = f * 2 + q
+                a = jnp.where(real, re[r + t], 0.0)
+                b = jnp.where(jnp.logical_and(real, inner), ro[r + t], 0.0)
                 to = g.at[f, 2 * place + q]
                 to[0:8, :] = jnp.where(up, b, a)
-                to[8:16, :] = jnp.where(real, sent[t], 0.0)
+                to[8:16, :] = jnp.where(real, mine[m + t], 0.0)
                 to[16:24, :] = jnp.where(up, a, b)
+            return carry
+
+        lax.fori_loop(0, 10, fill, 0)
 
     def start(p, carry):
         inv = inverse(*[g[4 + k, p] for k in range(6)])
@@ -387,19 +423,41 @@
 
 
 def finish(
-    pos, pre, e, o, be, bo, mid2, other, force_x, kinv_x, obst_x, clip_x, main, cross,
-    moved, residual, v0, v1, v2, mid_x, fine,
+    pos, pre, ge, go, r1e, r1o, r3e, r3o, mid2, other, force_x, kinv_x, obst_x, clip, main, cross,
+    moved, residual, v0, v1, v2, clip_x, mid_x, fine,
 ):
     par = jnp.bitwise_and(pos[0], 1)
     even, inside = sides(pos[0])
     up, inner = sides(pos[1])
     for c in range(3):
-        for p in range(10):
-            to = v0.at[c, p]
-            to[8:24, :] = pre_plane(pre, e, o, even, inside, c, p)
-            low, high = brick_rows(be, bo, up, inner, 160 + c * 10 + p, 0, 3)
-            to[5:8, :] = low
-            to[24:27, :] = high
+        for p in range(6):
+            v0[c, p + 2] = pre[c, p]
+        for p in range(4):
+            to = v0.at[c, p + 3]
+            to[5:7, :], to[25:27, :] = get_rows(r1e, r1o, up, inner, 40 + c * 2 + p // 2, 2 * (p % 2), 2)
+        for side in range(2):
+            low = side == 0
+            n = 2 * c + side
+            to = v0.at[c, 2 if low else 7]
+            to[6:8, :], to[24:26, :] = get_rows(r1e, r1o, up, inner, 50 + n // 2, 2 * (n % 2), 2)
+            for k in range(2):
+                to = v0.at[c, k if low else 8 + k]
+                to[8:24, :] = halo_plane(ge, go, even, inside, low, 2 * c + k)
+            to = v0.at[c, 1 if low else 8]
+            to[7:8, :], to[24:25, :] = get_rows(r3e, r3o, up, inner, 40 + side, c, 1)
+    for p in range(4):
+        to = clip_x.at[p + 3]
+        to[8:24, :] = clip[p].astype(F32)
+        to[5:8, :], to[24:27, :] = get_rows(r1e, r1o, up, inner, 46 + p, 0, 3)
+    for side in range(2):
+        low = side == 0
+        for k in range(3):
+            to = clip_x.at[k if low else 7 + k]
+            to[8:24, :] = halo_plane(ge, go, even, inside, low, 6 + k + (1 if low else 0))
+        to = clip_x.at[2 if low else 7]
+        to[6:8, :], to[24:26, :] = get_rows(r3e, r3o, up, inner, 42 + side, 0, 2)
+        to = clip_x.at[1 if low else 8]
+        to[7:8, :], to[24:25, :] = get_rows(r3e, r3o, up, inner, 42 + side, 2, 1)
     i, j = rows((128, 256)), lanes((128, 256))
     copy = jnp.where(lax.shift_right_logical(j, 1) == i, 1.0, 0.0)
     for c in range(3):
@@ -428,15 +486,16 @@
             moved[c, p] = v2[c, p + 1, 8:24, :]
 
 
-def call(kernel, outs, scratch, *args):
+def call(kernel, outs, scratch, *args, limit=0):
     vm = pl.BlockSpec(memory_space=pltpu.VMEM)
+    source = pl.BlockSpec(memory_space=pltpu.HBM) if limit else vm
     return pl.pallas_call(
         kernel,
-        out_shape=[jax.ShapeDtypeStruct(s, F32) for s in outs],
-        in_specs=[pl.BlockSpec(memory_space=pltpu.SMEM)] + [vm] * (len(args) - 1),
+        out_shape=[jax.ShapeDtypeStruct(x, F32) for x in outs],
+        in_specs=[pl.BlockSpec(memory_space=pltpu.SMEM)] + [source] * (len(args) - 1),
         out_specs=[vm] * len(outs),
-        scratch_shapes=[pltpu.VMEM(s, F32) for s in scratch],
-        compiler_params=pltpu.CompilerParams(vmem_limit_bytes=32 * 1024 * 1024),
+        scratch_shapes=[pltpu.VMEM(x, F32) if isinstance(x, tuple) else x for x in scratch],
+        compiler_params=pltpu.CompilerParams(vmem_limit_bytes=limit or 32 * 1024 * 1024),
     )(*args)
 
 
@@ -454,47 +513,54 @@
 
 def local(disp, trac, heat, main, cross, clear, touch, clip):
     pos = jnp.stack([lax.axis_index("grp"), lax.axis_index("brick")]).astype(jnp.int32)
-    own = (4, 16, 256)
-    me, mo, kinv, obst = call(
-        pack_grp, [(35, 16, 256), (35, 16, 256), (6,) + own, own], [],
-        pos, disp, trac, heat, main, cross, clear, touch, clip,
+    own, vec, six = (4, 16, 256), (3, 4, 16, 256), (6, 4, 16, 256)
+    kinv, obst, me, mo, be, bo = call(
+        load_pack,
+        [six, own] + [(32, 16, 256)] * 2 + [(36, 8, 128)] * 2,
+        [vec, vec, own, vec, vec, own, pltpu.VMEM(own, jnp.int32), pltpu.SemaphoreType.DMA((7,))],
+        pos, disp, trac, heat, main, cross, clear, touch, limit=58 * 1024 * 1024,
     )
     re, ro = swap_even(me, "grp"), swap_odd(mo, "grp")
-    be, bo = call(
-        pack_brick, [(90, 8, 128)] * 2, [],
-        pos, disp, heat, clip, trac, kinv, obst, re, ro,
+    re_b, ro_b = swap_even(be, "brick"), swap_odd(bo, "brick")
+    ce, co = call(pack_corner, [(13, 8, 128)] * 2, [], pos, re, ro)
+    re_c, ro_c = swap_even(ce, "brick"), swap_odd(co, "brick")
+    force_x, kinv_x, obst_x, pre, b0, planes, pe, po = call(
+        presmooth,
+        [(3, 8, 32, 256), (6, 8, 32, 256), (8, 32, 256), (3, 6, 32, 256), (20, 8, 128),
+         (10, 16, 256), (13, 8, 128), (13, 8, 128)],
+        [(3, 10, 32, 256), (10, 32, 256), (3, 8, 32, 256), (10, 2, 16, 128), (160, 256)],
+        pos, disp, heat, clip, trac, kinv, obst, main, cross, clear, touch,
+        re, ro, re_b, ro_b, re_c, ro_c,
     )
-    re_b, ro_b = swap_even(be, "brick"), swap_odd(bo, "brick")
-    force_x, kinv_x, obst_x, clip_x, pre, em, om = call(
-        presmooth,
-        [(3, 8, 32, 256), (6, 8, 32, 256), (8, 32, 256), (10, 32, 256), (3,) + own,
-         (56, 8, 128), (56, 8, 128)],
-        [(3, 10, 32, 256), (10, 32, 256), (3, 8, 32, 256), (3, 6, 32, 256),
-         (10, 2, 16, 128), (160, 256)],
-        pos, disp, heat, clip, trac, kinv, obst, main, cross, clear, touch, re, ro, re_b, ro_b,
-    )
-    e = swap_even(em, "grp")
-    o = swap_odd(jnp.concatenate([om[:20], e[:20], om[20:]], 0), "grp")
-    e2 = swap_even(o[:40], "grp")
-    o2 = swap_odd(e2, "grp")
-    ce, co = call(pack_coarse, [(190, 8, 128)] * 2, [], pos, pre, em, e, o, e2, o2)
-    re_c, ro_c = swap_even(ce, "brick"), swap_odd(co, "brick")
-    field = (3, 16, 24, 128)
-    third = (3, 8, 24, 128)
+    b1 = swap_even(b0, "grp")
+    b2 = swap_odd(jnp.concatenate([b0, b1], 0), "grp")
+    ge, go = swap_even(planes, "grp"), swap_odd(planes, "grp")
+    r1e = swap_even(jnp.concatenate([b0, b1, pe], 0), "brick")
+    r1o = swap_odd(jnp.concatenate([b0, b1, po], 0), "brick")
+    b3 = swap_even(b2, "grp")
+    second = jnp.concatenate([b2, b3], 0)
+    r2e, r2o = swap_even(second, "brick"), swap_odd(second, "brick")
+    b4 = swap_odd(b3, "grp")
+    qe, qo = call(pack_late, [(4, 8, 128)] * 2, [], pos, ge, go)
+    r3e = swap_even(jnp.concatenate([b4, qe], 0), "brick")
+    r3o = swap_odd(jnp.concatenate([b4, qo], 0), "brick")
+    field, third = (3, 16, 24, 128), (3, 8, 24, 128)
     mid2, mine = call(
         coarse,
         [(3, 4, 16, 128), (3, 2, 16, 128)],
         [(10, 16, 24, 128), (6, 16, 24, 128), field, field, third, (6, 8, 24, 128),
          (8, 24, 128), third],
-        pos, ce, re_c, ro_c,
+        pos, b0, b1, b2, b3, b4, r1e, r1o, r2e, r2o, r3e, r3o,
     )
     other = swap_even(mine, "grp")
     return tuple(
         call(
             finish,
-            [(3,) + own, (3,) + own],
-            [(3, 10, 32, 256), (3, 8, 32, 256), (3, 6, 32, 256), (3, 6, 16, 128), (2, 32, 128)],
-            pos, pre, e, o, re_c, ro_c, mid2, other, force_x, kinv_x, obst_x, clip_x, main, cross,
+            [vec, vec],
+            [(3, 10, 32, 256), (3, 8, 32, 256), (3, 6, 32, 256), (10, 32, 256), (3, 6, 16, 128),
+             (2, 32, 128)],
+            pos, pre, ge, go, r1e, r1o, r3e, r3o, mid2, other, force_x, kinv_x, obst_x, clip,
+            main, cross,
         )
     )
 

time: 115 us -> 97.8 us (0.85)
  waiting for transfers between devices: 66.1 us -> 37.9 us
  starting transfers between devices: 24.6 us -> 35.2 us
  local copies, waits for them, and re-layouts: 7.11 us -> 3.12 us
  Pallas kernels: 15.6 us -> 18.4 us
    ppermute x5 -> x9, waiting for transfers between devices: 44.5 us -> 27.8 us  [swap_odd(): return lax.ppermute(x, axis, ODD)]
    ppermute x6 -> x10, waiting for transfers between devices: 21.6 us -> 10.1 us  [swap_even(): return lax.ppermute(x, axis, EVEN)]
    ppermute x5 -> x9, starting transfers between devices: 21.4 us -> 32.4 us  [swap_odd(): return lax.ppermute(x, axis, ODD)]
    unnamed x20 -> x25, local copies, waits for them, and re-layouts: 7.07 us -> 3.1 us
    pallas_call x6, Pallas kernels: 15.6 us -> 18.4 us  [call(): pl.pallas_call(kernel, out_shape=[jax.ShapeDtypeStruct(x, F32) for x in o...]
    ppermute x6 -> x10, starting transfers between devices: 3.14 us -> 2.76 us  [swap_even(): return lax.ppermute(x, axis, EVEN)]
  transfers between devices with their start and end apart: 11 -> 19, of which waited for: 9 -> 10; matrix products, arithmetic and copies ran while one was open for 0% -> 0% of each run, Pallas kernels for 0% -> 1%
where the time goes in v2:
time: 97.8 us; the launch traced here: 96.2 us
  waiting for transfers between devices  37.9 us (39%)
  starting transfers between devices  35.2 us (36%)
  Pallas kernels  18.4 us (19%)
  local copies, waits for them, and re-layouts  3.12 us (3%)
    ppermute x9, starting transfers between devices, swap_odd(): return lax.ppermute(x, axis, ODD)  32.4 us
    ppermute x9, waiting for transfers between devices, swap_odd(): return lax.ppermute(x, axis, ODD)  27.8 us
    pallas_call x6, Pallas kernels, call(): pl.pallas_call(kernel, out_shape=[jax.ShapeDtypeStruct(x, F32) for x in o...  18.4 us
    ppermute x10, waiting for transfers between devices, swap_even(): return lax.ppermute(x, axis, EVEN)  10.1 us
    unnamed x25, local copies, waits for them, and re-layouts  3.1 us
    ppermute x10, starting transfers between devices, swap_even(): return lax.ppermute(x, axis, EVEN)  2.76 us
  transfers between devices with their start and end apart: 19, of which 10 were waited for; matrix products, arithmetic and copies ran while one was open for 0% of the time, Pallas kernels for 1%

profile of v2, /device:TPU:0, one launch (start us, length us, event | category | flops | bytes accessed | tf_op | source)
XLA Modules:
  0.0 96.2 jit_solution(2293059538957086981)
XLA Ops:
  0.6 0.0 copy-start.6
  0.6 0.0 copy-start
  0.7 0.0 copy-start.1
  0.7 0.0 copy-start.7
  0.7 0.0 copy-start.8
  0.7 0.0 copy-start.2
  0.7 0.0 copy-start.3
  0.7 0.6 pad_add_fusion.pos
  1.3 3.2 %shard_map.95 = (f32[6,4,16,256]{3,2,1,0:T(8,128)}, f32[4,16,256]{2,1,0:T(8,128)}, f32[32,16,256]{2,1,0:T(8,128)}, f32[32,16,256]{2,1,0:T(8,128)}, f32[36,8,128]{2,1,0:T(8,128)}, /*index=5*/f32[36,8,128]{2,1,0:T(8,128)}) custom-call(s32[2]{0:T(128)} %pad_add_fusion.pos, f32[3,4,16,256]{3,2,1,0:T(8,128)} %disp.1, f32[3,4,16,256]{3,2,1,0:T(8,128)} %trac.1, ...), custom_call_target="tpu_custom_call" | custom-call | tf_op jit(solution)/shard_map/pallas_call | solution.py:492
  4.6 0.3 collective-permute-start
  4.8 7.4 %collective-permute-start.1 = (f32[32,16,256]{2,1,0:T(8,128)}, f32[32,16,256]{2,1,0:T(8,128)S(1)}, u32[]{:S(2)}, u32[]{:S(2)}) collective-permute-start(f32[32,16,256]{2,1,0:T(8,128)} %get-tuple-element.25), channel_id=1, source_target_pairs={{0,240},{16,32},{32,16},{48,64},{64,48},{80,96},{96,80},{112,128},... | collective-permute-start | bytes 1572872 | tf_op jit(solution)/shard_map/ppermute | solution.py:511
  12.3 3.2 %collective-permute-start.3 = (f32[36,8,128]{2,1,0:T(8,128)}, f32[36,8,128]{2,1,0:T(8,128)S(1)}, u32[]{:S(2)}, u32[]{:S(2)}) collective-permute-start(f32[36,8,128]{2,1,0:T(8,128)} %get-tuple-element.27), channel_id=1, source_target_pairs={{0,15},{1,2},{2,1},{3,4},{4,3},{5,6},{6,5},{7,8},{8,7},{9,10},{10,... | collective-permute-start | bytes 442376 | tf_op jit(solution)/shard_map/ppermute | solution.py:511
  15.4 1.6 %collective-permute-done.re = f32[32,16,256]{2,1,0:T(8,128)S(1)} collective-permute-done((f32[32,16,256]{2,1,0:T(8,128)}, f32[32,16,256]{2,1,0:T(8,128)S(1)}, u32[]{:S(2)}, u32[]{:S(2)}) %collective-permute-start) | collective-permute-done | bytes 524320 | tf_op jit(solution)/shard_map/ppermute | solution.py:507
  17.0 7.2 %collective-permute-done.1.ro = f32[32,16,256]{2,1,0:T(8,128)S(1)} collective-permute-done((f32[32,16,256]{2,1,0:T(8,128)}, f32[32,16,256]{2,1,0:T(8,128)S(1)}, u32[]{:S(2)}, u32[]{:S(2)}) %collective-permute-start.1) | collective-permute-done | bytes 524320 | tf_op jit(solution)/shard_map/ppermute | solution.py:511
  24.2 0.6 copy-done.10
  24.8 0.6 shard_map.96
  25.4 0.1 collective-permute-start.4
  25.5 3.1 %collective-permute-start.5 = (f32[13,8,128]{2,1,0:T(8,128)S(1)}, f32[13,8,128]{2,1,0:T(8,128)S(1)}, u32[]{:S(2)}, u32[]{:S(2)}) collective-permute-start(f32[13,8,128]{2,1,0:T(8,128)S(1)} %get-tuple-element.29), channel_id=1, source_target_pairs={{0,15},{1,2},{2,1},{3,4},{4,3},{5,6},{6,5},{7,8},{8,7},{9,10},{10,... | collective-permute-start | bytes 159752 | tf_op jit(solution)/shard_map/ppermute | solution.py:511
  28.7 0.0 collective-permute-done.2.be
  28.7 0.0 collective-permute-done.3.bo
  28.7 0.0 collective-permute-done.4.ce
  28.7 2.6 %collective-permute-done.5.co = f32[13,8,128]{2,1,0:T(8,128)S(1)} collective-permute-done((f32[13,8,128]{2,1,0:T(8,128)S(1)}, f32[13,8,128]{2,1,0:T(8,128)S(1)}, u32[]{:S(2)}, u32[]{:S(2)}) %collective-permute-start.5) | collective-permute-done | bytes 53280 | tf_op jit(solution)/shard_map/ppermute | solution.py:511
  31.4 1.0 %copy-done.4 = f32[6,4,16,256]{3,2,1,0:T(8,128)S(1)} copy-done((f32[6,4,16,256]{3,2,1,0:T(8,128)S(1)}, f32[6,4,16,256]{3,2,1,0:T(8,128)}, u32[]{:S(2)}) %copy-start.4) | copy-done | bytes 393240
  32.4 0.8 copy-done.9
  33.2 0.6 copy-done.11
  33.8 4.1 %shard_map.97 = (f32[3,8,32,256]{3,2,1,0:T(8,128)S(1)}, f32[6,8,32,256]{3,2,1,0:T(8,128)S(1)}, f32[8,32,256]{2,1,0:T(8,128)S(1)}, f32[3,6,32,256]{3,2,1,0:T(8,12...) custom-call(s32[2]{0:T(128)S(1)} %copy-done.11, ...), custom_call_target="tpu_custom_call" | custom-call | tf_op jit(solution)/shard_map/pallas_call | solution.py:492
  37.9 0.1 collective-permute-start.8
  38.0 4.4 %collective-permute-done.8.b1 = f32[20,8,128]{2,1,0:T(8,128)S(1)} collective-permute-done((f32[20,8,128]{2,1,0:T(8,128)S(1)}, f32[20,8,128]{2,1,0:T(8,128)S(1)}, u32[]{:S(2)}, u32[]{:S(2)}) %collective-permute-start.8) | collective-permute-done | bytes 81952 | tf_op jit(solution)/shard_map/ppermute | solution.py:507
  42.5 5.4 %collective-permute-start.11 = (f32[40,8,128]{2,1,0:T(8,128)S(1)}, f32[40,8,128]{2,1,0:T(8,128)S(1)}, u32[]{:S(2)}, u32[]{:S(2)}) collective-permute-start(f32[40,8,128]{2,1,0:T(8,128)S(1)} %pad_maximum_fusion.5), channel_id=1, source_target_pairs={{0,240},{16,32},{32,16},{48,64},{64,48},{80,96},{96,80},{112,128},... | collective-permute-start | bytes 491528 | tf_op jit(solution)/shard_map/ppermute | solution.py:511
  47.9 3.6 %collective-permute-done.11.b2 = f32[40,8,128]{2,1,0:T(8,128)S(1)} collective-permute-done((f32[40,8,128]{2,1,0:T(8,128)S(1)}, f32[40,8,128]{2,1,0:T(8,128)S(1)}, u32[]{:S(2)}, u32[]{:S(2)}) %collective-permute-start.11) | collective-permute-done | bytes 163872 | tf_op jit(solution)/shard_map/ppermute | solution.py:511
  51.5 2.0 %collective-permute-start.6 = (f32[10,16,256]{2,1,0:T(8,128)S(1)}, f32[10,16,256]{2,1,0:T(8,128)S(1)}, u32[]{:S(2)}, u32[]{:S(2)}) collective-permute-start(f32[10,16,256]{2,1,0:T(8,128)S(1)} %get-tuple-element.31), channel_id=1, source_target_pairs={{0,16},{16,0},{32,48},{48,32},{64,80},{80,64},{96,112},{112,96},{1... | collective-permute-start | bytes 491528 | tf_op jit(solution)/shard_map/ppermute | solution.py:507
  53.5 5.4 %collective-permute-start.7 = (f32[10,16,256]{2,1,0:T(8,128)S(1)}, f32[10,16,256]{2,1,0:T(8,128)S(1)}, u32[]{:S(2)}, u32[]{:S(2)}) collective-permute-start(f32[10,16,256]{2,1,0:T(8,128)S(1)} %get-tuple-element.31), channel_id=1, source_target_pairs={{0,240},{16,32},{32,16},{48,64},{64,48},{80,96},{96,80},{112,128},... | collective-permute-start | bytes 491528 | tf_op jit(solution)/shard_map/ppermute | solution.py:511
  58.9 1.4 %collective-permute-start.10 = (f32[53,8,128]{2,1,0:T(8,128)S(1)}, f32[53,8,128]{2,1,0:T(8,128)S(1)}, u32[]{:S(2)}, u32[]{:S(2)}) collective-permute-start(f32[53,8,128]{2,1,0:T(8,128)S(1)} %get-tuple-element.44), channel_id=1, source_target_pairs={{0,15},{1,2},{2,1},{3,4},{4,3},{5,6},{6,5},{7,8},{8,7},{9,10},{10,... | collective-permute-start | bytes 651272 | tf_op jit(solution)/shard_map/ppermute | solution.py:511
  60.3 1.9 %collective-permute-start.13 = (f32[40,8,128]{2,1,0:T(8,128)S(1)}, f32[40,8,128]{2,1,0:T(8,128)S(1)}, u32[]{:S(2)}, u32[]{:S(2)}) collective-permute-start(f32[40,8,128]{2,1,0:T(8,128)S(1)} %collective-permute-done.12.b3), channel_id=1, source_target_pairs={{0,240},{16,32},{32,16},{48,64},{64,48},{80,96},{96,80},{112,128},... | collective-permute-start | bytes 491528 | tf_op jit(solution)/shard_map/ppermute | solution.py:511
  62.2 0.1 collective-permute-start.16
  62.3 4.2 %collective-permute-start.17 = (f32[80,8,128]{2,1,0:T(8,128)S(1)}, f32[80,8,128]{2,1,0:T(8,128)S(1)}, u32[]{:S(2)}, u32[]{:S(2)}) collective-permute-start(f32[80,8,128]{2,1,0:T(8,128)S(1)} %constant_dynamic-update-slice_fusion), channel_id=1, source_target_pairs={{0,15},{1,2},{2,1},{3,4},{4,3},{5,6},{6,5},{7,8},{8,7},{9,10},{10,... | collective-permute-start | bytes 983048 | tf_op jit(solution)/shard_map/ppermute | solution.py:511
  66.5 0.0 collective-permute-done.7.go
  66.5 0.6 shard_map.98
  67.1 2.1 %collective-permute-done.13.b4 = f32[40,8,128]{2,1,0:T(8,128)S(1)} collective-permute-done((f32[40,8,128]{2,1,0:T(8,128)S(1)}, f32[40,8,128]{2,1,0:T(8,128)S(1)}, u32[]{:S(2)}, u32[]{:S(2)}) %collective-permute-start.13) | collective-permute-done | bytes 163872 | tf_op jit(solution)/shard_map/ppermute | solution.py:511
  69.2 0.1 collective-permute-start.14
  69.3 2.9 %collective-permute-done.10.r1o = f32[53,8,128]{2,1,0:T(8,128)S(1)} collective-permute-done((f32[53,8,128]{2,1,0:T(8,128)S(1)}, f32[53,8,128]{2,1,0:T(8,128)S(1)}, u32[]{:S(2)}, u32[]{:S(2)}) %collective-permute-start.10) | collective-permute-done | bytes 217120 | tf_op jit(solution)/shard_map/ppermute | solution.py:511
  72.3 0.4 collective-permute-start.15
  72.7 6.6 %collective-permute-done.17.r2o = f32[80,8,128]{2,1,0:T(8,128)S(1)} collective-permute-done((f32[80,8,128]{2,1,0:T(8,128)S(1)}, f32[80,8,128]{2,1,0:T(8,128)S(1)}, u32[]{:S(2)}, u32[]{:S(2)}) %collective-permute-start.17) | collective-permute-done | bytes 327712 | tf_op jit(solution)/shard_map/ppermute | solution.py:511
  79.3 2.8 %collective-permute-done.15.r3o = f32[44,8,128]{2,1,0:T(8,128)S(1)} collective-permute-done((f32[44,8,128]{2,1,0:T(8,128)S(1)}, f32[44,8,128]{2,1,0:T(8,128)S(1)}, u32[]{:S(2)}, u32[]{:S(2)}) %collective-permute-start.15) | collective-permute-done | bytes 180256 | tf_op jit(solution)/shard_map/ppermute | solution.py:511
  82.1 5.9 %shard_map.99 = (f32[3,4,16,128]{3,2,1,0:T(8,128)S(1)}, f32[3,2,16,128]{3,2,1,0:T(8,128)S(1)}) custom-call(s32[2]{0:T(128)S(1)} %copy-done.11, f32[20,8,128]{2,1,0:T(8,128)S(1)} %get-tuple-element.32.b0, f32[20,8,128]{2,1,0:T(8,128)S(1)} %collective-permute-done.8.b1, f32[40,8,128]{2,1,0:T(8,128)S(1)} %collective-permute-done.11.b2, ...), custom_call_target="tpu_custom_call" | custom-call | tf_op jit(solution)/shard_map/pallas_call | solution.py:492
  88.0 0.1 collective-permute-start.18
  88.1 4.1 %collective-permute-done.18.other = f32[3,2,16,128]{3,2,1,0:T(8,128)S(1)} collective-permute-done((f32[3,2,16,128]{3,2,1,0:T(8,128)S(1)}, f32[3,2,16,128]{3,2,1,0:T(8,128)S(1)}, u32[]{:S(2)}, u32[]{:S(2)}) %collective-permute-start.18) | collective-permute-done | bytes 49184 | tf_op jit(solution)/shard_map/ppermute | solution.py:507
  92.2 4.0 %shard_map.100 = (f32[3,4,16,256]{3,2,1,0:T(8,128)}, f32[3,4,16,256]{3,2,1,0:T(8,128)}) custom-call(s32[2]{0:T(128)S(1)} %copy-done.11, f32[3,6,32,256]{3,2,1,0:T(8,128)S(1)} %get-tuple-element.30.pre, f32[10,16,256]{2,1,0:T(8,128)S(1)} %collective-permute-done.6.ge, f32[10,16,256]{2,1,0:T(8,128)S(1)} %collective-permute-done.7.go, ...), custom_call_target="tpu_custom_call" | custom-call | tf_op jit(solution)/shard_map/pallas_call | solution.py:492
  (26 shorter events, 0.1 us)
Async XLA Ops:
  0.6 30.7 %copy-start.6 = (f32[4,16,256]{2,1,0:T(8,128)S(1)}, f32[4,16,256]{2,1,0:T(8,128)}, u32[]{:S(2)}) copy-start(f32[4,16,256]{2,1,0:T(8,128)} %heat.1) | copy-start | bytes 196612
  0.6 30.7 %copy-start = (f32[3,4,16,256]{3,2,1,0:T(8,128)S(1)}, f32[3,4,16,256]{3,2,1,0:T(8,128)}, u32[]{:S(2)}) copy-start(f32[3,4,16,256]{3,2,1,0:T(8,128)} %main.3) | copy-start | bytes 589828
  0.7 30.6 %copy-start.1 = (f32[3,4,16,256]{3,2,1,0:T(8,128)S(1)}, f32[3,4,16,256]{3,2,1,0:T(8,128)}, u32[]{:S(2)}) copy-start(f32[3,4,16,256]{3,2,1,0:T(8,128)} %cross.3) | copy-start | bytes 589828
  0.7 30.6 %copy-start.7 = (f32[4,16,256]{2,1,0:T(8,128)S(1)}, f32[4,16,256]{2,1,0:T(8,128)}, u32[]{:S(2)}) copy-start(f32[4,16,256]{2,1,0:T(8,128)} %clear.1) | copy-start | bytes 196612
  0.7 30.6 %copy-start.8 = (s32[4,16,256]{2,1,0:T(8,128)S(1)}, s32[4,16,256]{2,1,0:T(8,128)}, u32[]{:S(2)}) copy-start(s32[4,16,256]{2,1,0:T(8,128)} %touch.1) | copy-start | bytes 196612
  0.7 30.6 %copy-start.2 = (f32[3,4,16,256]{3,2,1,0:T(8,128)S(1)}, f32[3,4,16,256]{3,2,1,0:T(8,128)}, u32[]{:S(2)}) copy-start(f32[3,4,16,256]{3,2,1,0:T(8,128)} %disp.1) | copy-start | bytes 589828
  0.7 30.6 %copy-start.3 = (f32[3,4,16,256]{3,2,1,0:T(8,128)S(1)}, f32[3,4,16,256]{3,2,1,0:T(8,128)}, u32[]{:S(2)}) copy-start(f32[3,4,16,256]{3,2,1,0:T(8,128)} %trac.1) | copy-start | bytes 589828
  0.7 30.6 %copy-start.5 = (s32[4,16,256]{2,1,0:T(8,128)S(1)}, s32[4,16,256]{2,1,0:T(8,128)}, u32[]{:S(2)}) copy-start(s32[4,16,256]{2,1,0:T(8,128)} %clip.3) | copy-start | bytes 196612
  4.6 12.4 %collective-permute-start = (f32[32,16,256]{2,1,0:T(8,128)}, f32[32,16,256]{2,1,0:T(8,128)S(1)}, u32[]{:S(2)}, u32[]{:S(2)}) collective-permute-start(f32[32,16,256]{2,1,0:T(8,128)} %get-tuple-element.24), channel_id=1, source_target_pairs={{0,16},{16,0},{32,48},{48,32},{64,80},{80,64},{96,112},{112,96},{1... | collective-permute-start | bytes 1572872 | tf_op jit(solution)/shard_map/ppermute | solution.py:507
  4.8 19.4 %collective-permute-start.1 = (f32[32,16,256]{2,1,0:T(8,128)}, f32[32,16,256]{2,1,0:T(8,128)S(1)}, u32[]{:S(2)}, u32[]{:S(2)}) collective-permute-start(f32[32,16,256]{2,1,0:T(8,128)} %get-tuple-element.25), channel_id=1, source_target_pairs={{0,240},{16,32},{32,16},{48,64},{64,48},{80,96},{96,80},{112,128},... | collective-permute-start | bytes 1572872 | tf_op jit(solution)/shard_map/ppermute | solution.py:511
  12.3 16.4 %collective-permute-start.2 = (f32[36,8,128]{2,1,0:T(8,128)}, f32[36,8,128]{2,1,0:T(8,128)S(1)}, u32[]{:S(2)}, u32[]{:S(2)}) collective-permute-start(f32[36,8,128]{2,1,0:T(8,128)} %get-tuple-element.26), channel_id=1, source_target_pairs={{0,1},{1,0},{2,3},{3,2},{4,5},{5,4},{6,7},{7,6},{8,9},{9,8},{10,11... | collective-permute-start | bytes 442376 | tf_op jit(solution)/shard_map/ppermute | solution.py:507
  12.3 16.4 %collective-permute-start.3 = (f32[36,8,128]{2,1,0:T(8,128)}, f32[36,8,128]{2,1,0:T(8,128)S(1)}, u32[]{:S(2)}, u32[]{:S(2)}) collective-permute-start(f32[36,8,128]{2,1,0:T(8,128)} %get-tuple-element.27), channel_id=1, source_target_pairs={{0,15},{1,2},{2,1},{3,4},{4,3},{5,6},{6,5},{7,8},{8,7},{9,10},{10,... | collective-permute-start | bytes 442376 | tf_op jit(solution)/shard_map/ppermute | solution.py:511
  24.2 0.6 copy-start.10
  25.4 3.3 %collective-permute-start.4 = (f32[13,8,128]{2,1,0:T(8,128)S(1)}, f32[13,8,128]{2,1,0:T(8,128)S(1)}, u32[]{:S(2)}, u32[]{:S(2)}) collective-permute-start(f32[13,8,128]{2,1,0:T(8,128)S(1)} %get-tuple-element.28), channel_id=1, source_target_pairs={{0,1},{1,0},{2,3},{3,2},{4,5},{5,4},{6,7},{7,6},{8,9},{9,8},{10,11... | collective-permute-start | bytes 159752 | tf_op jit(solution)/shard_map/ppermute | solution.py:507
  25.5 5.8 %collective-permute-start.5 = (f32[13,8,128]{2,1,0:T(8,128)S(1)}, f32[13,8,128]{2,1,0:T(8,128)S(1)}, u32[]{:S(2)}, u32[]{:S(2)}) collective-permute-start(f32[13,8,128]{2,1,0:T(8,128)S(1)} %get-tuple-element.29), channel_id=1, source_target_pairs={{0,15},{1,2},{2,1},{3,4},{4,3},{5,6},{6,5},{7,8},{8,7},{9,10},{10,... | collective-permute-start | bytes 159752 | tf_op jit(solution)/shard_map/ppermute | solution.py:511
  31.4 1.0 %copy-start.4 = (f32[6,4,16,256]{3,2,1,0:T(8,128)S(1)}, f32[6,4,16,256]{3,2,1,0:T(8,128)}, u32[]{:S(2)}) copy-start(f32[6,4,16,256]{3,2,1,0:T(8,128)} %get-tuple-element.22.kinv) | copy-start | bytes 1179652
  32.4 0.8 copy-start.9
  33.2 0.6 copy-start.11
  37.9 4.5 %collective-permute-start.8 = (f32[20,8,128]{2,1,0:T(8,128)S(1)}, f32[20,8,128]{2,1,0:T(8,128)S(1)}, u32[]{:S(2)}, u32[]{:S(2)}) collective-permute-start(f32[20,8,128]{2,1,0:T(8,128)S(1)} %get-tuple-element.32.b0), channel_id=1, source_target_pairs={{0,16},{16,0},{32,48},{48,32},{64,80},{80,64},{96,112},{112,96},{1... | collective-permute-start | bytes 245768 | tf_op jit(solution)/shard_map/ppermute | solution.py:507
  42.5 9.0 %collective-permute-start.11 = (f32[40,8,128]{2,1,0:T(8,128)S(1)}, f32[40,8,128]{2,1,0:T(8,128)S(1)}, u32[]{:S(2)}, u32[]{:S(2)}) collective-permute-start(f32[40,8,128]{2,1,0:T(8,128)S(1)} %pad_maximum_fusion.5), channel_id=1, source_target_pairs={{0,240},{16,32},{32,16},{48,64},{64,48},{80,96},{96,80},{112,128},... | collective-permute-start | bytes 491528 | tf_op jit(solution)/shard_map/ppermute | solution.py:511
  51.5 8.8 %collective-permute-start.12 = (f32[40,8,128]{2,1,0:T(8,128)S(1)}, f32[40,8,128]{2,1,0:T(8,128)S(1)}, u32[]{:S(2)}, u32[]{:S(2)}) collective-permute-start(f32[40,8,128]{2,1,0:T(8,128)S(1)} %collective-permute-done.11.b2), channel_id=1, source_target_pairs={{0,16},{16,0},{32,48},{48,32},{64,80},{80,64},{96,112},{112,96},{1... | collective-permute-start | bytes 491528 | tf_op jit(solution)/shard_map/ppermute | solution.py:507
  51.5 10.8 %collective-permute-start.6 = (f32[10,16,256]{2,1,0:T(8,128)S(1)}, f32[10,16,256]{2,1,0:T(8,128)S(1)}, u32[]{:S(2)}, u32[]{:S(2)}) collective-permute-start(f32[10,16,256]{2,1,0:T(8,128)S(1)} %get-tuple-element.31), channel_id=1, source_target_pairs={{0,16},{16,0},{32,48},{48,32},{64,80},{80,64},{96,112},{112,96},{1... | collective-permute-start | bytes 491528 | tf_op jit(solution)/shard_map/ppermute | solution.py:507
  53.5 13.0 %collective-permute-start.7 = (f32[10,16,256]{2,1,0:T(8,128)S(1)}, f32[10,16,256]{2,1,0:T(8,128)S(1)}, u32[]{:S(2)}, u32[]{:S(2)}) collective-permute-start(f32[10,16,256]{2,1,0:T(8,128)S(1)} %get-tuple-element.31), channel_id=1, source_target_pairs={{0,240},{16,32},{32,16},{48,64},{64,48},{80,96},{96,80},{112,128},... | collective-permute-start | bytes 491528 | tf_op jit(solution)/shard_map/ppermute | solution.py:511
  58.9 13.4 %collective-permute-start.10 = (f32[53,8,128]{2,1,0:T(8,128)S(1)}, f32[53,8,128]{2,1,0:T(8,128)S(1)}, u32[]{:S(2)}, u32[]{:S(2)}) collective-permute-start(f32[53,8,128]{2,1,0:T(8,128)S(1)} %get-tuple-element.44), channel_id=1, source_target_pairs={{0,15},{1,2},{2,1},{3,4},{4,3},{5,6},{6,5},{7,8},{8,7},{9,10},{10,... | collective-permute-start | bytes 651272 | tf_op jit(solution)/shard_map/ppermute | solution.py:511
  60.3 8.9 %collective-permute-start.13 = (f32[40,8,128]{2,1,0:T(8,128)S(1)}, f32[40,8,128]{2,1,0:T(8,128)S(1)}, u32[]{:S(2)}, u32[]{:S(2)}) collective-permute-start(f32[40,8,128]{2,1,0:T(8,128)S(1)} %collective-permute-done.12.b3), channel_id=1, source_target_pairs={{0,240},{16,32},{32,16},{48,64},{64,48},{80,96},{96,80},{112,128},... | collective-permute-start | bytes 491528 | tf_op jit(solution)/shard_map/ppermute | solution.py:511
  62.2 10.5 %collective-permute-start.16 = (f32[80,8,128]{2,1,0:T(8,128)S(1)}, f32[80,8,128]{2,1,0:T(8,128)S(1)}, u32[]{:S(2)}, u32[]{:S(2)}) collective-permute-start(f32[80,8,128]{2,1,0:T(8,128)S(1)} %constant_dynamic-update-slice_fusion), channel_id=1, source_target_pairs={{0,1},{1,0},{2,3},{3,2},{4,5},{5,4},{6,7},{7,6},{8,9},{9,8},{10,11... | collective-permute-start | bytes 983048 | tf_op jit(solution)/shard_map/ppermute | solution.py:507
  62.3 17.0 %collective-permute-start.17 = (f32[80,8,128]{2,1,0:T(8,128)S(1)}, f32[80,8,128]{2,1,0:T(8,128)S(1)}, u32[]{:S(2)}, u32[]{:S(2)}) collective-permute-start(f32[80,8,128]{2,1,0:T(8,128)S(1)} %constant_dynamic-update-slice_fusion), channel_id=1, source_target_pairs={{0,15},{1,2},{2,1},{3,4},{4,3},{5,6},{6,5},{7,8},{8,7},{9,10},{10,... | collective-permute-start | bytes 983048 | tf_op jit(solution)/shard_map/ppermute | solution.py:511
  66.5 6.2 %collective-permute-start.9 = (f32[53,8,128]{2,1,0:T(8,128)S(1)}, f32[53,8,128]{2,1,0:T(8,128)S(1)}, u32[]{:S(2)}, u32[]{:S(2)}) collective-permute-start(f32[53,8,128]{2,1,0:T(8,128)S(1)} %get-tuple-element.45), channel_id=1, source_target_pairs={{0,1},{1,0},{2,3},{3,2},{4,5},{5,4},{6,7},{7,6},{8,9},{9,8},{10,11... | collective-permute-start | bytes 651272 | tf_op jit(solution)/shard_map/ppermute | solution.py:507
  69.2 10.1 %collective-permute-start.14 = (f32[44,8,128]{2,1,0:T(8,128)S(1)}, f32[44,8,128]{2,1,0:T(8,128)S(1)}, u32[]{:S(2)}, u32[]{:S(2)}) collective-permute-start(f32[44,8,128]{2,1,0:T(8,128)S(1)} %get-tuple-element.43), channel_id=1, source_target_pairs={{0,1},{1,0},{2,3},{3,2},{4,5},{5,4},{6,7},{7,6},{8,9},{9,8},{10,11... | collective-permute-start | bytes 540680 | tf_op jit(solution)/shard_map/ppermute | solution.py:507
  72.3 9.8 %collective-permute-start.15 = (f32[44,8,128]{2,1,0:T(8,128)S(1)}, f32[44,8,128]{2,1,0:T(8,128)S(1)}, u32[]{:S(2)}, u32[]{:S(2)}) collective-permute-start(f32[44,8,128]{2,1,0:T(8,128)S(1)} %get-tuple-element.42), channel_id=1, source_target_pairs={{0,15},{1,2},{2,1},{3,4},{4,3},{5,6},{6,5},{7,8},{8,7},{9,10},{10,... | collective-permute-start | bytes 540680 | tf_op jit(solution)/shard_map/ppermute | solution.py:511
  88.0 4.2 %collective-permute-start.18 = (f32[3,2,16,128]{3,2,1,0:T(8,128)S(1)}, f32[3,2,16,128]{3,2,1,0:T(8,128)S(1)}, u32[]{:S(2)}, u32[]{:S(2)}) collective-permute-start(f32[3,2,16,128]{3,2,1,0:T(8,128)S(1)} %get-tuple-element.38), channel_id=1, source_target_pairs={{0,16},{16,0},{32,48},{48,32},{64,80},{80,64},{96,112},{112,96},{1... | collective-permute-start | bytes 147464 | tf_op jit(solution)/shard_map/ppermute | solution.py:507

commit v3 on v2

--- a/solution.py
+++ b/solution.py
@@ -166,20 +166,20 @@
             dst[2, p] = new[2]
             return carry
 
-        lax.fori_loop(0, planes, body, 0)
+        lax.fori_loop(0, planes, body, 0, unroll=4)
 
     one(v0, v1, 0, 8)
     one(v1, v2, 1, 6)
 
 
 def residual_plane(v2, force, main, cross, p):
-    own = [v2[c, p + 1][8:24] for c in range(3)]
+    own = [v2[c, p + 1][0:16] for c in range(3)]
     mat = [main[c, p] for c in range(3)] + [cross[c, p] for c in range(3)]
     kv = symmetric_times(mat, own)
     out = []
     for c in range(3):
-        near = v2[c, p, 8:24, :] + v2[c, p + 2, 8:24, :] + beside(v2[c, p + 1])[8:24]
-        out.append(force[c, p + 2, 8:24, :] - (kv[c] - near))
+        near = v2[c, p, 0:16, :] + v2[c, p + 2, 0:16, :] + beside(v2[c, p + 1])[0:16]
+        out.append(force[c, p + 2, 0:16, :] - (kv[c] - near))
     return out
 
 
@@ -200,30 +200,30 @@
     for f in range(4):
         for p in range(4):
             to = wide_to[f](p + 3)
-            to[8:24, :] = wide[f](p)
-            to[5:8, :], to[24:27, :] = get_rows(be, bo, up, inner, f * 4 + p, 0, 3)
+            to[0:16, :] = wide[f](p)
+            to[21:24, :], to[16:19, :] = get_rows(be, bo, up, inner, f * 4 + p, 0, 3)
         for side in range(2):
             low = side == 0
             for k in range(3):
                 to = wide_to[f](k if low else 7 + k)
-                to[8:24, :] = halo_plane(re, ro, even, inside, low, 3 * f + k)
+                to[0:16, :] = halo_plane(re, ro, even, inside, low, 3 * f + k)
             to = wide_to[f](2 if low else 7)
-            to[6:8, :], to[24:26, :] = get_rows(ce, co, up, inner, f * 2 + side, 0, 2)
+            to[22:24, :], to[16:18, :] = get_rows(ce, co, up, inner, f * 2 + side, 0, 2)
             to = wide_to[f](1 if low else 8)
-            to[7:8, :], to[24:25, :] = get_rows(ce, co, up, inner, f * 2 + side, 2, 1)
+            to[23:24, :], to[16:17, :] = get_rows(ce, co, up, inner, f * 2 + side, 2, 1)
     for f in range(10):
         for p in range(4):
             to = near_to[f](p + 2)
-            to[8:24, :] = near[f](p)
-            to[6:8, :], to[24:26, :] = get_rows(be, bo, up, inner, 16 + f * 2 + p // 2, 2 * (p % 2), 2)
+            to[0:16, :] = near[f](p)
+            to[22:24, :], to[16:18, :] = get_rows(be, bo, up, inner, 16 + f * 2 + p // 2, 2 * (p % 2), 2)
         for side in range(2):
             low = side == 0
             for k in range(2):
                 to = near_to[f](k if low else 6 + k)
-                to[8:24, :] = halo_plane(re, ro, even, inside, low, 12 + 2 * f + k)
+                to[0:16, :] = halo_plane(re, ro, even, inside, low, 12 + 2 * f + k)
             n = f * 2 + side
             to = near_to[f](1 if low else 6)
-            to[7:8, :], to[24:25, :] = get_rows(ce, co, up, inner, 8 + n // 4, n % 4, 1)
+            to[23:24, :], to[16:17, :] = get_rows(ce, co, up, inner, 8 + n // 4, n % 4, 1)
 
     def drift(p, carry):
         h = heat_x[p + 1]
@@ -231,7 +231,7 @@
         right = jnp.where(lane == 255, 0.0, pltpu.roll(h, 255, axis=1))
         left = jnp.where(lane == 0, 0.0, pltpu.roll(h, 1, axis=1))
         force_x[0, p] = force_x[0, p] - (heat_x[p + 2] - heat_x[p])
-        force_x[1, p] = force_x[1, p] - (pltpu.roll(h, 31, axis=0) - pltpu.roll(h, 1, axis=0))
+        force_x[1, p] = force_x[1, p] - (pltpu.roll(h, 23, axis=0) - pltpu.roll(h, 1, axis=0))
         force_x[2, p] = force_x[2, p] - (right - left)
         return carry
 
@@ -247,7 +247,7 @@
             cut = clip[p] == 1
             out[0] = jnp.where(cut, 0.0, out[0])
             gap = jnp.logical_and(touch[p] == 1, clip[p] != 1)
-            room = jnp.where(gap, clear[p] - v2[0, p + 1, 8:24, :], FREE)
+            room = jnp.where(gap, clear[p] - v2[0, p + 1, 0:16, :], FREE)
             part = out + [room] + [main[c, p] for c in range(3)] + [cross[c, p] for c in range(3)]
             if low is None:
                 low = part
@@ -276,15 +276,15 @@
     small_out[...] = small.reshape(20, 8, 128)
     for c in range(3):
         for k in range(2):
-            planes_out[2 * c + k] = v2[c, k + 2, 8:24, :]
+            planes_out[2 * c + k] = v2[c, k + 2, 0:16, :]
     for p in range(4):
         planes_out[6 + p] = clip[p].astype(F32)
     for c in range(3):
         for p in range(4):
-            put_rows(pe, po, up, c * 2 + p // 2, 2 * (p % 2), v2[c, p + 1, 8:24, :], 2, 1)
+            put_rows(pe, po, up, c * 2 + p // 2, 2 * (p % 2), v2[c, p + 1, 0:16, :], 2, 1)
         for side in range(2):
             n = 2 * c + side
-            put_rows(pe, po, up, 10 + n // 2, 2 * (n % 2), v2[c, 5 * side, 8:24, :], 2)
+            put_rows(pe, po, up, 10 + n // 2, 2 * (n % 2), v2[c, 5 * side, 0:16, :], 2)
     for p in range(4):
         put_rows(pe, po, up, 6 + p, 0, clip[p].astype(F32), 3)
 
@@ -333,12 +333,12 @@
                 a = jnp.where(real, re[r + t], 0.0)
                 b = jnp.where(jnp.logical_and(real, inner), ro[r + t], 0.0)
                 to = g.at[f, 2 * place + q]
-                to[0:8, :] = jnp.where(up, b, a)
-                to[8:16, :] = jnp.where(real, mine[m + t], 0.0)
-                to[16:24, :] = jnp.where(up, a, b)
+                to[0:8, :] = jnp.where(real, mine[m + t], 0.0)
+                to[8:16, :] = jnp.where(up, a, b)
+                to[16:24, :] = jnp.where(up, b, a)
             return carry
 
-        lax.fori_loop(0, 10, fill, 0)
+        lax.fori_loop(0, 10, fill, 0, unroll=2)
 
     def start(p, carry):
         inv = inverse(*[g[4 + k, p] for k in range(6)])
@@ -350,7 +350,7 @@
         va[2, p] = v[2]
         return carry
 
-    lax.fori_loop(0, 16, start, 0)
+    lax.fori_loop(0, 16, start, 0, unroll=4)
 
     def sweep(src, dst):
         def body(p, carry):
@@ -367,7 +367,7 @@
 
         return body
 
-    lax.fori_loop(1, 15, sweep(va, vb), 0)
+    lax.fori_loop(1, 15, sweep(va, vb), 0, unroll=4)
 
     def third(q, carry):
         total = None
@@ -397,7 +397,7 @@
         o3[q] = room
         return carry
 
-    lax.fori_loop(1, 7, third, 0)
+    lax.fori_loop(1, 7, third, 0, unroll=4)
 
     def lowest(q, carry):
         rest = []
@@ -412,14 +412,16 @@
                 va[c, p] = vb[c, p] + new[c]
         return carry
 
-    lax.fori_loop(2, 6, lowest, 0)
-    lax.fori_loop(5, 11, sweep(va, vb), 0)
-    lax.fori_loop(6, 10, sweep(vb, va), 0)
+    lax.fori_loop(2, 6, lowest, 0, unroll=4)
+    lax.fori_loop(5, 11, sweep(va, vb), 0, unroll=4)
+    lax.fori_loop(6, 10, sweep(vb, va), 0, unroll=4)
     for c in range(3):
         for k in range(4):
-            mid2[c, k] = va[c, 6 + k][4:20]
+            mid2[c, k, 0:10, :] = va[c, 6 + k, 0:10, :]
+            mid2[c, k, 10:12, :] = va[c, 6 + k, 22:24, :]
         for k in range(2):
-            own[c, k] = va[c, 8 - 2 * par + k][4:20]
+            own[c, k, 0:10, :] = va[c, 8 - 2 * par + k, 0:10, :]
+            own[c, k, 10:12, :] = va[c, 8 - 2 * par + k, 22:24, :]
 
 
 def finish(
@@ -434,30 +436,30 @@
             v0[c, p + 2] = pre[c, p]
         for p in range(4):
             to = v0.at[c, p + 3]
-            to[5:7, :], to[25:27, :] = get_rows(r1e, r1o, up, inner, 40 + c * 2 + p // 2, 2 * (p % 2), 2)
+            to[21:23, :], to[17:19, :] = get_rows(r1e, r1o, up, inner, 40 + c * 2 + p // 2, 2 * (p % 2), 2)
         for side in range(2):
             low = side == 0
             n = 2 * c + side
             to = v0.at[c, 2 if low else 7]
-            to[6:8, :], to[24:26, :] = get_rows(r1e, r1o, up, inner, 50 + n // 2, 2 * (n % 2), 2)
+            to[22:24, :], to[16:18, :] = get_rows(r1e, r1o, up, inner, 50 + n // 2, 2 * (n % 2), 2)
             for k in range(2):
                 to = v0.at[c, k if low else 8 + k]
-                to[8:24, :] = halo_plane(ge, go, even, inside, low, 2 * c + k)
+                to[0:16, :] = halo_plane(ge, go, even, inside, low, 2 * c + k)
             to = v0.at[c, 1 if low else 8]
-            to[7:8, :], to[24:25, :] = get_rows(r3e, r3o, up, inner, 40 + side, c, 1)
+            to[23:24, :], to[16:17, :] = get_rows(r3e, r3o, up, inner, 40 + side, c, 1)
     for p in range(4):
         to = clip_x.at[p + 3]
-        to[8:24, :] = clip[p].astype(F32)
-        to[5:8, :], to[24:27, :] = get_rows(r1e, r1o, up, inner, 46 + p, 0, 3)
+        to[0:16, :] = clip[p].astype(F32)
+        to[21:24, :], to[16:19, :] = get_rows(r1e, r1o, up, inner, 46 + p, 0, 3)
     for side in range(2):
         low = side == 0
         for k in range(3):
             to = clip_x.at[k if low else 7 + k]
-            to[8:24, :] = halo_plane(ge, go, even, inside, low, 6 + k + (1 if low else 0))
+            to[0:16, :] = halo_plane(ge, go, even, inside, low, 6 + k + (1 if low else 0))
         to = clip_x.at[2 if low else 7]
-        to[6:8, :], to[24:26, :] = get_rows(r3e, r3o, up, inner, 42 + side, 0, 2)
+        to[22:24, :], to[16:18, :] = get_rows(r3e, r3o, up, inner, 42 + side, 0, 2)
         to = clip_x.at[1 if low else 8]
-        to[7:8, :], to[24:25, :] = get_rows(r3e, r3o, up, inner, 42 + side, 2, 1)
+        to[23:24, :], to[16:17, :] = get_rows(r3e, r3o, up, inner, 42 + side, 2, 1)
     i, j = rows((128, 256)), lanes((128, 256))
     copy = jnp.where(lax.shift_right_logical(j, 1) == i, 1.0, 0.0)
     for c in range(3):
@@ -473,7 +475,7 @@
                 y = x[:, 128 * h : 128 * h + 128]
                 fine[h, pl.ds(0, 16, 2), :] = y
                 fine[h, pl.ds(1, 16, 2), :] = y
-            up2 = jnp.concatenate([fine[0], fine[1]], 1)
+            up2 = jnp.concatenate([fine[0, 0:24, :], fine[1, 0:24, :]], 1)
             for p in range(10):
                 if (p + 1) // 2 == k:
                     add = jnp.where(clip_x[p] == 1.0, 0.0, up2) if c == 0 else up2
@@ -483,7 +485,7 @@
         out = residual_plane(v2, force_x, main, cross, p)
         for c in range(3):
             residual[c, p] = out[c]
-            moved[c, p] = v2[c, p + 1, 8:24, :]
+            moved[c, p] = v2[c, p + 1, 0:16, :]
 
 
 def call(kernel, outs, scratch, *args, limit=0):
@@ -518,7 +520,7 @@
         load_pack,
         [six, own] + [(32, 16, 256)] * 2 + [(36, 8, 128)] * 2,
         [vec, vec, own, vec, vec, own, pltpu.VMEM(own, jnp.int32), pltpu.SemaphoreType.DMA((7,))],
-        pos, disp, trac, heat, main, cross, clear, touch, limit=58 * 1024 * 1024,
+        pos, *[pltpu.with_memory_space_constraint(z, pltpu.HBM) for z in (disp, trac, heat, main, cross, clear, touch)], limit=32 * 1024 * 1024,
     )
     re, ro = swap_even(me, "grp"), swap_odd(mo, "grp")
     re_b, ro_b = swap_even(be, "brick"), swap_odd(bo, "brick")
@@ -526,9 +528,9 @@
     re_c, ro_c = swap_even(ce, "brick"), swap_odd(co, "brick")
     force_x, kinv_x, obst_x, pre, b0, planes, pe, po = call(
         presmooth,
-        [(3, 8, 32, 256), (6, 8, 32, 256), (8, 32, 256), (3, 6, 32, 256), (20, 8, 128),
+        [(3, 8, 24, 256), (6, 8, 24, 256), (8, 24, 256), (3, 6, 24, 256), (20, 8, 128),
          (10, 16, 256), (13, 8, 128), (13, 8, 128)],
-        [(3, 10, 32, 256), (10, 32, 256), (3, 8, 32, 256), (10, 2, 16, 128), (160, 256)],
+        [(3, 10, 24, 256), (10, 24, 256), (3, 8, 24, 256), (10, 2, 16, 128), (160, 256)],
         pos, disp, heat, clip, trac, kinv, obst, main, cross, clear, touch,
         re, ro, re_b, ro_b, re_c, ro_c,
     )
@@ -557,7 +559,7 @@
         call(
             finish,
             [vec, vec],
-            [(3, 10, 32, 256), (3, 8, 32, 256), (3, 6, 32, 256), (10, 32, 256), (3, 6, 16, 128),
+            [(3, 10, 24, 256), (3, 8, 24, 256), (3, 6, 24, 256), (10, 24, 256), (3, 6, 16, 128),
              (2, 32, 128)],
             pos, pre, ge, go, r1e, r1o, r3e, r3o, mid2, other, force_x, kinv_x, obst_x, clip,
             main, cross,

time: 97.8 us -> 88.8 us (0.908)
  Pallas kernels: 18.4 us -> 13.3 us
  local copies, waits for them, and re-layouts: 3.12 us -> 0.07 us
    pallas_call x6, Pallas kernels: 18.4 us -> 13.3 us  [call(): pl.pallas_call(kernel, out_shape=[jax.ShapeDtypeStruct(x, F32) for x in o...]
    unnamed x25 -> x17, local copies, waits for them, and re-layouts: 3.1 us -> 0.06 us
where the time goes in v3:
time: 88.8 us; the launch traced here: 87.3 us
  waiting for transfers between devices  37.7 us (42%)
  starting transfers between devices  35.2 us (40%)
  Pallas kernels  13.3 us (15%)
    ppermute x9, starting transfers between devices, swap_odd(): return lax.ppermute(x, axis, ODD)  32.4 us
    ppermute x9, waiting for transfers between devices, swap_odd(): return lax.ppermute(x, axis, ODD)  27.8 us
    pallas_call x6, Pallas kernels, call(): pl.pallas_call(kernel, out_shape=[jax.ShapeDtypeStruct(x, F32) for x in o...  13.3 us
    ppermute x10, waiting for transfers between devices, swap_even(): return lax.ppermute(x, axis, EVEN)  9.88 us
    ppermute x10, starting transfers between devices, swap_even(): return lax.ppermute(x, axis, EVEN)  2.76 us
  transfers between devices with their start and end apart: 19, of which 10 were waited for; matrix products, arithmetic and copies ran while one was open for 0% of the time, Pallas kernels for 1%

profile of v3, /device:TPU:0, one launch (start us, length us, event | category | flops | bytes accessed | tf_op | source)
XLA Modules:
  0.0 87.3 jit_solution(10685227528841189331)
XLA Ops:
  0.6 0.0 copy-start.5
  0.6 0.0 copy-start
  0.7 0.0 copy-start.1
  0.7 0.0 copy-start.6
  0.7 0.0 copy-start.7
  0.7 0.0 copy-start.2
  0.7 0.0 copy-start.3
  0.7 0.1 pad_add_fusion.pos
  0.8 2.0 %shard_map.95 = (f32[6,4,16,256]{3,2,1,0:T(8,128)S(1)}, f32[4,16,256]{2,1,0:T(8,128)S(1)}, f32[32,16,256]{2,1,0:T(8,128)S(1)}, f32[32,16,256]{2,1,0:T(8,128)S(1)...) custom-call(s32[2]{0:T(128)S(1)} %pad_add_fusion.pos, f32[3,4,16,256]{3,2,1,0:T(8,128)} %disp.1, ...), custom_call_target="tpu_custom_call" | custom-call | tf_op jit(solution)/shard_map/pallas_call | solution.py:494
  2.8 0.3 collective-permute-start
  3.1 7.4 %collective-permute-start.1 = (f32[32,16,256]{2,1,0:T(8,128)S(1)}, f32[32,16,256]{2,1,0:T(8,128)S(1)}, u32[]{:S(2)}, u32[]{:S(2)}) collective-permute-start(f32[32,16,256]{2,1,0:T(8,128)S(1)} %get-tuple-element.25), channel_id=1, source_target_pairs={{0,240},{16,32},{32,16},{48,64},{64,48},{80,96},{96,80},{112,128},... | collective-permute-start | bytes 1572872 | tf_op jit(solution)/shard_map/ppermute | solution.py:513
  10.5 0.0 collective-permute-start.2
  10.5 3.2 %collective-permute-start.3 = (f32[36,8,128]{2,1,0:T(8,128)S(1)}, f32[36,8,128]{2,1,0:T(8,128)S(1)}, u32[]{:S(2)}, u32[]{:S(2)}) collective-permute-start(f32[36,8,128]{2,1,0:T(8,128)S(1)} %get-tuple-element.27), channel_id=1, source_target_pairs={{0,15},{1,2},{2,1},{3,4},{4,3},{5,6},{6,5},{7,8},{8,7},{9,10},{10,... | collective-permute-start | bytes 442376 | tf_op jit(solution)/shard_map/ppermute | solution.py:513
  13.6 1.4 %collective-permute-done.re = f32[32,16,256]{2,1,0:T(8,128)S(1)} collective-permute-done((f32[32,16,256]{2,1,0:T(8,128)S(1)}, f32[32,16,256]{2,1,0:T(8,128)S(1)}, u32[]{:S(2)}, u32[]{:S(2)}) %collective-permute-start) | collective-permute-done | bytes 524320 | tf_op jit(solution)/shard_map/ppermute | solution.py:509
  15.0 7.2 %collective-permute-done.1.ro = f32[32,16,256]{2,1,0:T(8,128)S(1)} collective-permute-done((f32[32,16,256]{2,1,0:T(8,128)S(1)}, f32[32,16,256]{2,1,0:T(8,128)S(1)}, u32[]{:S(2)}, u32[]{:S(2)}) %collective-permute-start.1) | collective-permute-done | bytes 524320 | tf_op jit(solution)/shard_map/ppermute | solution.py:513
  22.2 0.6 shard_map.96
  22.9 0.1 collective-permute-start.4
  23.0 3.1 %collective-permute-start.5 = (f32[13,8,128]{2,1,0:T(8,128)S(1)}, f32[13,8,128]{2,1,0:T(8,128)S(1)}, u32[]{:S(2)}, u32[]{:S(2)}) collective-permute-start(f32[13,8,128]{2,1,0:T(8,128)S(1)} %get-tuple-element.29), channel_id=1, source_target_pairs={{0,15},{1,2},{2,1},{3,4},{4,3},{5,6},{6,5},{7,8},{8,7},{9,10},{10,... | collective-permute-start | bytes 159752 | tf_op jit(solution)/shard_map/ppermute | solution.py:513
  26.1 0.0 collective-permute-done.2.be
  26.1 0.0 collective-permute-done.3.bo
  26.1 0.0 collective-permute-done.4.ce
  26.1 2.6 %collective-permute-done.5.co = f32[13,8,128]{2,1,0:T(8,128)S(1)} collective-permute-done((f32[13,8,128]{2,1,0:T(8,128)S(1)}, f32[13,8,128]{2,1,0:T(8,128)S(1)}, u32[]{:S(2)}, u32[]{:S(2)}) %collective-permute-start.5) | collective-permute-done | bytes 53280 | tf_op jit(solution)/shard_map/ppermute | solution.py:513
  28.8 3.2 %shard_map.97 = (f32[3,8,24,256]{3,2,1,0:T(8,128)S(1)}, f32[6,8,24,256]{3,2,1,0:T(8,128)S(1)}, f32[8,24,256]{2,1,0:T(8,128)S(1)}, f32[3,6,24,256]{3,2,1,0:T(8,12...) custom-call(s32[2]{0:T(128)S(1)} %pad_add_fusion.pos, ...), custom_call_target="tpu_custom_call" | custom-call | tf_op jit(solution)/shard_map/pallas_call | solution.py:494
  32.0 0.1 collective-permute-start.8
  32.1 4.4 %collective-permute-done.8.b1 = f32[20,8,128]{2,1,0:T(8,128)S(1)} collective-permute-done((f32[20,8,128]{2,1,0:T(8,128)S(1)}, f32[20,8,128]{2,1,0:T(8,128)S(1)}, u32[]{:S(2)}, u32[]{:S(2)}) %collective-permute-start.8) | collective-permute-done | bytes 81952 | tf_op jit(solution)/shard_map/ppermute | solution.py:509
  36.5 5.4 %collective-permute-start.11 = (f32[40,8,128]{2,1,0:T(8,128)S(1)}, f32[40,8,128]{2,1,0:T(8,128)S(1)}, u32[]{:S(2)}, u32[]{:S(2)}) collective-permute-start(f32[40,8,128]{2,1,0:T(8,128)S(1)} %pad_maximum_fusion.5), channel_id=1, source_target_pairs={{0,240},{16,32},{32,16},{48,64},{64,48},{80,96},{96,80},{112,128},... | collective-permute-start | bytes 491528 | tf_op jit(solution)/shard_map/ppermute | solution.py:513
  41.9 3.6 %collective-permute-done.11.b2 = f32[40,8,128]{2,1,0:T(8,128)S(1)} collective-permute-done((f32[40,8,128]{2,1,0:T(8,128)S(1)}, f32[40,8,128]{2,1,0:T(8,128)S(1)}, u32[]{:S(2)}, u32[]{:S(2)}) %collective-permute-start.11) | collective-permute-done | bytes 163872 | tf_op jit(solution)/shard_map/ppermute | solution.py:513
  45.5 2.0 %collective-permute-start.6 = (f32[10,16,256]{2,1,0:T(8,128)S(1)}, f32[10,16,256]{2,1,0:T(8,128)S(1)}, u32[]{:S(2)}, u32[]{:S(2)}) collective-permute-start(f32[10,16,256]{2,1,0:T(8,128)S(1)} %get-tuple-element.31), channel_id=1, source_target_pairs={{0,16},{16,0},{32,48},{48,32},{64,80},{80,64},{96,112},{112,96},{1... | collective-permute-start | bytes 491528 | tf_op jit(solution)/shard_map/ppermute | solution.py:509
  47.6 5.4 %collective-permute-start.7 = (f32[10,16,256]{2,1,0:T(8,128)S(1)}, f32[10,16,256]{2,1,0:T(8,128)S(1)}, u32[]{:S(2)}, u32[]{:S(2)}) collective-permute-start(f32[10,16,256]{2,1,0:T(8,128)S(1)} %get-tuple-element.31), channel_id=1, source_target_pairs={{0,240},{16,32},{32,16},{48,64},{64,48},{80,96},{96,80},{112,128},... | collective-permute-start | bytes 491528 | tf_op jit(solution)/shard_map/ppermute | solution.py:513
  52.9 1.4 %collective-permute-start.10 = (f32[53,8,128]{2,1,0:T(8,128)S(1)}, f32[53,8,128]{2,1,0:T(8,128)S(1)}, u32[]{:S(2)}, u32[]{:S(2)}) collective-permute-start(f32[53,8,128]{2,1,0:T(8,128)S(1)} %get-tuple-element.44), channel_id=1, source_target_pairs={{0,15},{1,2},{2,1},{3,4},{4,3},{5,6},{6,5},{7,8},{8,7},{9,10},{10,... | collective-permute-start | bytes 651272 | tf_op jit(solution)/shard_map/ppermute | solution.py:513
  54.3 1.9 %collective-permute-start.13 = (f32[40,8,128]{2,1,0:T(8,128)S(1)}, f32[40,8,128]{2,1,0:T(8,128)S(1)}, u32[]{:S(2)}, u32[]{:S(2)}) collective-permute-start(f32[40,8,128]{2,1,0:T(8,128)S(1)} %collective-permute-done.12.b3), channel_id=1, source_target_pairs={{0,240},{16,32},{32,16},{48,64},{64,48},{80,96},{96,80},{112,128},... | collective-permute-start | bytes 491528 | tf_op jit(solution)/shard_map/ppermute | solution.py:513
  56.2 0.1 collective-permute-start.16
  56.3 4.2 %collective-permute-start.17 = (f32[80,8,128]{2,1,0:T(8,128)S(1)}, f32[80,8,128]{2,1,0:T(8,128)S(1)}, u32[]{:S(2)}, u32[]{:S(2)}) collective-permute-start(f32[80,8,128]{2,1,0:T(8,128)S(1)} %constant_dynamic-update-slice_fusion), channel_id=1, source_target_pairs={{0,15},{1,2},{2,1},{3,4},{4,3},{5,6},{6,5},{7,8},{8,7},{9,10},{10,... | collective-permute-start | bytes 983048 | tf_op jit(solution)/shard_map/ppermute | solution.py:513
  60.6 0.0 collective-permute-done.7.go
  60.6 0.0 collective-permute-start.9
  60.6 0.6 shard_map.98
  61.1 2.1 %collective-permute-done.13.b4 = f32[40,8,128]{2,1,0:T(8,128)S(1)} collective-permute-done((f32[40,8,128]{2,1,0:T(8,128)S(1)}, f32[40,8,128]{2,1,0:T(8,128)S(1)}, u32[]{:S(2)}, u32[]{:S(2)}) %collective-permute-start.13) | collective-permute-done | bytes 163872 | tf_op jit(solution)/shard_map/ppermute | solution.py:513
  63.3 0.1 collective-permute-start.14
  63.4 2.9 %collective-permute-done.10.r1o = f32[53,8,128]{2,1,0:T(8,128)S(1)} collective-permute-done((f32[53,8,128]{2,1,0:T(8,128)S(1)}, f32[53,8,128]{2,1,0:T(8,128)S(1)}, u32[]{:S(2)}, u32[]{:S(2)}) %collective-permute-start.10) | collective-permute-done | bytes 217120 | tf_op jit(solution)/shard_map/ppermute | solution.py:513
  66.3 0.4 collective-permute-start.15
  66.8 0.0 collective-permute-done.9.r1e
  66.8 0.0 collective-permute-done.16.r2e
  66.8 6.6 %collective-permute-done.17.r2o = f32[80,8,128]{2,1,0:T(8,128)S(1)} collective-permute-done((f32[80,8,128]{2,1,0:T(8,128)S(1)}, f32[80,8,128]{2,1,0:T(8,128)S(1)}, u32[]{:S(2)}, u32[]{:S(2)}) %collective-permute-start.17) | collective-permute-done | bytes 327712 | tf_op jit(solution)/shard_map/ppermute | solution.py:513
  73.3 2.8 %collective-permute-done.15.r3o = f32[44,8,128]{2,1,0:T(8,128)S(1)} collective-permute-done((f32[44,8,128]{2,1,0:T(8,128)S(1)}, f32[44,8,128]{2,1,0:T(8,128)S(1)}, u32[]{:S(2)}, u32[]{:S(2)}) %collective-permute-start.15) | collective-permute-done | bytes 180256 | tf_op jit(solution)/shard_map/ppermute | solution.py:513
  76.2 3.9 %shard_map.99 = (f32[3,4,16,128]{3,2,1,0:T(8,128)S(1)}, f32[3,2,16,128]{3,2,1,0:T(8,128)S(1)}) custom-call(s32[2]{0:T(128)S(1)} %pad_add_fusion.pos, f32[20,8,128]{2,1,0:T(8,128)S(1)} %get-tuple-element.32.b0, f32[20,8,128]{2,1,0:T(8,128)S(1)} %collective-permute-done.8.b1, f32[40,8,128]{2,1,0:T(8,128)S(1)} %collective-permute-done.11.b2, ...), custom_call_target="tpu_custom_call" | custom-call | tf_op jit(solution)/shard_map/pallas_call | solution.py:494
  80.1 0.1 collective-permute-start.18
  80.1 4.1 %collective-permute-done.18.other = f32[3,2,16,128]{3,2,1,0:T(8,128)S(1)} collective-permute-done((f32[3,2,16,128]{3,2,1,0:T(8,128)S(1)}, f32[3,2,16,128]{3,2,1,0:T(8,128)S(1)}, u32[]{:S(2)}, u32[]{:S(2)}) %collective-permute-start.18) | collective-permute-done | bytes 49184 | tf_op jit(solution)/shard_map/ppermute | solution.py:509
  84.2 3.1 %shard_map.100 = (f32[3,4,16,256]{3,2,1,0:T(8,128)}, f32[3,4,16,256]{3,2,1,0:T(8,128)}) custom-call(s32[2]{0:T(128)S(1)} %pad_add_fusion.pos, f32[3,6,24,256]{3,2,1,0:T(8,128)S(1)} %get-tuple-element.30.pre, f32[10,16,256]{2,1,0:T(8,128)S(1)} %collective-permute-done.6.ge, f32[10,16,256]{2,1,0:T(8,128)S(1)} %collective-permute-done.7.go, ...), custom_call_target="tpu_custom_call" | custom-call | tf_op jit(solution)/shard_map/pallas_call | solution.py:494
  (18 shorter events, 0.1 us)
Async XLA Ops:
  0.6 28.1 %copy-start.5 = (f32[4,16,256]{2,1,0:T(8,128)S(1)}, f32[4,16,256]{2,1,0:T(8,128)}, u32[]{:S(2)}) copy-start(f32[4,16,256]{2,1,0:T(8,128)} %heat.1) | copy-start | bytes 196612
  0.6 28.1 %copy-start = (f32[3,4,16,256]{3,2,1,0:T(8,128)S(1)}, f32[3,4,16,256]{3,2,1,0:T(8,128)}, u32[]{:S(2)}) copy-start(f32[3,4,16,256]{3,2,1,0:T(8,128)} %main.3) | copy-start | bytes 589828
  0.7 28.1 %copy-start.1 = (f32[3,4,16,256]{3,2,1,0:T(8,128)S(1)}, f32[3,4,16,256]{3,2,1,0:T(8,128)}, u32[]{:S(2)}) copy-start(f32[3,4,16,256]{3,2,1,0:T(8,128)} %cross.3) | copy-start | bytes 589828
  0.7 28.1 %copy-start.6 = (f32[4,16,256]{2,1,0:T(8,128)S(1)}, f32[4,16,256]{2,1,0:T(8,128)}, u32[]{:S(2)}) copy-start(f32[4,16,256]{2,1,0:T(8,128)} %clear.1) | copy-start | bytes 196612
  0.7 28.1 %copy-start.7 = (s32[4,16,256]{2,1,0:T(8,128)S(1)}, s32[4,16,256]{2,1,0:T(8,128)}, u32[]{:S(2)}) copy-start(s32[4,16,256]{2,1,0:T(8,128)} %touch.1) | copy-start | bytes 196612
  0.7 28.1 %copy-start.2 = (f32[3,4,16,256]{3,2,1,0:T(8,128)S(1)}, f32[3,4,16,256]{3,2,1,0:T(8,128)}, u32[]{:S(2)}) copy-start(f32[3,4,16,256]{3,2,1,0:T(8,128)} %disp.1) | copy-start | bytes 589828
  0.7 28.1 %copy-start.3 = (f32[3,4,16,256]{3,2,1,0:T(8,128)S(1)}, f32[3,4,16,256]{3,2,1,0:T(8,128)}, u32[]{:S(2)}) copy-start(f32[3,4,16,256]{3,2,1,0:T(8,128)} %trac.1) | copy-start | bytes 589828
  0.7 28.0 %copy-start.4 = (s32[4,16,256]{2,1,0:T(8,128)S(1)}, s32[4,16,256]{2,1,0:T(8,128)}, u32[]{:S(2)}) copy-start(s32[4,16,256]{2,1,0:T(8,128)} %clip.3) | copy-start | bytes 196612
  2.8 12.2 %collective-permute-start = (f32[32,16,256]{2,1,0:T(8,128)S(1)}, f32[32,16,256]{2,1,0:T(8,128)S(1)}, u32[]{:S(2)}, u32[]{:S(2)}) collective-permute-start(f32[32,16,256]{2,1,0:T(8,128)S(1)} %get-tuple-element.24), channel_id=1, source_target_pairs={{0,16},{16,0},{32,48},{48,32},{64,80},{80,64},{96,112},{112,96},{1... | collective-permute-start | bytes 1572872 | tf_op jit(solution)/shard_map/ppermute | solution.py:509
  3.1 19.1 %collective-permute-start.1 = (f32[32,16,256]{2,1,0:T(8,128)S(1)}, f32[32,16,256]{2,1,0:T(8,128)S(1)}, u32[]{:S(2)}, u32[]{:S(2)}) collective-permute-start(f32[32,16,256]{2,1,0:T(8,128)S(1)} %get-tuple-element.25), channel_id=1, source_target_pairs={{0,240},{16,32},{32,16},{48,64},{64,48},{80,96},{96,80},{112,128},... | collective-permute-start | bytes 1572872 | tf_op jit(solution)/shard_map/ppermute | solution.py:513
  10.5 15.6 %collective-permute-start.2 = (f32[36,8,128]{2,1,0:T(8,128)S(1)}, f32[36,8,128]{2,1,0:T(8,128)S(1)}, u32[]{:S(2)}, u32[]{:S(2)}) collective-permute-start(f32[36,8,128]{2,1,0:T(8,128)S(1)} %get-tuple-element.26), channel_id=1, source_target_pairs={{0,1},{1,0},{2,3},{3,2},{4,5},{5,4},{6,7},{7,6},{8,9},{9,8},{10,11... | collective-permute-start | bytes 442376 | tf_op jit(solution)/shard_map/ppermute | solution.py:509
  10.5 15.6 %collective-permute-start.3 = (f32[36,8,128]{2,1,0:T(8,128)S(1)}, f32[36,8,128]{2,1,0:T(8,128)S(1)}, u32[]{:S(2)}, u32[]{:S(2)}) collective-permute-start(f32[36,8,128]{2,1,0:T(8,128)S(1)} %get-tuple-element.27), channel_id=1, source_target_pairs={{0,15},{1,2},{2,1},{3,4},{4,3},{5,6},{6,5},{7,8},{8,7},{9,10},{10,... | collective-permute-start | bytes 442376 | tf_op jit(solution)/shard_map/ppermute | solution.py:513
  22.9 3.3 %collective-permute-start.4 = (f32[13,8,128]{2,1,0:T(8,128)S(1)}, f32[13,8,128]{2,1,0:T(8,128)S(1)}, u32[]{:S(2)}, u32[]{:S(2)}) collective-permute-start(f32[13,8,128]{2,1,0:T(8,128)S(1)} %get-tuple-element.28), channel_id=1, source_target_pairs={{0,1},{1,0},{2,3},{3,2},{4,5},{5,4},{6,7},{7,6},{8,9},{9,8},{10,11... | collective-permute-start | bytes 159752 | tf_op jit(solution)/shard_map/ppermute | solution.py:509
  23.0 5.8 %collective-permute-start.5 = (f32[13,8,128]{2,1,0:T(8,128)S(1)}, f32[13,8,128]{2,1,0:T(8,128)S(1)}, u32[]{:S(2)}, u32[]{:S(2)}) collective-permute-start(f32[13,8,128]{2,1,0:T(8,128)S(1)} %get-tuple-element.29), channel_id=1, source_target_pairs={{0,15},{1,2},{2,1},{3,4},{4,3},{5,6},{6,5},{7,8},{8,7},{9,10},{10,... | collective-permute-start | bytes 159752 | tf_op jit(solution)/shard_map/ppermute | solution.py:513
  32.0 4.5 %collective-permute-start.8 = (f32[20,8,128]{2,1,0:T(8,128)S(1)}, f32[20,8,128]{2,1,0:T(8,128)S(1)}, u32[]{:S(2)}, u32[]{:S(2)}) collective-permute-start(f32[20,8,128]{2,1,0:T(8,128)S(1)} %get-tuple-element.32.b0), channel_id=1, source_target_pairs={{0,16},{16,0},{32,48},{48,32},{64,80},{80,64},{96,112},{112,96},{1... | collective-permute-start | bytes 245768 | tf_op jit(solution)/shard_map/ppermute | solution.py:509
  36.5 9.0 %collective-permute-start.11 = (f32[40,8,128]{2,1,0:T(8,128)S(1)}, f32[40,8,128]{2,1,0:T(8,128)S(1)}, u32[]{:S(2)}, u32[]{:S(2)}) collective-permute-start(f32[40,8,128]{2,1,0:T(8,128)S(1)} %pad_maximum_fusion.5), channel_id=1, source_target_pairs={{0,240},{16,32},{32,16},{48,64},{64,48},{80,96},{96,80},{112,128},... | collective-permute-start | bytes 491528 | tf_op jit(solution)/shard_map/ppermute | solution.py:513
  45.5 8.8 %collective-permute-start.12 = (f32[40,8,128]{2,1,0:T(8,128)S(1)}, f32[40,8,128]{2,1,0:T(8,128)S(1)}, u32[]{:S(2)}, u32[]{:S(2)}) collective-permute-start(f32[40,8,128]{2,1,0:T(8,128)S(1)} %collective-permute-done.11.b2), channel_id=1, source_target_pairs={{0,16},{16,0},{32,48},{48,32},{64,80},{80,64},{96,112},{112,96},{1... | collective-permute-start | bytes 491528 | tf_op jit(solution)/shard_map/ppermute | solution.py:509
  45.5 10.8 %collective-permute-start.6 = (f32[10,16,256]{2,1,0:T(8,128)S(1)}, f32[10,16,256]{2,1,0:T(8,128)S(1)}, u32[]{:S(2)}, u32[]{:S(2)}) collective-permute-start(f32[10,16,256]{2,1,0:T(8,128)S(1)} %get-tuple-element.31), channel_id=1, source_target_pairs={{0,16},{16,0},{32,48},{48,32},{64,80},{80,64},{96,112},{112,96},{1... | collective-permute-start | bytes 491528 | tf_op jit(solution)/shard_map/ppermute | solution.py:509
  47.6 13.0 %collective-permute-start.7 = (f32[10,16,256]{2,1,0:T(8,128)S(1)}, f32[10,16,256]{2,1,0:T(8,128)S(1)}, u32[]{:S(2)}, u32[]{:S(2)}) collective-permute-start(f32[10,16,256]{2,1,0:T(8,128)S(1)} %get-tuple-element.31), channel_id=1, source_target_pairs={{0,240},{16,32},{32,16},{48,64},{64,48},{80,96},{96,80},{112,128},... | collective-permute-start | bytes 491528 | tf_op jit(solution)/shard_map/ppermute | solution.py:513
  52.9 13.4 %collective-permute-start.10 = (f32[53,8,128]{2,1,0:T(8,128)S(1)}, f32[53,8,128]{2,1,0:T(8,128)S(1)}, u32[]{:S(2)}, u32[]{:S(2)}) collective-permute-start(f32[53,8,128]{2,1,0:T(8,128)S(1)} %get-tuple-element.44), channel_id=1, source_target_pairs={{0,15},{1,2},{2,1},{3,4},{4,3},{5,6},{6,5},{7,8},{8,7},{9,10},{10,... | collective-permute-start | bytes 651272 | tf_op jit(solution)/shard_map/ppermute | solution.py:513
  54.3 8.9 %collective-permute-start.13 = (f32[40,8,128]{2,1,0:T(8,128)S(1)}, f32[40,8,128]{2,1,0:T(8,128)S(1)}, u32[]{:S(2)}, u32[]{:S(2)}) collective-permute-start(f32[40,8,128]{2,1,0:T(8,128)S(1)} %collective-permute-done.12.b3), channel_id=1, source_target_pairs={{0,240},{16,32},{32,16},{48,64},{64,48},{80,96},{96,80},{112,128},... | collective-permute-start | bytes 491528 | tf_op jit(solution)/shard_map/ppermute | solution.py:513
  56.2 10.5 %collective-permute-start.16 = (f32[80,8,128]{2,1,0:T(8,128)S(1)}, f32[80,8,128]{2,1,0:T(8,128)S(1)}, u32[]{:S(2)}, u32[]{:S(2)}) collective-permute-start(f32[80,8,128]{2,1,0:T(8,128)S(1)} %constant_dynamic-update-slice_fusion), channel_id=1, source_target_pairs={{0,1},{1,0},{2,3},{3,2},{4,5},{5,4},{6,7},{7,6},{8,9},{9,8},{10,11... | collective-permute-start | bytes 983048 | tf_op jit(solution)/shard_map/ppermute | solution.py:509
  56.3 17.0 %collective-permute-start.17 = (f32[80,8,128]{2,1,0:T(8,128)S(1)}, f32[80,8,128]{2,1,0:T(8,128)S(1)}, u32[]{:S(2)}, u32[]{:S(2)}) collective-permute-start(f32[80,8,128]{2,1,0:T(8,128)S(1)} %constant_dynamic-update-slice_fusion), channel_id=1, source_target_pairs={{0,15},{1,2},{2,1},{3,4},{4,3},{5,6},{6,5},{7,8},{8,7},{9,10},{10,... | collective-permute-start | bytes 983048 | tf_op jit(solution)/shard_map/ppermute | solution.py:513
  60.6 6.2 %collective-permute-start.9 = (f32[53,8,128]{2,1,0:T(8,128)S(1)}, f32[53,8,128]{2,1,0:T(8,128)S(1)}, u32[]{:S(2)}, u32[]{:S(2)}) collective-permute-start(f32[53,8,128]{2,1,0:T(8,128)S(1)} %get-tuple-element.45), channel_id=1, source_target_pairs={{0,1},{1,0},{2,3},{3,2},{4,5},{5,4},{6,7},{7,6},{8,9},{9,8},{10,11... | collective-permute-start | bytes 651272 | tf_op jit(solution)/shard_map/ppermute | solution.py:509
  63.3 10.1 %collective-permute-start.14 = (f32[44,8,128]{2,1,0:T(8,128)S(1)}, f32[44,8,128]{2,1,0:T(8,128)S(1)}, u32[]{:S(2)}, u32[]{:S(2)}) collective-permute-start(f32[44,8,128]{2,1,0:T(8,128)S(1)} %get-tuple-element.43), channel_id=1, source_target_pairs={{0,1},{1,0},{2,3},{3,2},{4,5},{5,4},{6,7},{7,6},{8,9},{9,8},{10,11... | collective-permute-start | bytes 540680 | tf_op jit(solution)/shard_map/ppermute | solution.py:509
  66.3 9.9 %collective-permute-start.15 = (f32[44,8,128]{2,1,0:T(8,128)S(1)}, f32[44,8,128]{2,1,0:T(8,128)S(1)}, u32[]{:S(2)}, u32[]{:S(2)}) collective-permute-start(f32[44,8,128]{2,1,0:T(8,128)S(1)} %get-tuple-element.42), channel_id=1, source_target_pairs={{0,15},{1,2},{2,1},{3,4},{4,3},{5,6},{6,5},{7,8},{8,7},{9,10},{10,... | collective-permute-start | bytes 540680 | tf_op jit(solution)/shard_map/ppermute | solution.py:513
  80.1 4.2 %collective-permute-start.18 = (f32[3,2,16,128]{3,2,1,0:T(8,128)S(1)}, f32[3,2,16,128]{3,2,1,0:T(8,128)S(1)}, u32[]{:S(2)}, u32[]{:S(2)}) collective-permute-start(f32[3,2,16,128]{3,2,1,0:T(8,128)S(1)} %get-tuple-element.38), channel_id=1, source_target_pairs={{0,16},{16,0},{32,48},{48,32},{64,80},{80,64},{96,112},{112,96},{1... | collective-permute-start | bytes 147464 | tf_op jit(solution)/shard_map/ppermute | solution.py:509

commit v4 on v3

--- a/solution.py
+++ b/solution.py
@@ -82,13 +82,13 @@
 
 
 def load_pack(
-    pos, disp_h, trac_h, heat_h, main_h, cross_h, clear_h, touch_h,
-    kinv, obst, me, mo, be, bo,
-    disp, trac, heat, main, cross, clear, touch, sem,
+    pos, disp_h, trac_h, heat_h, main_h, cross_h, clear_h, touch_h, clip_h,
+    kinv, obst, me, mo, be, bo, k0,
+    disp, trac, heat, main, cross, clear, touch, clip, rest, gath, sem,
 ):
     pairs = [
         (main_h, main), (cross_h, cross), (clear_h, clear), (touch_h, touch),
-        (disp_h, disp), (trac_h, trac), (heat_h, heat),
+        (disp_h, disp), (trac_h, trac), (heat_h, heat), (clip_h, clip),
     ]
     copies = [pltpu.make_async_copy(x, y, sem.at[i]) for i, (x, y) in enumerate(pairs)]
     for c in copies:
@@ -105,6 +105,12 @@
         return carry
 
     lax.fori_loop(0, 4, invert, 0)
+    for k in range(6):
+        src, c = (main, k) if k < 3 else (cross, k - 3)
+        for q in range(2):
+            x = 0.125 * (src[c, 2 * q] + src[c, 2 * q + 1])
+            gath[(2 * k + q) * 8 : (2 * k + q) * 8 + 8, :] = pair_rows(rest.at[2 * k + q], x, jnp.add)
+    k0[...] = pair_lanes(gath[...]).reshape(12, 8, 128)
     copies[2].wait()
     copies[3].wait()
     obst[...] = jnp.where(touch[...] == 1, clear[...], FREE)
@@ -119,6 +125,9 @@
         for k in range(6):
             msg[18 + 2 * k : 20 + 2 * k] = kinv[k, pl.ds(2 * at, 2)]
         msg[30:32] = obst[pl.ds(2 * at, 2)]
+    for t in range(12):
+        r, h = 8 * (t % 4 // 2), 128 * (t % 2)
+        me[32 + t // 4, r : r + 8, h : h + 128] = k0[t]
     wide, near = fields(disp, heat, trac, kinv, obst)
     for f in range(4):
         for p in range(4):
@@ -126,6 +135,8 @@
     for f in range(10):
         for p in range(4):
             put_rows(be, bo, up, 16 + f * 2 + p // 2, 2 * (p % 2), near[f](p), 2)
+    for p in range(4):
+        put_rows(be, bo, up, 36 + p, 0, clip[p].astype(F32), 3)
 
 
 def halo_plane(re, ro, even, inside, low, k):
@@ -133,7 +144,11 @@
     return jnp.where(even, o, e) if low else jnp.where(even, e, o)
 
 
-def pack_corner(pos, re, ro, be, bo):
+def pack_corner(pos, re, ro, k0, be, bo, k01):
+    k01[0:12] = k0[...]
+    for t in range(12):
+        r, h = 8 * (t % 4 // 2), 128 * (t % 2)
+        k01[12 + t] = re[32 + t // 4, r : r + 8, h : h + 128]
     even, inside = sides(pos[0])
     up = jnp.bitwise_and(pos[1], 1) == 0
     for f in range(4):
@@ -181,6 +196,30 @@
         near = v2[c, p, 0:16, :] + v2[c, p + 2, 0:16, :] + beside(v2[c, p + 1])[0:16]
         out.append(force[c, p + 2, 0:16, :] - (kv[c] - near))
     return out
+
+
+def pair_rows(room, x, op):
+    for h in range(2):
+        room[h] = x[:, 128 * h : 128 * h + 128]
+    return jnp.concatenate(
+        [op(room[h, pl.ds(0, 8, 2), :], room[h, pl.ds(1, 8, 2), :]) for h in range(2)], 1
+    )
+
+
+def pair_lanes(x):
+    i, j = rows((256, 128)), lanes((256, 128))
+    pick = jnp.where(lax.shift_right_logical(i, 1) == j, 1.0, 0.0)
+    return jnp.dot(x, pick, precision=HIGH, preferred_element_type=F32)
+
+
+def put_extra(planes, n, x):
+    planes[10 + n // 16, n % 16 : n % 16 + x.shape[0], :] = x
+
+
+def get_extra(ge, go, even, inside, low, n, m):
+    e = ge[10 + n // 16, n % 16 : n % 16 + m, :]
+    o = jnp.where(inside, go[10 + n // 16, n % 16 : n % 16 + m, :], 0.0)
+    return jnp.where(even, o, e) if low else jnp.where(even, e, o)
 
 
 def presmooth(
@@ -248,59 +287,34 @@
             out[0] = jnp.where(cut, 0.0, out[0])
             gap = jnp.logical_and(touch[p] == 1, clip[p] != 1)
             room = jnp.where(gap, clear[p] - v2[0, p + 1, 0:16, :], FREE)
-            part = out + [room] + [main[c, p] for c in range(3)] + [cross[c, p] for c in range(3)]
+            part = out + [room]
             if low is None:
                 low = part
             else:
                 low = [jnp.minimum(x, y) if i == 3 else x + y for i, (x, y) in enumerate(zip(low, part))]
-        for i in range(10):
-            x = low[i]
-            if i < 3:
-                x = 0.25 * x
-            elif i > 3:
-                x = 0.125 * x
-            for h in range(2):
-                rest[i, h] = x[:, 128 * h : 128 * h + 128]
-            halves = []
-            for h in range(2):
-                a, b = rest[i, h, pl.ds(0, 8, 2), :], rest[i, h, pl.ds(1, 8, 2), :]
-                halves.append(jnp.minimum(a, b) if i == 3 else a + b)
-            x = jnp.concatenate(halves, 1)
+        for i in range(4):
+            x = pair_rows(rest.at[i], low[i] if i == 3 else 0.25 * low[i], jnp.minimum if i == 3 else jnp.add)
             if i == 3:
                 x = jnp.minimum(x, pltpu.roll(x, 255, axis=1))
                 x = jnp.where(first[0:8], x, 0.0)
             gath[(2 * i + q) * 8 : (2 * i + q) * 8 + 8, :] = x
-    i, j = rows((256, 128)), lanes((256, 128))
-    pick = jnp.where(lax.shift_right_logical(i, 1) == j, 1.0, 0.0)
-    small = jnp.dot(gath[...], pick, precision=HIGH, preferred_element_type=F32)
-    small_out[...] = small.reshape(20, 8, 128)
+    small_out[...] = pair_lanes(gath[...]).reshape(8, 8, 128)
     for c in range(3):
         for k in range(2):
             planes_out[2 * c + k] = v2[c, k + 2, 0:16, :]
+            for side in range(2):
+                put_extra(planes_out, (c * 2 + k) * 2 + side, v2[c, k + 2, 16 if side else 23 : 17 if side else 24, :])
     for p in range(4):
         planes_out[6 + p] = clip[p].astype(F32)
+        low, high = get_rows(be, bo, up, inner, 36 + p, 0, 3)
+        put_extra(planes_out, 12 + 4 * p, low[1:3])
+        put_extra(planes_out, 14 + 4 * p, high[0:2])
     for c in range(3):
         for p in range(4):
             put_rows(pe, po, up, c * 2 + p // 2, 2 * (p % 2), v2[c, p + 1, 0:16, :], 2, 1)
         for side in range(2):
             n = 2 * c + side
-            put_rows(pe, po, up, 10 + n // 2, 2 * (n % 2), v2[c, 5 * side, 0:16, :], 2)
-    for p in range(4):
-        put_rows(pe, po, up, 6 + p, 0, clip[p].astype(F32), 3)
-
-
-def pack_late(pos, ge, go, be, bo):
-    even, inside = sides(pos[0])
-    up = jnp.bitwise_and(pos[1], 1) == 0
-    for side in range(2):
-        low = side == 0
-        for c in range(3):
-            x = halo_plane(ge, go, even, inside, low, 2 * c + (1 if low else 0))
-            put_rows(be, bo, up, side, c, x, 1)
-        x = halo_plane(ge, go, even, inside, low, 6 + (3 if low else 0))
-        put_rows(be, bo, up, 2 + side, 0, x, 2)
-        x = halo_plane(ge, go, even, inside, low, 6 + (2 if low else 1))
-        put_rows(be, bo, up, 2 + side, 2, x, 1)
+            put_rows(pe, po, up, 6 + n // 2, 2 * (n % 2), v2[c, 5 * side, 0:16, :], 2)
 
 
 def pair_spread(x, op):
@@ -312,33 +326,47 @@
 
 
 def coarse(
-    pos, b0, b1, b2, b3, b4, r1e, r1o, r2e, r2o, r3e, r3o,
+    pos, b0, eb, ob, b3, b4, k01, k23, r1e, r1o, rme, rmo, r2e, r2o,
     mid2, own, g, ki, va, vb, f3, k3, o3, l3,
 ):
     par = jnp.bitwise_and(pos[0], 1)
     up, inner = sides(pos[1])
     grp = pos[0]
+    one, mid, two = (r1e, r1o), (rme, rmo), (r2e, r2o)
     slots = [
-        (b0, 0, r1e, r1o, 0), (b1, 0, r1e, r1o, 20), (b2, 0, r2e, r2o, 0), (b2, 20, r2e, r2o, 20),
-        (b3, 0, r2e, r2o, 40), (b3, 20, r2e, r2o, 60), (b4, 0, r3e, r3o, 0), (b4, 20, r3e, r3o, 20),
+        (b0, 0, one, 0, k01, 0, one, 8), (eb, 0, mid, 0, k01, 12, one, 20),
+        (ob, 0, mid, 32, k23, 0, one, 32), (ob, 8, mid, 40, k23, 12, one, 44),
+        (b3, 0, two, 0, eb, 8, mid, 8), (b3, 8, two, 8, eb, 20, mid, 20),
+        (b4, 0, two, 16, ob, 16, mid, 48), (b4, 8, two, 24, ob, 28, mid, 60),
     ]
-    for s, (mine, m, re, ro, r) in enumerate(slots):
+    for s, (mine, m, (re, ro), r, mat, k, (ke, ko), kr) in enumerate(slots):
         place = jnp.where(par == 0, EVEN_SLOTS[s], 7 - EVEN_SLOTS[s])
         where = grp + place - jnp.where(par == 0, 4, 3)
         real = jnp.logical_and(where >= 0, where < 16)
+        real_o = jnp.logical_and(real, inner)
+
+        def lay(f, q, x, e, o):
+            a = jnp.where(real, e, 0.0)
+            b = jnp.where(real_o, o, 0.0)
+            to = g.at[f, 2 * place + q]
+            to[0:8, :] = jnp.where(real, x, 0.0)
+            to[8:16, :] = jnp.where(up, a, b)
+            to[16:24, :] = jnp.where(up, b, a)
 
         def fill(f, carry):
             for q in range(2):
-                t = f * 2 + q
-                a = jnp.where(real, re[r + t], 0.0)
-                b = jnp.where(jnp.logical_and(real, inner), ro[r + t], 0.0)
-                to = g.at[f, 2 * place + q]
-                to[0:8, :] = jnp.where(real, mine[m + t], 0.0)
-                to[8:16, :] = jnp.where(up, a, b)
-                to[16:24, :] = jnp.where(up, b, a)
+                t = 2 * f + q
+                lay(f, q, mine[m + t], re[r + t], ro[r + t])
             return carry
 
-        lax.fori_loop(0, 10, fill, 0, unroll=2)
+        def fill_k(f, carry):
+            for q in range(2):
+                t = 2 * f + q
+                lay(4 + f, q, mat[k + t], ke[kr + t], ko[kr + t])
+            return carry
+
+        lax.fori_loop(0, 4, fill, 0, unroll=2)
+        lax.fori_loop(0, 6, fill_k, 0, unroll=2)
 
     def start(p, carry):
         inv = inverse(*[g[4 + k, p] for k in range(6)])
@@ -425,7 +453,7 @@
 
 
 def finish(
-    pos, pre, ge, go, r1e, r1o, r3e, r3o, mid2, other, force_x, kinv_x, obst_x, clip, main, cross,
+    pos, pre, ge, go, r1e, r1o, be, bo, mid2, other, force_x, kinv_x, obst_x, clip, main, cross,
     moved, residual, v0, v1, v2, clip_x, mid_x, fine,
 ):
     par = jnp.bitwise_and(pos[0], 1)
@@ -436,30 +464,36 @@
             v0[c, p + 2] = pre[c, p]
         for p in range(4):
             to = v0.at[c, p + 3]
-            to[21:23, :], to[17:19, :] = get_rows(r1e, r1o, up, inner, 40 + c * 2 + p // 2, 2 * (p % 2), 2)
+            to[21:23, :], to[17:19, :] = get_rows(r1e, r1o, up, inner, 56 + c * 2 + p // 2, 2 * (p % 2), 2)
         for side in range(2):
             low = side == 0
             n = 2 * c + side
             to = v0.at[c, 2 if low else 7]
-            to[22:24, :], to[16:18, :] = get_rows(r1e, r1o, up, inner, 50 + n // 2, 2 * (n % 2), 2)
+            to[22:24, :], to[16:18, :] = get_rows(r1e, r1o, up, inner, 56 + 6 + n // 2, 2 * (n % 2), 2)
             for k in range(2):
                 to = v0.at[c, k if low else 8 + k]
                 to[0:16, :] = halo_plane(ge, go, even, inside, low, 2 * c + k)
+            k = 1 if low else 0
             to = v0.at[c, 1 if low else 8]
-            to[23:24, :], to[16:17, :] = get_rows(r3e, r3o, up, inner, 40 + side, c, 1)
+            to[23:24, :] = get_extra(ge, go, even, inside, low, (c * 2 + k) * 2, 1)
+            to[16:17, :] = get_extra(ge, go, even, inside, low, (c * 2 + k) * 2 + 1, 1)
     for p in range(4):
         to = clip_x.at[p + 3]
         to[0:16, :] = clip[p].astype(F32)
-        to[21:24, :], to[16:19, :] = get_rows(r1e, r1o, up, inner, 46 + p, 0, 3)
+        to[21:24, :], to[16:19, :] = get_rows(be, bo, up, inner, 36 + p, 0, 3)
     for side in range(2):
         low = side == 0
         for k in range(3):
             to = clip_x.at[k if low else 7 + k]
             to[0:16, :] = halo_plane(ge, go, even, inside, low, 6 + k + (1 if low else 0))
         to = clip_x.at[2 if low else 7]
-        to[22:24, :], to[16:18, :] = get_rows(r3e, r3o, up, inner, 42 + side, 0, 2)
+        n = 12 + 4 * (3 if low else 0)
+        to[22:24, :] = get_extra(ge, go, even, inside, low, n, 2)
+        to[16:18, :] = get_extra(ge, go, even, inside, low, n + 2, 2)
+        n = 12 + 4 * (2 if low else 1)
         to = clip_x.at[1 if low else 8]
-        to[23:24, :], to[16:17, :] = get_rows(r3e, r3o, up, inner, 42 + side, 2, 1)
+        to[23:24, :] = get_extra(ge, go, even, inside, low, n + 1, 1)
+        to[16:17, :] = get_extra(ge, go, even, inside, low, n + 2, 1)
     i, j = rows((128, 256)), lanes((128, 256))
     copy = jnp.where(lax.shift_right_logical(j, 1) == i, 1.0, 0.0)
     for c in range(3):
@@ -516,43 +550,46 @@
 def local(disp, trac, heat, main, cross, clear, touch, clip):
     pos = jnp.stack([lax.axis_index("grp"), lax.axis_index("brick")]).astype(jnp.int32)
     own, vec, six = (4, 16, 256), (3, 4, 16, 256), (6, 4, 16, 256)
-    kinv, obst, me, mo, be, bo = call(
+    kinv, obst, me, mo, be, bo, k0 = call(
         load_pack,
-        [six, own] + [(32, 16, 256)] * 2 + [(36, 8, 128)] * 2,
-        [vec, vec, own, vec, vec, own, pltpu.VMEM(own, jnp.int32), pltpu.SemaphoreType.DMA((7,))],
-        pos, *[pltpu.with_memory_space_constraint(z, pltpu.HBM) for z in (disp, trac, heat, main, cross, clear, touch)], limit=32 * 1024 * 1024,
+        [six, own, (35, 16, 256), (32, 16, 256), (40, 8, 128), (40, 8, 128), (12, 8, 128)],
+        [vec, vec, own, vec, vec, own, pltpu.VMEM(own, jnp.int32), pltpu.VMEM(own, jnp.int32),
+         (12, 2, 16, 128), (96, 256), pltpu.SemaphoreType.DMA((8,))],
+        pos, *[pltpu.with_memory_space_constraint(z, pltpu.HBM) for z in (disp, trac, heat, main, cross, clear, touch, clip)], limit=32 * 1024 * 1024,
     )
     re, ro = swap_even(me, "grp"), swap_odd(mo, "grp")
     re_b, ro_b = swap_even(be, "brick"), swap_odd(bo, "brick")
-    ce, co = call(pack_corner, [(13, 8, 128)] * 2, [], pos, re, ro)
+    ce, co, k01 = call(pack_corner, [(13, 8, 128)] * 2 + [(24, 8, 128)], [], pos, re, ro, k0)
     re_c, ro_c = swap_even(ce, "brick"), swap_odd(co, "brick")
+    k23 = swap_odd(k01, "grp")
     force_x, kinv_x, obst_x, pre, b0, planes, pe, po = call(
         presmooth,
-        [(3, 8, 24, 256), (6, 8, 24, 256), (8, 24, 256), (3, 6, 24, 256), (20, 8, 128),
-         (10, 16, 256), (13, 8, 128), (13, 8, 128)],
-        [(3, 10, 24, 256), (10, 24, 256), (3, 8, 24, 256), (10, 2, 16, 128), (160, 256)],
+        [(3, 8, 24, 256), (6, 8, 24, 256), (8, 24, 256), (3, 6, 24, 256), (8, 8, 128),
+         (12, 16, 256), (9, 8, 128), (9, 8, 128)],
+        [(3, 10, 24, 256), (10, 24, 256), (3, 8, 24, 256), (4, 2, 16, 128), (64, 256)],
         pos, disp, heat, clip, trac, kinv, obst, main, cross, clear, touch,
         re, ro, re_b, ro_b, re_c, ro_c,
     )
-    b1 = swap_even(b0, "grp")
-    b2 = swap_odd(jnp.concatenate([b0, b1], 0), "grp")
+    eb = swap_even(jnp.concatenate([b0, k23], 0), "grp")
+    ob = swap_odd(jnp.concatenate([b0, eb], 0), "grp")
     ge, go = swap_even(planes, "grp"), swap_odd(planes, "grp")
-    r1e = swap_even(jnp.concatenate([b0, b1, pe], 0), "brick")
-    r1o = swap_odd(jnp.concatenate([b0, b1, po], 0), "brick")
-    b3 = swap_even(b2, "grp")
-    second = jnp.concatenate([b2, b3], 0)
-    r2e, r2o = swap_even(second, "brick"), swap_odd(second, "brick")
+    after, go = lax.optimization_barrier((b0, go))
+    r1e = swap_even(jnp.concatenate([after, k01, k23, pe], 0), "brick")
+    r1o = swap_odd(jnp.concatenate([after, k01, k23, po], 0), "brick")
+    after, ge = lax.optimization_barrier((eb, ge))
+    middle = jnp.concatenate([after, ob], 0)
+    rme, rmo = swap_even(middle, "brick"), swap_odd(middle, "brick")
+    b3 = swap_even(ob[:16], "grp")
     b4 = swap_odd(b3, "grp")
-    qe, qo = call(pack_late, [(4, 8, 128)] * 2, [], pos, ge, go)
-    r3e = swap_even(jnp.concatenate([b4, qe], 0), "brick")
-    r3o = swap_odd(jnp.concatenate([b4, qo], 0), "brick")
+    last = jnp.concatenate([b3, b4], 0)
+    r2e, r2o = swap_even(last, "brick"), swap_odd(last, "brick")
     field, third = (3, 16, 24, 128), (3, 8, 24, 128)
     mid2, mine = call(
         coarse,
         [(3, 4, 16, 128), (3, 2, 16, 128)],
         [(10, 16, 24, 128), (6, 16, 24, 128), field, field, third, (6, 8, 24, 128),
          (8, 24, 128), third],
-        pos, b0, b1, b2, b3, b4, r1e, r1o, r2e, r2o, r3e, r3o,
+        pos, b0, eb, ob, b3, b4, k01, k23, r1e, r1o, rme, rmo, r2e, r2o,
     )
     other = swap_even(mine, "grp")
     return tuple(
@@ -561,7 +598,7 @@
             [vec, vec],
             [(3, 10, 24, 256), (3, 8, 24, 256), (3, 6, 24, 256), (10, 24, 256), (3, 6, 16, 128),
              (2, 32, 128)],
-            pos, pre, ge, go, r1e, r1o, r3e, r3o, mid2, other, force_x, kinv_x, obst_x, clip,
+            pos, pre, ge, go, r1e, r1o, re_b, ro_b, mid2, other, force_x, kinv_x, obst_x, clip,
             main, cross,
         )
     )

time: 88.8 us -> 84.3 us (0.949); the launches traced: 87.3 us -> 84.2 us
  starting transfers between devices: 35.2 us -> 26.2 us
  waiting for transfers between devices: 37.7 us -> 44.1 us
    ppermute x9 -> x10, starting transfers between devices: 32.4 us -> 23.9 us  [swap_odd(): return lax.ppermute(x, axis, ODD)]
    ppermute x9 -> x10, waiting for transfers between devices: 27.8 us -> 32.1 us  [swap_odd(): return lax.ppermute(x, axis, ODD)]
    ppermute x10, waiting for transfers between devices: 9.88 us -> 11.9 us  [swap_even(): return lax.ppermute(x, axis, EVEN)]
    pallas_call x6 -> x5, Pallas kernels: 13.3 us -> 12.8 us  [call(): pl.pallas_call(kernel, out_shape=[jax.ShapeDtypeStruct(x, F32) for x in o...]
  transfers between devices with their start and end apart: 19 -> 20, of which waited for: 10 -> 10; matrix products, arithmetic and copies ran while one was open for 0% -> 0% of each run, Pallas kernels for 1% -> 4%
where the time goes in v4:
time: 84.3 us; the launch traced here: 84.2 us
  waiting for transfers between devices  44.1 us (52%)
  starting transfers between devices  26.2 us (31%)
  Pallas kernels  12.8 us (15%)
  between operations  0.88 us (1%)
    ppermute x10, waiting for transfers between devices, swap_odd(): return lax.ppermute(x, axis, ODD)  32.1 us
    ppermute x10, starting transfers between devices, swap_odd(): return lax.ppermute(x, axis, ODD)  23.9 us
    pallas_call x5, Pallas kernels, call(): pl.pallas_call(kernel, out_shape=[jax.ShapeDtypeStruct(x, F32) for x in o...  12.8 us
    ppermute x10, waiting for transfers between devices, swap_even(): return lax.ppermute(x, axis, EVEN)  11.9 us
    ppermute x10, starting transfers between devices, swap_even(): return lax.ppermute(x, axis, EVEN)  2.29 us
  transfers between devices with their start and end apart: 20, of which 10 were waited for; matrix products, arithmetic and copies ran while one was open for 0% of the time, Pallas kernels for 4%

profile of v4, /device:TPU:0, one launch (start us, length us, event | category | flops | bytes accessed | tf_op | source)
XLA Modules:
  0.0 84.2 jit_solution(2359179601214567034)
XLA Ops:
  0.6 0.0 copy-start.2
  0.6 0.0 copy-start.5
  0.7 0.0 copy-start.4
  0.7 0.0 copy-start.3
  0.7 0.0 copy-start
  0.7 0.0 copy-start.1
  0.7 0.0 copy-start.6
  0.7 0.0 copy-start.7
  0.7 0.1 pad_add_fusion.pos
  0.8 2.2 %shard_map.95 = (f32[6,4,16,256]{3,2,1,0:T(8,128)S(1)}, f32[4,16,256]{2,1,0:T(8,128)S(1)}, f32[35,16,256]{2,1,0:T(8,128)S(1)}, f32[32,16,256]{2,1,0:T(8,128)S(1)...) custom-call(s32[2]{0:T(128)S(1)} %pad_add_fusion.pos, f32[3,4,16,256]{3,2,1,0:T(8,128)} %disp.1, ...), custom_call_target="tpu_custom_call" | custom-call | tf_op jit(solution)/shard_map/pallas_call | solution.py:528
  3.0 0.3 collective-permute-start
  3.2 7.4 %collective-permute-start.1 = (f32[32,16,256]{2,1,0:T(8,128)S(1)}, f32[32,16,256]{2,1,0:T(8,128)S(1)}, u32[]{:S(2)}, u32[]{:S(2)}) collective-permute-start(f32[32,16,256]{2,1,0:T(8,128)S(1)} %get-tuple-element.29), channel_id=1, source_target_pairs={{0,240},{16,32},{32,16},{48,64},{64,48},{80,96},{96,80},{112,128},... | collective-permute-start | bytes 1572872 | tf_op jit(solution)/shard_map/ppermute | solution.py:547
  10.7 3.2 %collective-permute-start.3 = (f32[40,8,128]{2,1,0:T(8,128)S(1)}, f32[40,8,128]{2,1,0:T(8,128)S(1)}, u32[]{:S(2)}, u32[]{:S(2)}) collective-permute-start(f32[40,8,128]{2,1,0:T(8,128)S(1)} %get-tuple-element.31), channel_id=1, source_target_pairs={{0,15},{1,2},{2,1},{3,4},{4,3},{5,6},{6,5},{7,8},{8,7},{9,10},{10,... | collective-permute-start | bytes 491528 | tf_op jit(solution)/shard_map/ppermute | solution.py:547
  13.8 8.6 %collective-permute-done.1.ro = f32[32,16,256]{2,1,0:T(8,128)S(1)} collective-permute-done((f32[32,16,256]{2,1,0:T(8,128)S(1)}, f32[32,16,256]{2,1,0:T(8,128)S(1)}, u32[]{:S(2)}, u32[]{:S(2)}) %collective-permute-start.1) | collective-permute-done | bytes 524320 | tf_op jit(solution)/shard_map/ppermute | solution.py:547
  22.4 0.6 shard_map.96
  23.0 5.4 %collective-permute-start.6 = (f32[24,8,128]{2,1,0:T(8,128)S(1)}, f32[24,8,128]{2,1,0:T(8,128)S(1)}, u32[]{:S(2)}, u32[]{:S(2)}) collective-permute-start(f32[24,8,128]{2,1,0:T(8,128)S(1)} %get-tuple-element.37.k01), channel_id=1, source_target_pairs={{0,240},{16,32},{32,16},{48,64},{64,48},{80,96},{96,80},{112,128},... | collective-permute-start | bytes 294920 | tf_op jit(solution)/shard_map/ppermute | solution.py:547
  28.5 0.0 collective-permute-start.4
  28.5 3.2 %collective-permute-start.5 = (f32[13,8,128]{2,1,0:T(8,128)S(1)}, f32[13,8,128]{2,1,0:T(8,128)S(1)}, u32[]{:S(2)}, u32[]{:S(2)}) collective-permute-start(f32[13,8,128]{2,1,0:T(8,128)S(1)} %get-tuple-element.34), channel_id=1, source_target_pairs={{0,15},{1,2},{2,1},{3,4},{4,3},{5,6},{6,5},{7,8},{8,7},{9,10},{10,... | collective-permute-start | bytes 159752 | tf_op jit(solution)/shard_map/ppermute | solution.py:547
  31.6 0.0 collective-permute-done.2.be
  31.6 0.0 collective-permute-done.3.bo
  31.6 2.5 %collective-permute-done.5.co = f32[13,8,128]{2,1,0:T(8,128)S(1)} collective-permute-done((f32[13,8,128]{2,1,0:T(8,128)S(1)}, f32[13,8,128]{2,1,0:T(8,128)S(1)}, u32[]{:S(2)}, u32[]{:S(2)}) %collective-permute-start.5) | collective-permute-done | bytes 53280 | tf_op jit(solution)/shard_map/ppermute | solution.py:547
  34.2 3.1 %shard_map.97 = (f32[3,8,24,256]{3,2,1,0:T(8,128)S(1)}, f32[6,8,24,256]{3,2,1,0:T(8,128)S(1)}, f32[8,24,256]{2,1,0:T(8,128)S(1)}, f32[3,6,24,256]{3,2,1,0:T(8,12...) custom-call(s32[2]{0:T(128)S(1)} %pad_add_fusion.pos, ...), custom_call_target="tpu_custom_call" | custom-call | tf_op jit(solution)/shard_map/pallas_call | solution.py:528
  37.3 0.1 collective-permute-start.7
  37.4 0.4 collective-permute-start.9
  37.8 1.6 %collective-permute-start.8 = (f32[12,16,256]{2,1,0:T(8,128)S(1)}, f32[12,16,256]{2,1,0:T(8,128)S(1)}, u32[]{:S(2)}, u32[]{:S(2)}) collective-permute-start(f32[12,16,256]{2,1,0:T(8,128)S(1)} %get-tuple-element.38), channel_id=1, source_target_pairs={{0,16},{16,0},{32,48},{48,32},{64,80},{80,64},{96,112},{112,96},{1... | collective-permute-start | bytes 589832 | tf_op jit(solution)/shard_map/ppermute | solution.py:543
  39.5 4.3 %collective-permute-done.7.eb = f32[32,8,128]{2,1,0:T(8,128)S(1)} collective-permute-done((f32[32,8,128]{2,1,0:T(8,128)S(1)}, f32[32,8,128]{2,1,0:T(8,128)S(1)}, u32[]{:S(2)}, u32[]{:S(2)}) %collective-permute-start.7) | collective-permute-done | bytes 131104 | tf_op jit(solution)/shard_map/ppermute | solution.py:543
  43.8 0.1 collective-permute-start.12
  43.9 3.5 %collective-permute-done.9.go = f32[12,16,256]{2,1,0:T(8,128)S(1)} collective-permute-done((f32[12,16,256]{2,1,0:T(8,128)S(1)}, f32[12,16,256]{2,1,0:T(8,128)S(1)}, u32[]{:S(2)}, u32[]{:S(2)}) %collective-permute-start.9) | collective-permute-done | bytes 196640 | tf_op jit(solution)/shard_map/ppermute | solution.py:547
  47.4 0.0 collective-permute-done.8.ge
  47.4 0.1 collective-permute-start.10
  47.5 2.0 %collective-permute-start.11 = (f32[65,8,128]{2,1,0:T(8,128)S(1)}, f32[65,8,128]{2,1,0:T(8,128)S(1)}, u32[]{:S(2)}, u32[]{:S(2)}) collective-permute-start(f32[65,8,128]{2,1,0:T(8,128)S(1)} %get-tuple-element.50), channel_id=1, source_target_pairs={{0,15},{1,2},{2,1},{3,4},{4,3},{5,6},{6,5},{7,8},{8,7},{9,10},{10,... | collective-permute-start | bytes 798728 | tf_op jit(solution)/shard_map/ppermute | solution.py:547
  49.5 3.3 %collective-permute-done.12.ob = f32[40,8,128]{2,1,0:T(8,128)S(1)} collective-permute-done((f32[40,8,128]{2,1,0:T(8,128)S(1)}, f32[40,8,128]{2,1,0:T(8,128)S(1)}, u32[]{:S(2)}, u32[]{:S(2)}) %collective-permute-start.12) | collective-permute-done | bytes 163872 | tf_op jit(solution)/shard_map/ppermute | solution.py:547
  52.9 0.1 collective-permute-start.15
  53.0 1.3 %collective-permute-start.16 = (f32[72,8,128]{2,1,0:T(8,128)S(1)}, f32[72,8,128]{2,1,0:T(8,128)S(1)}, u32[]{:S(2)}, u32[]{:S(2)}) collective-permute-start(f32[72,8,128]{2,1,0:T(8,128)S(1)} %constant_dynamic-update-slice_fusion), channel_id=1, source_target_pairs={{0,15},{1,2},{2,1},{3,4},{4,3},{5,6},{6,5},{7,8},{8,7},{9,10},{10,... | collective-permute-start | bytes 884744 | tf_op jit(solution)/shard_map/ppermute | solution.py:547
  54.3 2.8 %collective-permute-done.13.b3 = f32[16,8,128]{2,1,0:T(8,128)S(1)} collective-permute-done((f32[16,8,128]{2,1,0:T(8,128)S(1)}, f32[16,8,128]{2,1,0:T(8,128)S(1)}, u32[]{:S(2)}, u32[]{:S(2)}) %collective-permute-start.13) | collective-permute-done | bytes 65568 | tf_op jit(solution)/shard_map/ppermute | solution.py:543
  57.1 0.4 collective-permute-start.14
  57.6 7.6 %collective-permute-done.14.b4 = f32[16,8,128]{2,1,0:T(8,128)S(1)} collective-permute-done((f32[16,8,128]{2,1,0:T(8,128)S(1)}, f32[16,8,128]{2,1,0:T(8,128)S(1)}, u32[]{:S(2)}, u32[]{:S(2)}) %collective-permute-start.14) | collective-permute-done | bytes 65568 | tf_op jit(solution)/shard_map/ppermute | solution.py:547
  65.1 0.0 collective-permute-done.10.r1e
  65.2 0.6 collective-permute-start.18
  65.7 0.0 collective-permute-done.11.r1o
  65.8 0.7 collective-permute-done.17.r2e
  66.5 6.6 %collective-permute-done.18.r2o = f32[32,8,128]{2,1,0:T(8,128)S(1)} collective-permute-done((f32[32,8,128]{2,1,0:T(8,128)S(1)}, f32[32,8,128]{2,1,0:T(8,128)S(1)}, u32[]{:S(2)}, u32[]{:S(2)}) %collective-permute-start.18) | collective-permute-done | bytes 131104 | tf_op jit(solution)/shard_map/ppermute | solution.py:547
  73.1 0.0 collective-permute-done.15.rme
  73.1 0.0 collective-permute-done.16.rmo
  73.1 3.8 %shard_map.98 = (f32[3,4,16,128]{3,2,1,0:T(8,128)S(1)}, f32[3,2,16,128]{3,2,1,0:T(8,128)S(1)}) custom-call(s32[2]{0:T(128)S(1)} %pad_add_fusion.pos, f32[8,8,128]{2,1,0:T(8,128)S(1)} %get-tuple-element.41.b0, f32[32,8,128]{2,1,0:T(8,128)S(1)} %collective-permute-done.7.eb, f32[40,8,128]{2,1,0:T(8,128)S(1)} %collective-permute-done.12.ob, ...), custom_call_target="tpu_custom_call" | custom-call | tf_op jit(solution)/shard_map/pallas_call | solution.py:528
  77.0 0.1 collective-permute-start.19
  77.1 4.1 %collective-permute-done.19.other = f32[3,2,16,128]{3,2,1,0:T(8,128)S(1)} collective-permute-done((f32[3,2,16,128]{3,2,1,0:T(8,128)S(1)}, f32[3,2,16,128]{3,2,1,0:T(8,128)S(1)}, u32[]{:S(2)}, u32[]{:S(2)}) %collective-permute-start.19) | collective-permute-done | bytes 49184 | tf_op jit(solution)/shard_map/ppermute | solution.py:543
  81.1 3.0 %shard_map.99 = (f32[3,4,16,256]{3,2,1,0:T(8,128)}, f32[3,4,16,256]{3,2,1,0:T(8,128)}) custom-call(s32[2]{0:T(128)S(1)} %pad_add_fusion.pos, f32[3,6,24,256]{3,2,1,0:T(8,128)S(1)} %get-tuple-element.35.pre, f32[12,16,256]{2,1,0:T(8,128)S(1)} %collective-permute-done.8.ge, f32[12,16,256]{2,1,0:T(8,128)S(1)} %collective-permute-done.9.go, ...), custom_call_target="tpu_custom_call" | custom-call | tf_op jit(solution)/shard_map/pallas_call | solution.py:528
  (22 shorter events, 0.1 us)
Async XLA Ops:
  0.6 33.5 %copy-start.2 = (f32[3,4,16,256]{3,2,1,0:T(8,128)S(1)}, f32[3,4,16,256]{3,2,1,0:T(8,128)}, u32[]{:S(2)}) copy-start(f32[3,4,16,256]{3,2,1,0:T(8,128)} %disp.1) | copy-start | bytes 589828
  0.6 33.5 %copy-start.5 = (f32[4,16,256]{2,1,0:T(8,128)S(1)}, f32[4,16,256]{2,1,0:T(8,128)}, u32[]{:S(2)}) copy-start(f32[4,16,256]{2,1,0:T(8,128)} %heat.1) | copy-start | bytes 196612
  0.7 33.5 %copy-start.4 = (s32[4,16,256]{2,1,0:T(8,128)S(1)}, s32[4,16,256]{2,1,0:T(8,128)}, u32[]{:S(2)}) copy-start(s32[4,16,256]{2,1,0:T(8,128)} %clip.3) | copy-start | bytes 196612
  0.7 33.5 %copy-start.3 = (f32[3,4,16,256]{3,2,1,0:T(8,128)S(1)}, f32[3,4,16,256]{3,2,1,0:T(8,128)}, u32[]{:S(2)}) copy-start(f32[3,4,16,256]{3,2,1,0:T(8,128)} %trac.1) | copy-start | bytes 589828
  0.7 33.5 %copy-start = (f32[3,4,16,256]{3,2,1,0:T(8,128)S(1)}, f32[3,4,16,256]{3,2,1,0:T(8,128)}, u32[]{:S(2)}) copy-start(f32[3,4,16,256]{3,2,1,0:T(8,128)} %main.3) | copy-start | bytes 589828
  0.7 33.5 %copy-start.1 = (f32[3,4,16,256]{3,2,1,0:T(8,128)S(1)}, f32[3,4,16,256]{3,2,1,0:T(8,128)}, u32[]{:S(2)}) copy-start(f32[3,4,16,256]{3,2,1,0:T(8,128)} %cross.3) | copy-start | bytes 589828
  0.7 33.5 %copy-start.6 = (f32[4,16,256]{2,1,0:T(8,128)S(1)}, f32[4,16,256]{2,1,0:T(8,128)}, u32[]{:S(2)}) copy-start(f32[4,16,256]{2,1,0:T(8,128)} %clear.1) | copy-start | bytes 196612
  0.7 33.5 %copy-start.7 = (s32[4,16,256]{2,1,0:T(8,128)S(1)}, s32[4,16,256]{2,1,0:T(8,128)}, u32[]{:S(2)}) copy-start(s32[4,16,256]{2,1,0:T(8,128)} %touch.1) | copy-start | bytes 196612
  3.0 19.4 %collective-permute-start = (f32[35,16,256]{2,1,0:T(8,128)S(1)}, f32[35,16,256]{2,1,0:T(8,128)S(1)}, u32[]{:S(2)}, u32[]{:S(2)}) collective-permute-start(f32[35,16,256]{2,1,0:T(8,128)S(1)} %get-tuple-element.28), channel_id=1, source_target_pairs={{0,16},{16,0},{32,48},{48,32},{64,80},{80,64},{96,112},{112,96},{1... | collective-permute-start | bytes 1720328 | tf_op jit(solution)/shard_map/ppermute | solution.py:543
  3.2 19.1 %collective-permute-start.1 = (f32[32,16,256]{2,1,0:T(8,128)S(1)}, f32[32,16,256]{2,1,0:T(8,128)S(1)}, u32[]{:S(2)}, u32[]{:S(2)}) collective-permute-start(f32[32,16,256]{2,1,0:T(8,128)S(1)} %get-tuple-element.29), channel_id=1, source_target_pairs={{0,240},{16,32},{32,16},{48,64},{64,48},{80,96},{96,80},{112,128},... | collective-permute-start | bytes 1572872 | tf_op jit(solution)/shard_map/ppermute | solution.py:547
  10.7 21.0 %collective-permute-start.2 = (f32[40,8,128]{2,1,0:T(8,128)S(1)}, f32[40,8,128]{2,1,0:T(8,128)S(1)}, u32[]{:S(2)}, u32[]{:S(2)}) collective-permute-start(f32[40,8,128]{2,1,0:T(8,128)S(1)} %get-tuple-element.30), channel_id=1, source_target_pairs={{0,1},{1,0},{2,3},{3,2},{4,5},{5,4},{6,7},{7,6},{8,9},{9,8},{10,11... | collective-permute-start | bytes 491528 | tf_op jit(solution)/shard_map/ppermute | solution.py:543
  10.7 21.0 %collective-permute-start.3 = (f32[40,8,128]{2,1,0:T(8,128)S(1)}, f32[40,8,128]{2,1,0:T(8,128)S(1)}, u32[]{:S(2)}, u32[]{:S(2)}) collective-permute-start(f32[40,8,128]{2,1,0:T(8,128)S(1)} %get-tuple-element.31), channel_id=1, source_target_pairs={{0,15},{1,2},{2,1},{3,4},{4,3},{5,6},{6,5},{7,8},{8,7},{9,10},{10,... | collective-permute-start | bytes 491528 | tf_op jit(solution)/shard_map/ppermute | solution.py:547
  23.0 14.3 %collective-permute-start.6 = (f32[24,8,128]{2,1,0:T(8,128)S(1)}, f32[24,8,128]{2,1,0:T(8,128)S(1)}, u32[]{:S(2)}, u32[]{:S(2)}) collective-permute-start(f32[24,8,128]{2,1,0:T(8,128)S(1)} %get-tuple-element.37.k01), channel_id=1, source_target_pairs={{0,240},{16,32},{32,16},{48,64},{64,48},{80,96},{96,80},{112,128},... | collective-permute-start | bytes 294920 | tf_op jit(solution)/shard_map/ppermute | solution.py:547
  28.5 3.2 %collective-permute-start.4 = (f32[13,8,128]{2,1,0:T(8,128)S(1)}, f32[13,8,128]{2,1,0:T(8,128)S(1)}, u32[]{:S(2)}, u32[]{:S(2)}) collective-permute-start(f32[13,8,128]{2,1,0:T(8,128)S(1)} %get-tuple-element.33), channel_id=1, source_target_pairs={{0,1},{1,0},{2,3},{3,2},{4,5},{5,4},{6,7},{7,6},{8,9},{9,8},{10,11... | collective-permute-start | bytes 159752 | tf_op jit(solution)/shard_map/ppermute | solution.py:543
  28.5 5.7 %collective-permute-start.5 = (f32[13,8,128]{2,1,0:T(8,128)S(1)}, f32[13,8,128]{2,1,0:T(8,128)S(1)}, u32[]{:S(2)}, u32[]{:S(2)}) collective-permute-start(f32[13,8,128]{2,1,0:T(8,128)S(1)} %get-tuple-element.34), channel_id=1, source_target_pairs={{0,15},{1,2},{2,1},{3,4},{4,3},{5,6},{6,5},{7,8},{8,7},{9,10},{10,... | collective-permute-start | bytes 159752 | tf_op jit(solution)/shard_map/ppermute | solution.py:547
  37.3 6.4 %collective-permute-start.7 = (f32[32,8,128]{2,1,0:T(8,128)S(1)}, f32[32,8,128]{2,1,0:T(8,128)S(1)}, u32[]{:S(2)}, u32[]{:S(2)}) collective-permute-start(f32[32,8,128]{2,1,0:T(8,128)S(1)} %pad_maximum_fusion.4), channel_id=1, source_target_pairs={{0,16},{16,0},{32,48},{48,32},{64,80},{80,64},{96,112},{112,96},{1... | collective-permute-start | bytes 393224 | tf_op jit(solution)/shard_map/ppermute | solution.py:543
  37.4 9.9 %collective-permute-start.9 = (f32[12,16,256]{2,1,0:T(8,128)S(1)}, f32[12,16,256]{2,1,0:T(8,128)S(1)}, u32[]{:S(2)}, u32[]{:S(2)}) collective-permute-start(f32[12,16,256]{2,1,0:T(8,128)S(1)} %get-tuple-element.38), channel_id=1, source_target_pairs={{0,240},{16,32},{32,16},{48,64},{64,48},{80,96},{96,80},{112,128},... | collective-permute-start | bytes 589832 | tf_op jit(solution)/shard_map/ppermute | solution.py:547
  37.8 9.6 %collective-permute-start.8 = (f32[12,16,256]{2,1,0:T(8,128)S(1)}, f32[12,16,256]{2,1,0:T(8,128)S(1)}, u32[]{:S(2)}, u32[]{:S(2)}) collective-permute-start(f32[12,16,256]{2,1,0:T(8,128)S(1)} %get-tuple-element.38), channel_id=1, source_target_pairs={{0,16},{16,0},{32,48},{48,32},{64,80},{80,64},{96,112},{112,96},{1... | collective-permute-start | bytes 589832 | tf_op jit(solution)/shard_map/ppermute | solution.py:543
  43.8 9.1 %collective-permute-start.12 = (f32[40,8,128]{2,1,0:T(8,128)S(1)}, f32[40,8,128]{2,1,0:T(8,128)S(1)}, u32[]{:S(2)}, u32[]{:S(2)}) collective-permute-start(f32[40,8,128]{2,1,0:T(8,128)S(1)} %pad_maximum_fusion.3), channel_id=1, source_target_pairs={{0,240},{16,32},{32,16},{48,64},{64,48},{80,96},{96,80},{112,128},... | collective-permute-start | bytes 491528 | tf_op jit(solution)/shard_map/ppermute | solution.py:547
  47.4 17.7 %collective-permute-start.10 = (f32[65,8,128]{2,1,0:T(8,128)S(1)}, f32[65,8,128]{2,1,0:T(8,128)S(1)}, u32[]{:S(2)}, u32[]{:S(2)}) collective-permute-start(f32[65,8,128]{2,1,0:T(8,128)S(1)} %get-tuple-element.51), channel_id=1, source_target_pairs={{0,1},{1,0},{2,3},{3,2},{4,5},{5,4},{6,7},{7,6},{8,9},{9,8},{10,11... | collective-permute-start | bytes 798728 | tf_op jit(solution)/shard_map/ppermute | solution.py:543
  47.5 18.2 %collective-permute-start.11 = (f32[65,8,128]{2,1,0:T(8,128)S(1)}, f32[65,8,128]{2,1,0:T(8,128)S(1)}, u32[]{:S(2)}, u32[]{:S(2)}) collective-permute-start(f32[65,8,128]{2,1,0:T(8,128)S(1)} %get-tuple-element.50), channel_id=1, source_target_pairs={{0,15},{1,2},{2,1},{3,4},{4,3},{5,6},{6,5},{7,8},{8,7},{9,10},{10,... | collective-permute-start | bytes 798728 | tf_op jit(solution)/shard_map/ppermute | solution.py:547
  52.9 4.3 %collective-permute-start.13 = (f32[16,8,128]{2,1,0:T(8,128)S(1)}, f32[16,8,128]{2,1,0:T(8,128)S(1)}, u32[]{:S(2)}, u32[]{:S(2)}) collective-permute-start(f32[16,8,128]{2,1,0:T(8,128)S(1)} %slice.4), channel_id=1, source_target_pairs={{0,16},{16,0},{32,48},{48,32},{64,80},{80,64},{96,112},{112,96},{1... | collective-permute-start | bytes 196616 | tf_op jit(solution)/shard_map/ppermute | solution.py:543
  52.9 20.2 %collective-permute-start.15 = (f32[72,8,128]{2,1,0:T(8,128)S(1)}, f32[72,8,128]{2,1,0:T(8,128)S(1)}, u32[]{:S(2)}, u32[]{:S(2)}) collective-permute-start(f32[72,8,128]{2,1,0:T(8,128)S(1)} %constant_dynamic-update-slice_fusion), channel_id=1, source_target_pairs={{0,1},{1,0},{2,3},{3,2},{4,5},{5,4},{6,7},{7,6},{8,9},{9,8},{10,11... | collective-permute-start | bytes 884744 | tf_op jit(solution)/shard_map/ppermute | solution.py:543
  53.0 20.1 %collective-permute-start.16 = (f32[72,8,128]{2,1,0:T(8,128)S(1)}, f32[72,8,128]{2,1,0:T(8,128)S(1)}, u32[]{:S(2)}, u32[]{:S(2)}) collective-permute-start(f32[72,8,128]{2,1,0:T(8,128)S(1)} %constant_dynamic-update-slice_fusion), channel_id=1, source_target_pairs={{0,15},{1,2},{2,1},{3,4},{4,3},{5,6},{6,5},{7,8},{8,7},{9,10},{10,... | collective-permute-start | bytes 884744 | tf_op jit(solution)/shard_map/ppermute | solution.py:547
  57.1 8.0 %collective-permute-start.14 = (f32[16,8,128]{2,1,0:T(8,128)S(1)}, f32[16,8,128]{2,1,0:T(8,128)S(1)}, u32[]{:S(2)}, u32[]{:S(2)}) collective-permute-start(f32[16,8,128]{2,1,0:T(8,128)S(1)} %collective-permute-done.13.b3), channel_id=1, source_target_pairs={{0,240},{16,32},{32,16},{48,64},{64,48},{80,96},{96,80},{112,128},... | collective-permute-start | bytes 196616 | tf_op jit(solution)/shard_map/ppermute | solution.py:547
  65.1 1.3 %collective-permute-start.17 = (f32[32,8,128]{2,1,0:T(8,128)S(1)}, f32[32,8,128]{2,1,0:T(8,128)S(1)}, u32[]{:S(2)}, u32[]{:S(2)}) collective-permute-start(f32[32,8,128]{2,1,0:T(8,128)S(1)} %constant_dynamic-update-slice_fusion.2), channel_id=1, source_target_pairs={{0,1},{1,0},{2,3},{3,2},{4,5},{5,4},{6,7},{7,6},{8,9},{9,8},{10,11... | collective-permute-start | bytes 393224 | tf_op jit(solution)/shard_map/ppermute | solution.py:543
  65.2 8.0 %collective-permute-start.18 = (f32[32,8,128]{2,1,0:T(8,128)S(1)}, f32[32,8,128]{2,1,0:T(8,128)S(1)}, u32[]{:S(2)}, u32[]{:S(2)}) collective-permute-start(f32[32,8,128]{2,1,0:T(8,128)S(1)} %constant_dynamic-update-slice_fusion.2), channel_id=1, source_target_pairs={{0,15},{1,2},{2,1},{3,4},{4,3},{5,6},{6,5},{7,8},{8,7},{9,10},{10,... | collective-permute-start | bytes 393224 | tf_op jit(solution)/shard_map/ppermute | solution.py:547
  77.0 4.2 %collective-permute-start.19 = (f32[3,2,16,128]{3,2,1,0:T(8,128)S(1)}, f32[3,2,16,128]{3,2,1,0:T(8,128)S(1)}, u32[]{:S(2)}, u32[]{:S(2)}) collective-permute-start(f32[3,2,16,128]{3,2,1,0:T(8,128)S(1)} %get-tuple-element.46), channel_id=1, source_target_pairs={{0,16},{16,0},{32,48},{48,32},{64,80},{80,64},{96,112},{112,96},{1... | collective-permute-start | bytes 147464 | tf_op jit(solution)/shard_map/ppermute | solution.py:543

commit v5 on v4

--- a/solution.py
+++ b/solution.py
@@ -325,54 +325,73 @@
     return op(x, jnp.where(even, pltpu.roll(x, n - 1, axis=0), pltpu.roll(x, 1, axis=0)))
 
 
-def coarse(
-    pos, b0, eb, ob, b3, b4, k01, k23, r1e, r1o, rme, rmo, r2e, r2o,
-    mid2, own, g, ki, va, vb, f3, k3, o3, l3,
-):
+SLOTS = (
+    ("b0", 0, "one", 0, "k01", 0, "one", 8), ("eb", 0, "mid", 0, "k01", 12, "one", 20),
+    ("ob", 0, "mid", 32, "k23", 0, "one", 32), ("ob", 8, "mid", 40, "k23", 12, "one", 44),
+    ("b3", 0, "two", 0, "eb", 8, "mid", 8), ("b3", 8, "two", 8, "eb", 20, "mid", 20),
+    ("b4", 0, "two", 16, "ob", 16, "mid", 48), ("b4", 8, "two", 24, "ob", 28, "mid", 60),
+)
+
+
+def lay_window(pos, refs, g, force):
     par = jnp.bitwise_and(pos[0], 1)
     up, inner = sides(pos[1])
     grp = pos[0]
-    one, mid, two = (r1e, r1o), (rme, rmo), (r2e, r2o)
-    slots = [
-        (b0, 0, one, 0, k01, 0, one, 8), (eb, 0, mid, 0, k01, 12, one, 20),
-        (ob, 0, mid, 32, k23, 0, one, 32), (ob, 8, mid, 40, k23, 12, one, 44),
-        (b3, 0, two, 0, eb, 8, mid, 8), (b3, 8, two, 8, eb, 20, mid, 20),
-        (b4, 0, two, 16, ob, 16, mid, 48), (b4, 8, two, 24, ob, 28, mid, 60),
-    ]
-    for s, (mine, m, (re, ro), r, mat, k, (ke, ko), kr) in enumerate(slots):
+    for s, (mine, m, row, r, mat, k, krow, kr) in enumerate(SLOTS):
+        if not force:
+            mine, m, row, r = mat, k, krow, kr
+        mine, (re, ro) = refs[mine], refs[row]
         place = jnp.where(par == 0, EVEN_SLOTS[s], 7 - EVEN_SLOTS[s])
         where = grp + place - jnp.where(par == 0, 4, 3)
         real = jnp.logical_and(where >= 0, where < 16)
         real_o = jnp.logical_and(real, inner)
 
-        def lay(f, q, x, e, o):
-            a = jnp.where(real, e, 0.0)
-            b = jnp.where(real_o, o, 0.0)
-            to = g.at[f, 2 * place + q]
-            to[0:8, :] = jnp.where(real, x, 0.0)
-            to[8:16, :] = jnp.where(up, a, b)
-            to[16:24, :] = jnp.where(up, b, a)
-
         def fill(f, carry):
             for q in range(2):
                 t = 2 * f + q
-                lay(f, q, mine[m + t], re[r + t], ro[r + t])
+                a = jnp.where(real, re[r + t], 0.0)
+                b = jnp.where(real_o, ro[r + t], 0.0)
+                to = g.at[f, 2 * place + q]
+                to[0:8, :] = jnp.where(real, mine[m + t], 0.0)
+                to[8:16, :] = jnp.where(up, a, b)
+                to[16:24, :] = jnp.where(up, b, a)
             return carry
 
-        def fill_k(f, carry):
-            for q in range(2):
-                t = 2 * f + q
-                lay(4 + f, q, mat[k + t], ke[kr + t], ko[kr + t])
-            return carry
-
-        lax.fori_loop(0, 4, fill, 0, unroll=2)
-        lax.fori_loop(0, 6, fill_k, 0, unroll=2)
-
-    def start(p, carry):
-        inv = inverse(*[g[4 + k, p] for k in range(6)])
+        lax.fori_loop(0, 4 if force else 6, fill, 0, unroll=2)
+
+
+def coarse_blocks(pos, eb, ob, k01, k23, r1e, r1o, rme, rmo, gk, ki, k3):
+    refs = dict(eb=eb, ob=ob, k01=k01, k23=k23, one=(r1e, r1o), mid=(rme, rmo))
+    lay_window(pos, refs, gk, False)
+
+    def invert(p, carry):
+        inv = inverse(*[gk[k, p] for k in range(6)])
         for k in range(6):
             ki[k, p] = inv[k]
-        v = symmetric_times(inv, [OMEGA * g[c, p] for c in range(3)])
+        return carry
+
+    lax.fori_loop(0, 16, invert, 0, unroll=4)
+
+    def third(q, carry):
+        mat = [0.125 * pair_spread(gk[k, 2 * q] + gk[k, 2 * q + 1], jnp.add) for k in range(6)]
+        inv = inverse(*mat)
+        for k in range(6):
+            k3[k, q] = inv[k]
+        return carry
+
+    lax.fori_loop(1, 7, third, 0, unroll=2)
+
+
+def coarse(
+    pos, b0, eb, ob, b3, b4, r1e, r1o, rme, rmo, r2e, r2o, gk, ki, k3,
+    mid2, own, g, va, vb, f3, o3, l3,
+):
+    par = jnp.bitwise_and(pos[0], 1)
+    refs = dict(b0=b0, eb=eb, ob=ob, b3=b3, b4=b4, one=(r1e, r1o), mid=(rme, rmo), two=(r2e, r2o))
+    lay_window(pos, refs, g, True)
+
+    def start(p, carry):
+        v = symmetric_times([ki[k, p] for k in range(6)], [OMEGA * g[c, p] for c in range(3)])
         va[0, p] = jnp.minimum(v[0], g[3, p])
         va[1, p] = v[1]
         va[2, p] = v[2]
@@ -400,28 +419,24 @@
     def third(q, carry):
         total = None
         for p in (2 * q, 2 * q + 1):
-            mat = [g[4 + k, p] for k in range(6)]
+            mat = [gk[k, p] for k in range(6)]
             kv = symmetric_times(mat, [vb[c, p] for c in range(3)])
             part = []
             for c in range(3):
                 near = vb[c, p - 1] + vb[c, p + 1] + beside(vb[c, p])
                 part.append(g[c, p] - (kv[c] - near))
-            part += mat + [g[3, p] - vb[0, p]]
+            part.append(g[3, p] - vb[0, p])
             if total is None:
                 total = part
             else:
-                total = [jnp.minimum(x, y) if i == 9 else x + y for i, (x, y) in enumerate(zip(total, part))]
+                total = [jnp.minimum(x, y) if i == 3 else x + y for i, (x, y) in enumerate(zip(total, part))]
         force = [0.25 * pair_spread(total[c], jnp.add) for c in range(3)]
-        mat = [0.125 * pair_spread(total[3 + k], jnp.add) for k in range(6)]
-        room = pair_spread(total[9], jnp.minimum)
-        inv = inverse(*mat)
-        v = symmetric_times(inv, [OMEGA * x for x in force])
+        room = pair_spread(total[3], jnp.minimum)
+        v = symmetric_times([k3[k, q] for k in range(6)], [OMEGA * x for x in force])
         v[0] = jnp.minimum(v[0], room)
         for c in range(3):
             f3[c, q] = force[c]
             l3[c, q] = v[c]
-        for k in range(6):
-            k3[k, q] = inv[k]
         o3[q] = room
         return carry
 
@@ -452,11 +467,7 @@
             own[c, k, 10:12, :] = va[c, 8 - 2 * par + k, 22:24, :]
 
 
-def finish(
-    pos, pre, ge, go, r1e, r1o, be, bo, mid2, other, force_x, kinv_x, obst_x, clip, main, cross,
-    moved, residual, v0, v1, v2, clip_x, mid_x, fine,
-):
-    par = jnp.bitwise_and(pos[0], 1)
+def gather_pre(pos, pre, ge, go, r1e, r1o, be, bo, clip, v0, clip_x):
     even, inside = sides(pos[0])
     up, inner = sides(pos[1])
     for c in range(3):
@@ -494,6 +505,13 @@
         to = clip_x.at[1 if low else 8]
         to[23:24, :] = get_extra(ge, go, even, inside, low, n + 1, 1)
         to[16:17, :] = get_extra(ge, go, even, inside, low, n + 2, 1)
+
+
+def finish(
+    pos, held, mid2, other, force_x, kinv_x, obst_x, clip_x, main, cross,
+    moved, residual, v0, v1, v2, mid_x, fine,
+):
+    par = jnp.bitwise_and(pos[0], 1)
     i, j = rows((128, 256)), lanes((128, 256))
     copy = jnp.where(lax.shift_right_logical(j, 1) == i, 1.0, 0.0)
     for c in range(3):
@@ -513,7 +531,7 @@
             for p in range(10):
                 if (p + 1) // 2 == k:
                     add = jnp.where(clip_x[p] == 1.0, 0.0, up2) if c == 0 else up2
-                    v0[c, p] = v0[c, p] + add
+                    v0[c, p] = held[c, p] + add
     smooth(v0, force_x, kinv_x, obst_x, v1, v2)
     for p in range(4):
         out = residual_plane(v2, force_x, main, cross, p)
@@ -584,22 +602,29 @@
     last = jnp.concatenate([b3, b4], 0)
     r2e, r2o = swap_even(last, "brick"), swap_odd(last, "brick")
     field, third = (3, 16, 24, 128), (3, 8, 24, 128)
+    gk, ki, k3 = call(
+        coarse_blocks,
+        [(6, 16, 24, 128), (6, 16, 24, 128), (6, 8, 24, 128)],
+        [],
+        pos, eb, ob, k01, k23, r1e, r1o, rme, rmo,
+    )
     mid2, mine = call(
         coarse,
         [(3, 4, 16, 128), (3, 2, 16, 128)],
-        [(10, 16, 24, 128), (6, 16, 24, 128), field, field, third, (6, 8, 24, 128),
-         (8, 24, 128), third],
-        pos, b0, eb, ob, b3, b4, k01, k23, r1e, r1o, rme, rmo, r2e, r2o,
+        [(4, 16, 24, 128), field, field, third, (8, 24, 128), third],
+        pos, b0, eb, ob, b3, b4, r1e, r1o, rme, rmo, r2e, r2o, gk, ki, k3,
     )
     other = swap_even(mine, "grp")
+    held, clip_x = call(
+        gather_pre, [(3, 10, 24, 256), (10, 24, 256)], [],
+        pos, pre, ge, go, r1e, r1o, re_b, ro_b, clip,
+    )
     return tuple(
         call(
             finish,
             [vec, vec],
-            [(3, 10, 24, 256), (3, 8, 24, 256), (3, 6, 24, 256), (10, 24, 256), (3, 6, 16, 128),
-             (2, 32, 128)],
-            pos, pre, ge, go, r1e, r1o, re_b, ro_b, mid2, other, force_x, kinv_x, obst_x, clip,
-            main, cross,
+            [(3, 10, 24, 256), (3, 8, 24, 256), (3, 6, 24, 256), (3, 6, 16, 128), (2, 32, 128)],
+            pos, held, mid2, other, force_x, kinv_x, obst_x, clip_x, main, cross,
         )
     )
 

time: 84.3 us -> 82.2 us (0.975)
  waiting for transfers between devices: 44.1 us -> 41.3 us
  Pallas kernels: 12.8 us -> 14.4 us
  starting transfers between devices: 26.2 us -> 25.3 us
    pallas_call x5 -> x7, Pallas kernels: 12.8 us -> 14.4 us  [call(): pl.pallas_call(kernel, out_shape=[jax.ShapeDtypeStruct(x, F32) for x in o...]
    ppermute x10, waiting for transfers between devices: 32.1 us -> 30.6 us  [swap_odd(): return lax.ppermute(x, axis, ODD)]
    ppermute x10, waiting for transfers between devices: 11.9 us -> 10.7 us  [swap_even(): return lax.ppermute(x, axis, EVEN)]
    ppermute x10, starting transfers between devices: 23.9 us -> 22.9 us  [swap_odd(): return lax.ppermute(x, axis, ODD)]
  transfers between devices with their start and end apart: 20 -> 20, of which waited for: 10 -> 10; matrix products, arithmetic and copies ran while one was open for 0% -> 0% of each run, Pallas kernels for 4% -> 7%
where the time goes in v5:
time: 82.2 us; the launch traced here: 82.1 us
  waiting for transfers between devices  41.3 us (50%)
  starting transfers between devices  25.3 us (31%)
  Pallas kernels  14.4 us (18%)
  between operations  0.9 us (1%)
    ppermute x10, waiting for transfers between devices, swap_odd(): return lax.ppermute(x, axis, ODD)  30.6 us
    ppermute x10, starting transfers between devices, swap_odd(): return lax.ppermute(x, axis, ODD)  22.9 us
    pallas_call x7, Pallas kernels, call(): pl.pallas_call(kernel, out_shape=[jax.ShapeDtypeStruct(x, F32) for x in o...  14.4 us
    ppermute x10, waiting for transfers between devices, swap_even(): return lax.ppermute(x, axis, EVEN)  10.7 us
    ppermute x10, starting transfers between devices, swap_even(): return lax.ppermute(x, axis, EVEN)  2.38 us
  transfers between devices with their start and end apart: 20, of which 10 were waited for; matrix products, arithmetic and copies ran while one was open for 0% of the time, Pallas kernels for 7%

profile of v5, /device:TPU:0, one launch (start us, length us, event | category | flops | bytes accessed | tf_op | source)
XLA Modules:
  0.0 82.1 jit_solution(11690604203427905626)
XLA Ops:
  0.6 0.0 copy-start.4
  0.6 0.0 copy-start.1
  0.7 0.0 copy-start
  0.7 0.0 copy-start.7
  0.7 0.0 copy-start.6
  0.7 0.0 copy-start.5
  0.7 0.0 copy-start.3
  0.7 0.0 copy-start.2
  0.7 0.1 pad_add_fusion.pos
  0.8 2.2 %shard_map.95 = (f32[6,4,16,256]{3,2,1,0:T(8,128)S(1)}, f32[4,16,256]{2,1,0:T(8,128)S(1)}, f32[35,16,256]{2,1,0:T(8,128)S(1)}, f32[32,16,256]{2,1,0:T(8,128)S(1)...) custom-call(s32[2]{0:T(128)S(1)} %pad_add_fusion.pos, f32[3,4,16,256]{3,2,1,0:T(8,128)} %disp.1, ...), custom_call_target="tpu_custom_call" | custom-call | tf_op jit(solution)/shard_map/pallas_call | solution.py:546
  3.0 0.3 collective-permute-start
  3.2 7.4 %collective-permute-start.1 = (f32[32,16,256]{2,1,0:T(8,128)S(1)}, f32[32,16,256]{2,1,0:T(8,128)S(1)}, u32[]{:S(2)}, u32[]{:S(2)}) collective-permute-start(f32[32,16,256]{2,1,0:T(8,128)S(1)} %get-tuple-element.34), channel_id=1, source_target_pairs={{0,240},{16,32},{32,16},{48,64},{64,48},{80,96},{96,80},{112,128},... | collective-permute-start | bytes 1572872 | tf_op jit(solution)/shard_map/ppermute | solution.py:565
  10.7 0.0 collective-permute-start.2
  10.7 3.2 %collective-permute-start.3 = (f32[40,8,128]{2,1,0:T(8,128)S(1)}, f32[40,8,128]{2,1,0:T(8,128)S(1)}, u32[]{:S(2)}, u32[]{:S(2)}) collective-permute-start(f32[40,8,128]{2,1,0:T(8,128)S(1)} %get-tuple-element.36), channel_id=1, source_target_pairs={{0,15},{1,2},{2,1},{3,4},{4,3},{5,6},{6,5},{7,8},{8,7},{9,10},{10,... | collective-permute-start | bytes 491528 | tf_op jit(solution)/shard_map/ppermute | solution.py:565
  13.8 8.6 %collective-permute-done.1.ro = f32[32,16,256]{2,1,0:T(8,128)S(1)} collective-permute-done((f32[32,16,256]{2,1,0:T(8,128)S(1)}, f32[32,16,256]{2,1,0:T(8,128)S(1)}, u32[]{:S(2)}, u32[]{:S(2)}) %collective-permute-start.1) | collective-permute-done | bytes 524320 | tf_op jit(solution)/shard_map/ppermute | solution.py:565
  22.4 0.0 collective-permute-done.re
  22.4 0.6 shard_map.96
  23.0 5.4 %collective-permute-start.6 = (f32[24,8,128]{2,1,0:T(8,128)S(1)}, f32[24,8,128]{2,1,0:T(8,128)S(1)}, u32[]{:S(2)}, u32[]{:S(2)}) collective-permute-start(f32[24,8,128]{2,1,0:T(8,128)S(1)} %get-tuple-element.42.k01), channel_id=1, source_target_pairs={{0,240},{16,32},{32,16},{48,64},{64,48},{80,96},{96,80},{112,128},... | collective-permute-start | bytes 294920 | tf_op jit(solution)/shard_map/ppermute | solution.py:565
  28.5 3.2 %collective-permute-start.5 = (f32[13,8,128]{2,1,0:T(8,128)S(1)}, f32[13,8,128]{2,1,0:T(8,128)S(1)}, u32[]{:S(2)}, u32[]{:S(2)}) collective-permute-start(f32[13,8,128]{2,1,0:T(8,128)S(1)} %get-tuple-element.39), channel_id=1, source_target_pairs={{0,15},{1,2},{2,1},{3,4},{4,3},{5,6},{6,5},{7,8},{8,7},{9,10},{10,... | collective-permute-start | bytes 159752 | tf_op jit(solution)/shard_map/ppermute | solution.py:565
  31.6 0.0 collective-permute-done.2.be
  31.6 0.0 collective-permute-done.3.bo
  31.6 0.0 collective-permute-done.4.ce
  31.6 2.5 %collective-permute-done.5.co = f32[13,8,128]{2,1,0:T(8,128)S(1)} collective-permute-done((f32[13,8,128]{2,1,0:T(8,128)S(1)}, f32[13,8,128]{2,1,0:T(8,128)S(1)}, u32[]{:S(2)}, u32[]{:S(2)}) %collective-permute-start.5) | collective-permute-done | bytes 53280 | tf_op jit(solution)/shard_map/ppermute | solution.py:565
  34.2 3.1 %shard_map.97 = (f32[3,8,24,256]{3,2,1,0:T(8,128)S(1)}, f32[6,8,24,256]{3,2,1,0:T(8,128)S(1)}, f32[8,24,256]{2,1,0:T(8,128)S(1)}, f32[3,6,24,256]{3,2,1,0:T(8,12...) custom-call(s32[2]{0:T(128)S(1)} %pad_add_fusion.pos, ...), custom_call_target="tpu_custom_call" | custom-call | tf_op jit(solution)/shard_map/pallas_call | solution.py:546
  37.3 0.0 collective-permute-done.6.k23
  37.3 0.1 collective-permute-start.7
  37.4 0.4 collective-permute-start.9
  37.8 1.6 %collective-permute-start.8 = (f32[12,16,256]{2,1,0:T(8,128)S(1)}, f32[12,16,256]{2,1,0:T(8,128)S(1)}, u32[]{:S(2)}, u32[]{:S(2)}) collective-permute-start(f32[12,16,256]{2,1,0:T(8,128)S(1)} %get-tuple-element.43), channel_id=1, source_target_pairs={{0,16},{16,0},{32,48},{48,32},{64,80},{80,64},{96,112},{112,96},{1... | collective-permute-start | bytes 589832 | tf_op jit(solution)/shard_map/ppermute | solution.py:561
  39.5 4.3 %collective-permute-done.7.eb = f32[32,8,128]{2,1,0:T(8,128)S(1)} collective-permute-done((f32[32,8,128]{2,1,0:T(8,128)S(1)}, f32[32,8,128]{2,1,0:T(8,128)S(1)}, u32[]{:S(2)}, u32[]{:S(2)}) %collective-permute-start.7) | collective-permute-done | bytes 131104 | tf_op jit(solution)/shard_map/ppermute | solution.py:561
  43.8 0.1 collective-permute-start.12
  43.9 3.5 %collective-permute-done.9.go = f32[12,16,256]{2,1,0:T(8,128)S(1)} collective-permute-done((f32[12,16,256]{2,1,0:T(8,128)S(1)}, f32[12,16,256]{2,1,0:T(8,128)S(1)}, u32[]{:S(2)}, u32[]{:S(2)}) %collective-permute-start.9) | collective-permute-done | bytes 196640 | tf_op jit(solution)/shard_map/ppermute | solution.py:565
  47.4 2.0 %collective-permute-start.11 = (f32[65,8,128]{2,1,0:T(8,128)S(1)}, f32[65,8,128]{2,1,0:T(8,128)S(1)}, u32[]{:S(2)}, u32[]{:S(2)}) collective-permute-start(f32[65,8,128]{2,1,0:T(8,128)S(1)} %get-tuple-element.60), channel_id=1, source_target_pairs={{0,15},{1,2},{2,1},{3,4},{4,3},{5,6},{6,5},{7,8},{8,7},{9,10},{10,... | collective-permute-start | bytes 798728 | tf_op jit(solution)/shard_map/ppermute | solution.py:565
  49.4 3.5 %collective-permute-done.12.ob = f32[40,8,128]{2,1,0:T(8,128)S(1)} collective-permute-done((f32[40,8,128]{2,1,0:T(8,128)S(1)}, f32[40,8,128]{2,1,0:T(8,128)S(1)}, u32[]{:S(2)}, u32[]{:S(2)}) %collective-permute-start.12) | collective-permute-done | bytes 163872 | tf_op jit(solution)/shard_map/ppermute | solution.py:565
  52.9 0.0 collective-permute-start.13
  52.9 1.2 %collective-permute-start.16 = (f32[72,8,128]{2,1,0:T(8,128)S(1)}, f32[72,8,128]{2,1,0:T(8,128)S(1)}, u32[]{:S(2)}, u32[]{:S(2)}) collective-permute-start(f32[72,8,128]{2,1,0:T(8,128)S(1)} %constant_dynamic-update-slice_fusion), channel_id=1, source_target_pairs={{0,15},{1,2},{2,1},{3,4},{4,3},{5,6},{6,5},{7,8},{8,7},{9,10},{10,... | collective-permute-start | bytes 884744 | tf_op jit(solution)/shard_map/ppermute | solution.py:565
  54.2 3.0 %collective-permute-done.13.b3 = f32[16,8,128]{2,1,0:T(8,128)S(1)} collective-permute-done((f32[16,8,128]{2,1,0:T(8,128)S(1)}, f32[16,8,128]{2,1,0:T(8,128)S(1)}, u32[]{:S(2)}, u32[]{:S(2)}) %collective-permute-start.13) | collective-permute-done | bytes 65568 | tf_op jit(solution)/shard_map/ppermute | solution.py:561
  57.2 0.0 collective-permute-start.14
  57.2 8.0 %collective-permute-done.14.b4 = f32[16,8,128]{2,1,0:T(8,128)S(1)} collective-permute-done((f32[16,8,128]{2,1,0:T(8,128)S(1)}, f32[16,8,128]{2,1,0:T(8,128)S(1)}, u32[]{:S(2)}, u32[]{:S(2)}) %collective-permute-start.14) | collective-permute-done | bytes 65568 | tf_op jit(solution)/shard_map/ppermute | solution.py:565
  65.2 0.0 collective-permute-done.11.r1o
  65.2 0.3 collective-permute-start.17
  65.5 0.4 collective-permute-done.16.rmo
  65.9 1.6 %shard_map.99 = (f32[6,16,24,128]{3,2,1,0:T(8,128)S(1)}, f32[6,16,24,128]{3,2,1,0:T(8,128)S(1)}, f32[6,8,24,128]{3,2,1,0:T(8,128)S(1)}) custom-call(s32[2]{0:T(128)S(1)} %pad_add_fusion.pos, f32[32,8,128]{2,1,0:T(8,128)S(1)} %collective-permute-done.7.eb, f32[40,8,128]{2,1,0:T(8,128)S(1)} %collective-permute-done.12.ob, ...), custom_call_target="tpu_custom_call" | custom-call | tf_op jit(solution)/shard_map/pallas_call | solution.py:546
  67.5 4.2 %collective-permute-done.18.r2o = f32[32,8,128]{2,1,0:T(8,128)S(1)} collective-permute-done((f32[32,8,128]{2,1,0:T(8,128)S(1)}, f32[32,8,128]{2,1,0:T(8,128)S(1)}, u32[]{:S(2)}, u32[]{:S(2)}) %collective-permute-start.18) | collective-permute-done | bytes 131104 | tf_op jit(solution)/shard_map/ppermute | solution.py:565
  71.7 3.2 %shard_map.100 = (f32[3,4,16,128]{3,2,1,0:T(8,128)S(1)}, f32[3,2,16,128]{3,2,1,0:T(8,128)S(1)}) custom-call(s32[2]{0:T(128)S(1)} %pad_add_fusion.pos, f32[8,8,128]{2,1,0:T(8,128)S(1)} %get-tuple-element.46.b0, f32[32,8,128]{2,1,0:T(8,128)S(1)} %collective-permute-done.7.eb, f32[40,8,128]{2,1,0:T(8,128)S(1)} %collective-permute-done.12.ob, ...), custom_call_target="tpu_custom_call" | custom-call | tf_op jit(solution)/shard_map/pallas_call | solution.py:546
  74.9 0.1 collective-permute-start.19
  75.0 0.7 shard_map.98
  75.7 3.4 %collective-permute-done.19.other = f32[3,2,16,128]{3,2,1,0:T(8,128)S(1)} collective-permute-done((f32[3,2,16,128]{3,2,1,0:T(8,128)S(1)}, f32[3,2,16,128]{3,2,1,0:T(8,128)S(1)}, u32[]{:S(2)}, u32[]{:S(2)}) %collective-permute-start.19) | collective-permute-done | bytes 49184 | tf_op jit(solution)/shard_map/ppermute | solution.py:561
  79.1 3.0 %shard_map.101 = (f32[3,4,16,256]{3,2,1,0:T(8,128)}, f32[3,4,16,256]{3,2,1,0:T(8,128)}) custom-call(s32[2]{0:T(128)S(1)} %pad_add_fusion.pos, f32[3,10,24,256]{3,2,1,0:T(8,128)S(1)} %get-tuple-element.49.held, f32[3,4,16,128]{3,2,1,0:T(8,128)S(1)} %get-tuple-element.54.mid2, f32[3,2,16,128]{3,2,1,0:T(8,128)S(1)} %collective-permute-done.19.other, ...), custom_call_target="tpu_custom_call" | custom-call | tf_op jit(solution)/shard_map/pallas_call | solution.py:546
  (24 shorter events, 0.1 us)
Async XLA Ops:
  0.6 33.5 %copy-start.4 = (s32[4,16,256]{2,1,0:T(8,128)S(1)}, s32[4,16,256]{2,1,0:T(8,128)}, u32[]{:S(2)}) copy-start(s32[4,16,256]{2,1,0:T(8,128)} %clip.3) | copy-start | bytes 196612
  0.6 33.5 %copy-start.1 = (f32[3,4,16,256]{3,2,1,0:T(8,128)S(1)}, f32[3,4,16,256]{3,2,1,0:T(8,128)}, u32[]{:S(2)}) copy-start(f32[3,4,16,256]{3,2,1,0:T(8,128)} %cross.3) | copy-start | bytes 589828
  0.7 33.5 %copy-start = (f32[3,4,16,256]{3,2,1,0:T(8,128)S(1)}, f32[3,4,16,256]{3,2,1,0:T(8,128)}, u32[]{:S(2)}) copy-start(f32[3,4,16,256]{3,2,1,0:T(8,128)} %main.3) | copy-start | bytes 589828
  0.7 33.5 %copy-start.7 = (s32[4,16,256]{2,1,0:T(8,128)S(1)}, s32[4,16,256]{2,1,0:T(8,128)}, u32[]{:S(2)}) copy-start(s32[4,16,256]{2,1,0:T(8,128)} %touch.1) | copy-start | bytes 196612
  0.7 33.5 %copy-start.6 = (f32[4,16,256]{2,1,0:T(8,128)S(1)}, f32[4,16,256]{2,1,0:T(8,128)}, u32[]{:S(2)}) copy-start(f32[4,16,256]{2,1,0:T(8,128)} %clear.1) | copy-start | bytes 196612
  0.7 33.5 %copy-start.5 = (f32[4,16,256]{2,1,0:T(8,128)S(1)}, f32[4,16,256]{2,1,0:T(8,128)}, u32[]{:S(2)}) copy-start(f32[4,16,256]{2,1,0:T(8,128)} %heat.1) | copy-start | bytes 196612
  0.7 33.5 %copy-start.3 = (f32[3,4,16,256]{3,2,1,0:T(8,128)S(1)}, f32[3,4,16,256]{3,2,1,0:T(8,128)}, u32[]{:S(2)}) copy-start(f32[3,4,16,256]{3,2,1,0:T(8,128)} %trac.1) | copy-start | bytes 589828
  0.7 33.5 %copy-start.2 = (f32[3,4,16,256]{3,2,1,0:T(8,128)S(1)}, f32[3,4,16,256]{3,2,1,0:T(8,128)}, u32[]{:S(2)}) copy-start(f32[3,4,16,256]{3,2,1,0:T(8,128)} %disp.1) | copy-start | bytes 589828
  3.0 19.4 %collective-permute-start = (f32[35,16,256]{2,1,0:T(8,128)S(1)}, f32[35,16,256]{2,1,0:T(8,128)S(1)}, u32[]{:S(2)}, u32[]{:S(2)}) collective-permute-start(f32[35,16,256]{2,1,0:T(8,128)S(1)} %get-tuple-element.33), channel_id=1, source_target_pairs={{0,16},{16,0},{32,48},{48,32},{64,80},{80,64},{96,112},{112,96},{1... | collective-permute-start | bytes 1720328 | tf_op jit(solution)/shard_map/ppermute | solution.py:561
  3.2 19.1 %collective-permute-start.1 = (f32[32,16,256]{2,1,0:T(8,128)S(1)}, f32[32,16,256]{2,1,0:T(8,128)S(1)}, u32[]{:S(2)}, u32[]{:S(2)}) collective-permute-start(f32[32,16,256]{2,1,0:T(8,128)S(1)} %get-tuple-element.34), channel_id=1, source_target_pairs={{0,240},{16,32},{32,16},{48,64},{64,48},{80,96},{96,80},{112,128},... | collective-permute-start | bytes 1572872 | tf_op jit(solution)/shard_map/ppermute | solution.py:565
  10.7 21.0 %collective-permute-start.2 = (f32[40,8,128]{2,1,0:T(8,128)S(1)}, f32[40,8,128]{2,1,0:T(8,128)S(1)}, u32[]{:S(2)}, u32[]{:S(2)}) collective-permute-start(f32[40,8,128]{2,1,0:T(8,128)S(1)} %get-tuple-element.35), channel_id=1, source_target_pairs={{0,1},{1,0},{2,3},{3,2},{4,5},{5,4},{6,7},{7,6},{8,9},{9,8},{10,11... | collective-permute-start | bytes 491528 | tf_op jit(solution)/shard_map/ppermute | solution.py:561
  10.7 21.0 %collective-permute-start.3 = (f32[40,8,128]{2,1,0:T(8,128)S(1)}, f32[40,8,128]{2,1,0:T(8,128)S(1)}, u32[]{:S(2)}, u32[]{:S(2)}) collective-permute-start(f32[40,8,128]{2,1,0:T(8,128)S(1)} %get-tuple-element.36), channel_id=1, source_target_pairs={{0,15},{1,2},{2,1},{3,4},{4,3},{5,6},{6,5},{7,8},{8,7},{9,10},{10,... | collective-permute-start | bytes 491528 | tf_op jit(solution)/shard_map/ppermute | solution.py:565
  23.0 14.3 %collective-permute-start.6 = (f32[24,8,128]{2,1,0:T(8,128)S(1)}, f32[24,8,128]{2,1,0:T(8,128)S(1)}, u32[]{:S(2)}, u32[]{:S(2)}) collective-permute-start(f32[24,8,128]{2,1,0:T(8,128)S(1)} %get-tuple-element.42.k01), channel_id=1, source_target_pairs={{0,240},{16,32},{32,16},{48,64},{64,48},{80,96},{96,80},{112,128},... | collective-permute-start | bytes 294920 | tf_op jit(solution)/shard_map/ppermute | solution.py:565
  28.5 3.2 %collective-permute-start.4 = (f32[13,8,128]{2,1,0:T(8,128)S(1)}, f32[13,8,128]{2,1,0:T(8,128)S(1)}, u32[]{:S(2)}, u32[]{:S(2)}) collective-permute-start(f32[13,8,128]{2,1,0:T(8,128)S(1)} %get-tuple-element.38), channel_id=1, source_target_pairs={{0,1},{1,0},{2,3},{3,2},{4,5},{5,4},{6,7},{7,6},{8,9},{9,8},{10,11... | collective-permute-start | bytes 159752 | tf_op jit(solution)/shard_map/ppermute | solution.py:561
  28.5 5.7 %collective-permute-start.5 = (f32[13,8,128]{2,1,0:T(8,128)S(1)}, f32[13,8,128]{2,1,0:T(8,128)S(1)}, u32[]{:S(2)}, u32[]{:S(2)}) collective-permute-start(f32[13,8,128]{2,1,0:T(8,128)S(1)} %get-tuple-element.39), channel_id=1, source_target_pairs={{0,15},{1,2},{2,1},{3,4},{4,3},{5,6},{6,5},{7,8},{8,7},{9,10},{10,... | collective-permute-start | bytes 159752 | tf_op jit(solution)/shard_map/ppermute | solution.py:565
  37.3 6.4 %collective-permute-start.7 = (f32[32,8,128]{2,1,0:T(8,128)S(1)}, f32[32,8,128]{2,1,0:T(8,128)S(1)}, u32[]{:S(2)}, u32[]{:S(2)}) collective-permute-start(f32[32,8,128]{2,1,0:T(8,128)S(1)} %pad_maximum_fusion.4), channel_id=1, source_target_pairs={{0,16},{16,0},{32,48},{48,32},{64,80},{80,64},{96,112},{112,96},{1... | collective-permute-start | bytes 393224 | tf_op jit(solution)/shard_map/ppermute | solution.py:561
  37.4 9.9 %collective-permute-start.9 = (f32[12,16,256]{2,1,0:T(8,128)S(1)}, f32[12,16,256]{2,1,0:T(8,128)S(1)}, u32[]{:S(2)}, u32[]{:S(2)}) collective-permute-start(f32[12,16,256]{2,1,0:T(8,128)S(1)} %get-tuple-element.43), channel_id=1, source_target_pairs={{0,240},{16,32},{32,16},{48,64},{64,48},{80,96},{96,80},{112,128},... | collective-permute-start | bytes 589832 | tf_op jit(solution)/shard_map/ppermute | solution.py:565
  37.8 9.6 %collective-permute-start.8 = (f32[12,16,256]{2,1,0:T(8,128)S(1)}, f32[12,16,256]{2,1,0:T(8,128)S(1)}, u32[]{:S(2)}, u32[]{:S(2)}) collective-permute-start(f32[12,16,256]{2,1,0:T(8,128)S(1)} %get-tuple-element.43), channel_id=1, source_target_pairs={{0,16},{16,0},{32,48},{48,32},{64,80},{80,64},{96,112},{112,96},{1... | collective-permute-start | bytes 589832 | tf_op jit(solution)/shard_map/ppermute | solution.py:561
  43.8 9.1 %collective-permute-start.12 = (f32[40,8,128]{2,1,0:T(8,128)S(1)}, f32[40,8,128]{2,1,0:T(8,128)S(1)}, u32[]{:S(2)}, u32[]{:S(2)}) collective-permute-start(f32[40,8,128]{2,1,0:T(8,128)S(1)} %pad_maximum_fusion.3), channel_id=1, source_target_pairs={{0,240},{16,32},{32,16},{48,64},{64,48},{80,96},{96,80},{112,128},... | collective-permute-start | bytes 491528 | tf_op jit(solution)/shard_map/ppermute | solution.py:565
  47.4 17.7 %collective-permute-start.11 = (f32[65,8,128]{2,1,0:T(8,128)S(1)}, f32[65,8,128]{2,1,0:T(8,128)S(1)}, u32[]{:S(2)}, u32[]{:S(2)}) collective-permute-start(f32[65,8,128]{2,1,0:T(8,128)S(1)} %get-tuple-element.60), channel_id=1, source_target_pairs={{0,15},{1,2},{2,1},{3,4},{4,3},{5,6},{6,5},{7,8},{8,7},{9,10},{10,... | collective-permute-start | bytes 798728 | tf_op jit(solution)/shard_map/ppermute | solution.py:565
  49.4 16.0 %collective-permute-start.10 = (f32[65,8,128]{2,1,0:T(8,128)S(1)}, f32[65,8,128]{2,1,0:T(8,128)S(1)}, u32[]{:S(2)}, u32[]{:S(2)}) collective-permute-start(f32[65,8,128]{2,1,0:T(8,128)S(1)} %get-tuple-element.61), channel_id=1, source_target_pairs={{0,1},{1,0},{2,3},{3,2},{4,5},{5,4},{6,7},{7,6},{8,9},{9,8},{10,11... | collective-permute-start | bytes 798728 | tf_op jit(solution)/shard_map/ppermute | solution.py:561
  52.9 4.3 %collective-permute-start.13 = (f32[16,8,128]{2,1,0:T(8,128)S(1)}, f32[16,8,128]{2,1,0:T(8,128)S(1)}, u32[]{:S(2)}, u32[]{:S(2)}) collective-permute-start(f32[16,8,128]{2,1,0:T(8,128)S(1)} %slice.4), channel_id=1, source_target_pairs={{0,16},{16,0},{32,48},{48,32},{64,80},{80,64},{96,112},{112,96},{1... | collective-permute-start | bytes 196616 | tf_op jit(solution)/shard_map/ppermute | solution.py:561
  52.9 13.0 %collective-permute-start.16 = (f32[72,8,128]{2,1,0:T(8,128)S(1)}, f32[72,8,128]{2,1,0:T(8,128)S(1)}, u32[]{:S(2)}, u32[]{:S(2)}) collective-permute-start(f32[72,8,128]{2,1,0:T(8,128)S(1)} %constant_dynamic-update-slice_fusion), channel_id=1, source_target_pairs={{0,15},{1,2},{2,1},{3,4},{4,3},{5,6},{6,5},{7,8},{8,7},{9,10},{10,... | collective-permute-start | bytes 884744 | tf_op jit(solution)/shard_map/ppermute | solution.py:565
  54.2 11.7 %collective-permute-start.15 = (f32[72,8,128]{2,1,0:T(8,128)S(1)}, f32[72,8,128]{2,1,0:T(8,128)S(1)}, u32[]{:S(2)}, u32[]{:S(2)}) collective-permute-start(f32[72,8,128]{2,1,0:T(8,128)S(1)} %constant_dynamic-update-slice_fusion), channel_id=1, source_target_pairs={{0,1},{1,0},{2,3},{3,2},{4,5},{5,4},{6,7},{7,6},{8,9},{9,8},{10,11... | collective-permute-start | bytes 884744 | tf_op jit(solution)/shard_map/ppermute | solution.py:561
  57.2 8.0 %collective-permute-start.14 = (f32[16,8,128]{2,1,0:T(8,128)S(1)}, f32[16,8,128]{2,1,0:T(8,128)S(1)}, u32[]{:S(2)}, u32[]{:S(2)}) collective-permute-start(f32[16,8,128]{2,1,0:T(8,128)S(1)} %collective-permute-done.13.b3), channel_id=1, source_target_pairs={{0,240},{16,32},{32,16},{48,64},{64,48},{80,96},{96,80},{112,128},... | collective-permute-start | bytes 196616 | tf_op jit(solution)/shard_map/ppermute | solution.py:565
  65.2 6.5 %collective-permute-start.18 = (f32[32,8,128]{2,1,0:T(8,128)S(1)}, f32[32,8,128]{2,1,0:T(8,128)S(1)}, u32[]{:S(2)}, u32[]{:S(2)}) collective-permute-start(f32[32,8,128]{2,1,0:T(8,128)S(1)} %constant_dynamic-update-slice_fusion.2), channel_id=1, source_target_pairs={{0,15},{1,2},{2,1},{3,4},{4,3},{5,6},{6,5},{7,8},{8,7},{9,10},{10,... | collective-permute-start | bytes 393224 | tf_op jit(solution)/shard_map/ppermute | solution.py:565
  65.2 6.5 %collective-permute-start.17 = (f32[32,8,128]{2,1,0:T(8,128)S(1)}, f32[32,8,128]{2,1,0:T(8,128)S(1)}, u32[]{:S(2)}, u32[]{:S(2)}) collective-permute-start(f32[32,8,128]{2,1,0:T(8,128)S(1)} %constant_dynamic-update-slice_fusion.2), channel_id=1, source_target_pairs={{0,1},{1,0},{2,3},{3,2},{4,5},{5,4},{6,7},{7,6},{8,9},{9,8},{10,11... | collective-permute-start | bytes 393224 | tf_op jit(solution)/shard_map/ppermute | solution.py:561
  74.9 4.2 %collective-permute-start.19 = (f32[3,2,16,128]{3,2,1,0:T(8,128)S(1)}, f32[3,2,16,128]{3,2,1,0:T(8,128)S(1)}, u32[]{:S(2)}, u32[]{:S(2)}) collective-permute-start(f32[3,2,16,128]{3,2,1,0:T(8,128)S(1)} %get-tuple-element.55), channel_id=1, source_target_pairs={{0,16},{16,0},{32,48},{48,32},{64,80},{80,64},{96,112},{112,96},{1... | collective-permute-start | bytes 147464 | tf_op jit(solution)/shard_map/ppermute | solution.py:561

commit v6 on v5

--- a/solution.py
+++ b/solution.py
@@ -274,7 +274,7 @@
         force_x[2, p] = force_x[2, p] - (right - left)
         return carry
 
-    lax.fori_loop(0, 8, drift, 0)
+    lax.fori_loop(0, 8, drift, 0, unroll=4)
     smooth(v0, force_x, kinv_x, obst_x, v1, v2)
 
     shape = (16, 256)

time: 82.2 us -> 81.8 us (level)
  no operation moved by 1% of the time
where the time goes in v6:
time: 81.8 us; the launch traced here: 81.7 us
  waiting for transfers between devices  41.6 us (51%)
  starting transfers between devices  25 us (31%)
  Pallas kernels  14 us (17%)
  between operations  0.89 us (1%)
    ppermute x10, waiting for transfers between devices, swap_odd(): return lax.ppermute(x, axis, ODD)  30.6 us
    ppermute x10, starting transfers between devices, swap_odd(): return lax.ppermute(x, axis, ODD)  22.6 us
    pallas_call x7, Pallas kernels, call(): pl.pallas_call(kernel, out_shape=[jax.ShapeDtypeStruct(x, F32) for x in o...  14 us
    ppermute x10, waiting for transfers between devices, swap_even(): return lax.ppermute(x, axis, EVEN)  11 us
    ppermute x10, starting transfers between devices, swap_even(): return lax.ppermute(x, axis, EVEN)  2.38 us
  transfers between devices with their start and end apart: 20, of which 10 were waited for; matrix products, arithmetic and copies ran while one was open for 0% of the time, Pallas kernels for 7%

profile of v6, /device:TPU:0, one launch (start us, length us, event | category | flops | bytes accessed | tf_op | source)
XLA Modules:
  0.0 81.7 jit_solution(11519096279887806906)
XLA Ops:
  0.6 0.0 copy-start.4
  0.6 0.0 copy-start.1
  0.7 0.0 copy-start
  0.7 0.0 copy-start.7
  0.7 0.0 copy-start.6
  0.7 0.0 copy-start.5
  0.7 0.0 copy-start.3
  0.7 0.0 copy-start.2
  0.7 0.1 pad_add_fusion.pos
  0.8 2.2 %shard_map.95 = (f32[6,4,16,256]{3,2,1,0:T(8,128)S(1)}, f32[4,16,256]{2,1,0:T(8,128)S(1)}, f32[35,16,256]{2,1,0:T(8,128)S(1)}, f32[32,16,256]{2,1,0:T(8,128)S(1)...) custom-call(s32[2]{0:T(128)S(1)} %pad_add_fusion.pos, f32[3,4,16,256]{3,2,1,0:T(8,128)} %disp.1, ...), custom_call_target="tpu_custom_call" | custom-call | tf_op jit(solution)/shard_map/pallas_call | solution.py:546
  3.0 0.3 collective-permute-start
  3.2 7.4 %collective-permute-start.1 = (f32[32,16,256]{2,1,0:T(8,128)S(1)}, f32[32,16,256]{2,1,0:T(8,128)S(1)}, u32[]{:S(2)}, u32[]{:S(2)}) collective-permute-start(f32[32,16,256]{2,1,0:T(8,128)S(1)} %get-tuple-element.34), channel_id=1, source_target_pairs={{0,240},{16,32},{32,16},{48,64},{64,48},{80,96},{96,80},{112,128},... | collective-permute-start | bytes 1572872 | tf_op jit(solution)/shard_map/ppermute | solution.py:565
  10.7 0.0 collective-permute-start.2
  10.7 3.2 %collective-permute-start.3 = (f32[40,8,128]{2,1,0:T(8,128)S(1)}, f32[40,8,128]{2,1,0:T(8,128)S(1)}, u32[]{:S(2)}, u32[]{:S(2)}) collective-permute-start(f32[40,8,128]{2,1,0:T(8,128)S(1)} %get-tuple-element.36), channel_id=1, source_target_pairs={{0,15},{1,2},{2,1},{3,4},{4,3},{5,6},{6,5},{7,8},{8,7},{9,10},{10,... | collective-permute-start | bytes 491528 | tf_op jit(solution)/shard_map/ppermute | solution.py:565
  13.8 8.6 %collective-permute-done.1.ro = f32[32,16,256]{2,1,0:T(8,128)S(1)} collective-permute-done((f32[32,16,256]{2,1,0:T(8,128)S(1)}, f32[32,16,256]{2,1,0:T(8,128)S(1)}, u32[]{:S(2)}, u32[]{:S(2)}) %collective-permute-start.1) | collective-permute-done | bytes 524320 | tf_op jit(solution)/shard_map/ppermute | solution.py:565
  22.4 0.0 collective-permute-done.re
  22.4 0.6 shard_map.96
  23.0 5.4 %collective-permute-start.6 = (f32[24,8,128]{2,1,0:T(8,128)S(1)}, f32[24,8,128]{2,1,0:T(8,128)S(1)}, u32[]{:S(2)}, u32[]{:S(2)}) collective-permute-start(f32[24,8,128]{2,1,0:T(8,128)S(1)} %get-tuple-element.42.k01), channel_id=1, source_target_pairs={{0,240},{16,32},{32,16},{48,64},{64,48},{80,96},{96,80},{112,128},... | collective-permute-start | bytes 294920 | tf_op jit(solution)/shard_map/ppermute | solution.py:565
  28.5 3.2 %collective-permute-start.5 = (f32[13,8,128]{2,1,0:T(8,128)S(1)}, f32[13,8,128]{2,1,0:T(8,128)S(1)}, u32[]{:S(2)}, u32[]{:S(2)}) collective-permute-start(f32[13,8,128]{2,1,0:T(8,128)S(1)} %get-tuple-element.39), channel_id=1, source_target_pairs={{0,15},{1,2},{2,1},{3,4},{4,3},{5,6},{6,5},{7,8},{8,7},{9,10},{10,... | collective-permute-start | bytes 159752 | tf_op jit(solution)/shard_map/ppermute | solution.py:565
  31.6 0.0 collective-permute-done.2.be
  31.6 0.0 collective-permute-done.3.bo
  31.6 0.0 collective-permute-done.4.ce
  31.6 2.5 %collective-permute-done.5.co = f32[13,8,128]{2,1,0:T(8,128)S(1)} collective-permute-done((f32[13,8,128]{2,1,0:T(8,128)S(1)}, f32[13,8,128]{2,1,0:T(8,128)S(1)}, u32[]{:S(2)}, u32[]{:S(2)}) %collective-permute-start.5) | collective-permute-done | bytes 53280 | tf_op jit(solution)/shard_map/ppermute | solution.py:565
  34.2 2.7 %shard_map.97 = (f32[3,8,24,256]{3,2,1,0:T(8,128)S(1)}, f32[6,8,24,256]{3,2,1,0:T(8,128)S(1)}, f32[8,24,256]{2,1,0:T(8,128)S(1)}, f32[3,6,24,256]{3,2,1,0:T(8,12...) custom-call(s32[2]{0:T(128)S(1)} %pad_add_fusion.pos, ...), custom_call_target="tpu_custom_call" | custom-call | tf_op jit(solution)/shard_map/pallas_call | solution.py:546
  36.9 0.1 collective-permute-start.7
  37.0 0.4 collective-permute-start.9
  37.4 1.6 %collective-permute-start.8 = (f32[12,16,256]{2,1,0:T(8,128)S(1)}, f32[12,16,256]{2,1,0:T(8,128)S(1)}, u32[]{:S(2)}, u32[]{:S(2)}) collective-permute-start(f32[12,16,256]{2,1,0:T(8,128)S(1)} %get-tuple-element.43), channel_id=1, source_target_pairs={{0,16},{16,0},{32,48},{48,32},{64,80},{80,64},{96,112},{112,96},{1... | collective-permute-start | bytes 589832 | tf_op jit(solution)/shard_map/ppermute | solution.py:561
  39.0 4.3 %collective-permute-done.7.eb = f32[32,8,128]{2,1,0:T(8,128)S(1)} collective-permute-done((f32[32,8,128]{2,1,0:T(8,128)S(1)}, f32[32,8,128]{2,1,0:T(8,128)S(1)}, u32[]{:S(2)}, u32[]{:S(2)}) %collective-permute-start.7) | collective-permute-done | bytes 131104 | tf_op jit(solution)/shard_map/ppermute | solution.py:561
  43.3 0.1 collective-permute-start.12
  43.4 3.5 %collective-permute-done.9.go = f32[12,16,256]{2,1,0:T(8,128)S(1)} collective-permute-done((f32[12,16,256]{2,1,0:T(8,128)S(1)}, f32[12,16,256]{2,1,0:T(8,128)S(1)}, u32[]{:S(2)}, u32[]{:S(2)}) %collective-permute-start.9) | collective-permute-done | bytes 196640 | tf_op jit(solution)/shard_map/ppermute | solution.py:565
  47.0 0.0 collective-permute-done.8.ge
  47.0 2.0 %collective-permute-start.11 = (f32[65,8,128]{2,1,0:T(8,128)S(1)}, f32[65,8,128]{2,1,0:T(8,128)S(1)}, u32[]{:S(2)}, u32[]{:S(2)}) collective-permute-start(f32[65,8,128]{2,1,0:T(8,128)S(1)} %get-tuple-element.60), channel_id=1, source_target_pairs={{0,15},{1,2},{2,1},{3,4},{4,3},{5,6},{6,5},{7,8},{8,7},{9,10},{10,... | collective-permute-start | bytes 798728 | tf_op jit(solution)/shard_map/ppermute | solution.py:565
  49.0 0.0 collective-permute-start.10
  49.0 3.5 %collective-permute-done.12.ob = f32[40,8,128]{2,1,0:T(8,128)S(1)} collective-permute-done((f32[40,8,128]{2,1,0:T(8,128)S(1)}, f32[40,8,128]{2,1,0:T(8,128)S(1)}, u32[]{:S(2)}, u32[]{:S(2)}) %collective-permute-start.12) | collective-permute-done | bytes 163872 | tf_op jit(solution)/shard_map/ppermute | solution.py:565
  52.5 1.0 %collective-permute-start.16 = (f32[72,8,128]{2,1,0:T(8,128)S(1)}, f32[72,8,128]{2,1,0:T(8,128)S(1)}, u32[]{:S(2)}, u32[]{:S(2)}) collective-permute-start(f32[72,8,128]{2,1,0:T(8,128)S(1)} %constant_dynamic-update-slice_fusion), channel_id=1, source_target_pairs={{0,15},{1,2},{2,1},{3,4},{4,3},{5,6},{6,5},{7,8},{8,7},{9,10},{10,... | collective-permute-start | bytes 884744 | tf_op jit(solution)/shard_map/ppermute | solution.py:565
  53.5 0.0 collective-permute-start.15
  53.5 3.3 %collective-permute-done.13.b3 = f32[16,8,128]{2,1,0:T(8,128)S(1)} collective-permute-done((f32[16,8,128]{2,1,0:T(8,128)S(1)}, f32[16,8,128]{2,1,0:T(8,128)S(1)}, u32[]{:S(2)}, u32[]{:S(2)}) %collective-permute-start.13) | collective-permute-done | bytes 65568 | tf_op jit(solution)/shard_map/ppermute | solution.py:561
  56.7 0.0 collective-permute-start.14
  56.7 8.0 %collective-permute-done.14.b4 = f32[16,8,128]{2,1,0:T(8,128)S(1)} collective-permute-done((f32[16,8,128]{2,1,0:T(8,128)S(1)}, f32[16,8,128]{2,1,0:T(8,128)S(1)}, u32[]{:S(2)}, u32[]{:S(2)}) %collective-permute-start.14) | collective-permute-done | bytes 65568 | tf_op jit(solution)/shard_map/ppermute | solution.py:565
  64.7 0.3 collective-permute-start.17
  65.0 0.1 collective-permute-done.16.rmo
  65.2 1.6 %shard_map.99 = (f32[6,16,24,128]{3,2,1,0:T(8,128)S(1)}, f32[6,16,24,128]{3,2,1,0:T(8,128)S(1)}, f32[6,8,24,128]{3,2,1,0:T(8,128)S(1)}) custom-call(s32[2]{0:T(128)S(1)} %pad_add_fusion.pos, f32[32,8,128]{2,1,0:T(8,128)S(1)} %collective-permute-done.7.eb, f32[40,8,128]{2,1,0:T(8,128)S(1)} %collective-permute-done.12.ob, ...), custom_call_target="tpu_custom_call" | custom-call | tf_op jit(solution)/shard_map/pallas_call | solution.py:546
  66.8 4.4 %collective-permute-done.18.r2o = f32[32,8,128]{2,1,0:T(8,128)S(1)} collective-permute-done((f32[32,8,128]{2,1,0:T(8,128)S(1)}, f32[32,8,128]{2,1,0:T(8,128)S(1)}, u32[]{:S(2)}, u32[]{:S(2)}) %collective-permute-start.18) | collective-permute-done | bytes 131104 | tf_op jit(solution)/shard_map/ppermute | solution.py:565
  71.2 3.2 %shard_map.100 = (f32[3,4,16,128]{3,2,1,0:T(8,128)S(1)}, f32[3,2,16,128]{3,2,1,0:T(8,128)S(1)}) custom-call(s32[2]{0:T(128)S(1)} %pad_add_fusion.pos, f32[8,8,128]{2,1,0:T(8,128)S(1)} %get-tuple-element.46.b0, f32[32,8,128]{2,1,0:T(8,128)S(1)} %collective-permute-done.7.eb, f32[40,8,128]{2,1,0:T(8,128)S(1)} %collective-permute-done.12.ob, ...), custom_call_target="tpu_custom_call" | custom-call | tf_op jit(solution)/shard_map/pallas_call | solution.py:546
  74.5 0.1 collective-permute-start.19
  74.6 0.7 shard_map.98
  75.2 3.4 %collective-permute-done.19.other = f32[3,2,16,128]{3,2,1,0:T(8,128)S(1)} collective-permute-done((f32[3,2,16,128]{3,2,1,0:T(8,128)S(1)}, f32[3,2,16,128]{3,2,1,0:T(8,128)S(1)}, u32[]{:S(2)}, u32[]{:S(2)}) %collective-permute-start.19) | collective-permute-done | bytes 49184 | tf_op jit(solution)/shard_map/ppermute | solution.py:561
  78.6 3.0 %shard_map.101 = (f32[3,4,16,256]{3,2,1,0:T(8,128)}, f32[3,4,16,256]{3,2,1,0:T(8,128)}) custom-call(s32[2]{0:T(128)S(1)} %pad_add_fusion.pos, f32[3,10,24,256]{3,2,1,0:T(8,128)S(1)} %get-tuple-element.49.held, f32[3,4,16,128]{3,2,1,0:T(8,128)S(1)} %get-tuple-element.54.mid2, f32[3,2,16,128]{3,2,1,0:T(8,128)S(1)} %collective-permute-done.19.other, ...), custom_call_target="tpu_custom_call" | custom-call | tf_op jit(solution)/shard_map/pallas_call | solution.py:546
  (24 shorter events, 0.1 us)
Async XLA Ops:
  0.6 33.5 %copy-start.4 = (s32[4,16,256]{2,1,0:T(8,128)S(1)}, s32[4,16,256]{2,1,0:T(8,128)}, u32[]{:S(2)}) copy-start(s32[4,16,256]{2,1,0:T(8,128)} %clip.3) | copy-start | bytes 196612
  0.6 33.5 %copy-start.1 = (f32[3,4,16,256]{3,2,1,0:T(8,128)S(1)}, f32[3,4,16,256]{3,2,1,0:T(8,128)}, u32[]{:S(2)}) copy-start(f32[3,4,16,256]{3,2,1,0:T(8,128)} %cross.3) | copy-start | bytes 589828
  0.7 33.5 %copy-start = (f32[3,4,16,256]{3,2,1,0:T(8,128)S(1)}, f32[3,4,16,256]{3,2,1,0:T(8,128)}, u32[]{:S(2)}) copy-start(f32[3,4,16,256]{3,2,1,0:T(8,128)} %main.3) | copy-start | bytes 589828
  0.7 33.5 %copy-start.7 = (s32[4,16,256]{2,1,0:T(8,128)S(1)}, s32[4,16,256]{2,1,0:T(8,128)}, u32[]{:S(2)}) copy-start(s32[4,16,256]{2,1,0:T(8,128)} %touch.1) | copy-start | bytes 196612
  0.7 33.5 %copy-start.6 = (f32[4,16,256]{2,1,0:T(8,128)S(1)}, f32[4,16,256]{2,1,0:T(8,128)}, u32[]{:S(2)}) copy-start(f32[4,16,256]{2,1,0:T(8,128)} %clear.1) | copy-start | bytes 196612
  0.7 33.5 %copy-start.5 = (f32[4,16,256]{2,1,0:T(8,128)S(1)}, f32[4,16,256]{2,1,0:T(8,128)}, u32[]{:S(2)}) copy-start(f32[4,16,256]{2,1,0:T(8,128)} %heat.1) | copy-start | bytes 196612
  0.7 33.5 %copy-start.3 = (f32[3,4,16,256]{3,2,1,0:T(8,128)S(1)}, f32[3,4,16,256]{3,2,1,0:T(8,128)}, u32[]{:S(2)}) copy-start(f32[3,4,16,256]{3,2,1,0:T(8,128)} %trac.1) | copy-start | bytes 589828
  0.7 33.5 %copy-start.2 = (f32[3,4,16,256]{3,2,1,0:T(8,128)S(1)}, f32[3,4,16,256]{3,2,1,0:T(8,128)}, u32[]{:S(2)}) copy-start(f32[3,4,16,256]{3,2,1,0:T(8,128)} %disp.1) | copy-start | bytes 589828
  3.0 19.4 %collective-permute-start = (f32[35,16,256]{2,1,0:T(8,128)S(1)}, f32[35,16,256]{2,1,0:T(8,128)S(1)}, u32[]{:S(2)}, u32[]{:S(2)}) collective-permute-start(f32[35,16,256]{2,1,0:T(8,128)S(1)} %get-tuple-element.33), channel_id=1, source_target_pairs={{0,16},{16,0},{32,48},{48,32},{64,80},{80,64},{96,112},{112,96},{1... | collective-permute-start | bytes 1720328 | tf_op jit(solution)/shard_map/ppermute | solution.py:561
  3.2 19.1 %collective-permute-start.1 = (f32[32,16,256]{2,1,0:T(8,128)S(1)}, f32[32,16,256]{2,1,0:T(8,128)S(1)}, u32[]{:S(2)}, u32[]{:S(2)}) collective-permute-start(f32[32,16,256]{2,1,0:T(8,128)S(1)} %get-tuple-element.34), channel_id=1, source_target_pairs={{0,240},{16,32},{32,16},{48,64},{64,48},{80,96},{96,80},{112,128},... | collective-permute-start | bytes 1572872 | tf_op jit(solution)/shard_map/ppermute | solution.py:565
  10.7 21.0 %collective-permute-start.2 = (f32[40,8,128]{2,1,0:T(8,128)S(1)}, f32[40,8,128]{2,1,0:T(8,128)S(1)}, u32[]{:S(2)}, u32[]{:S(2)}) collective-permute-start(f32[40,8,128]{2,1,0:T(8,128)S(1)} %get-tuple-element.35), channel_id=1, source_target_pairs={{0,1},{1,0},{2,3},{3,2},{4,5},{5,4},{6,7},{7,6},{8,9},{9,8},{10,11... | collective-permute-start | bytes 491528 | tf_op jit(solution)/shard_map/ppermute | solution.py:561
  10.7 21.0 %collective-permute-start.3 = (f32[40,8,128]{2,1,0:T(8,128)S(1)}, f32[40,8,128]{2,1,0:T(8,128)S(1)}, u32[]{:S(2)}, u32[]{:S(2)}) collective-permute-start(f32[40,8,128]{2,1,0:T(8,128)S(1)} %get-tuple-element.36), channel_id=1, source_target_pairs={{0,15},{1,2},{2,1},{3,4},{4,3},{5,6},{6,5},{7,8},{8,7},{9,10},{10,... | collective-permute-start | bytes 491528 | tf_op jit(solution)/shard_map/ppermute | solution.py:565
  23.0 13.9 %collective-permute-start.6 = (f32[24,8,128]{2,1,0:T(8,128)S(1)}, f32[24,8,128]{2,1,0:T(8,128)S(1)}, u32[]{:S(2)}, u32[]{:S(2)}) collective-permute-start(f32[24,8,128]{2,1,0:T(8,128)S(1)} %get-tuple-element.42.k01), channel_id=1, source_target_pairs={{0,240},{16,32},{32,16},{48,64},{64,48},{80,96},{96,80},{112,128},... | collective-permute-start | bytes 294920 | tf_op jit(solution)/shard_map/ppermute | solution.py:565
  28.5 3.2 %collective-permute-start.4 = (f32[13,8,128]{2,1,0:T(8,128)S(1)}, f32[13,8,128]{2,1,0:T(8,128)S(1)}, u32[]{:S(2)}, u32[]{:S(2)}) collective-permute-start(f32[13,8,128]{2,1,0:T(8,128)S(1)} %get-tuple-element.38), channel_id=1, source_target_pairs={{0,1},{1,0},{2,3},{3,2},{4,5},{5,4},{6,7},{7,6},{8,9},{9,8},{10,11... | collective-permute-start | bytes 159752 | tf_op jit(solution)/shard_map/ppermute | solution.py:561
  28.5 5.7 %collective-permute-start.5 = (f32[13,8,128]{2,1,0:T(8,128)S(1)}, f32[13,8,128]{2,1,0:T(8,128)S(1)}, u32[]{:S(2)}, u32[]{:S(2)}) collective-permute-start(f32[13,8,128]{2,1,0:T(8,128)S(1)} %get-tuple-element.39), channel_id=1, source_target_pairs={{0,15},{1,2},{2,1},{3,4},{4,3},{5,6},{6,5},{7,8},{8,7},{9,10},{10,... | collective-permute-start | bytes 159752 | tf_op jit(solution)/shard_map/ppermute | solution.py:565
  36.9 6.4 %collective-permute-start.7 = (f32[32,8,128]{2,1,0:T(8,128)S(1)}, f32[32,8,128]{2,1,0:T(8,128)S(1)}, u32[]{:S(2)}, u32[]{:S(2)}) collective-permute-start(f32[32,8,128]{2,1,0:T(8,128)S(1)} %pad_maximum_fusion.4), channel_id=1, source_target_pairs={{0,16},{16,0},{32,48},{48,32},{64,80},{80,64},{96,112},{112,96},{1... | collective-permute-start | bytes 393224 | tf_op jit(solution)/shard_map/ppermute | solution.py:561
  37.0 9.9 %collective-permute-start.9 = (f32[12,16,256]{2,1,0:T(8,128)S(1)}, f32[12,16,256]{2,1,0:T(8,128)S(1)}, u32[]{:S(2)}, u32[]{:S(2)}) collective-permute-start(f32[12,16,256]{2,1,0:T(8,128)S(1)} %get-tuple-element.43), channel_id=1, source_target_pairs={{0,240},{16,32},{32,16},{48,64},{64,48},{80,96},{96,80},{112,128},... | collective-permute-start | bytes 589832 | tf_op jit(solution)/shard_map/ppermute | solution.py:565
  37.4 9.6 %collective-permute-start.8 = (f32[12,16,256]{2,1,0:T(8,128)S(1)}, f32[12,16,256]{2,1,0:T(8,128)S(1)}, u32[]{:S(2)}, u32[]{:S(2)}) collective-permute-start(f32[12,16,256]{2,1,0:T(8,128)S(1)} %get-tuple-element.43), channel_id=1, source_target_pairs={{0,16},{16,0},{32,48},{48,32},{64,80},{80,64},{96,112},{112,96},{1... | collective-permute-start | bytes 589832 | tf_op jit(solution)/shard_map/ppermute | solution.py:561
  43.3 9.1 %collective-permute-start.12 = (f32[40,8,128]{2,1,0:T(8,128)S(1)}, f32[40,8,128]{2,1,0:T(8,128)S(1)}, u32[]{:S(2)}, u32[]{:S(2)}) collective-permute-start(f32[40,8,128]{2,1,0:T(8,128)S(1)} %pad_maximum_fusion.3), channel_id=1, source_target_pairs={{0,240},{16,32},{32,16},{48,64},{64,48},{80,96},{96,80},{112,128},... | collective-permute-start | bytes 491528 | tf_op jit(solution)/shard_map/ppermute | solution.py:565
  47.0 17.7 %collective-permute-start.11 = (f32[65,8,128]{2,1,0:T(8,128)S(1)}, f32[65,8,128]{2,1,0:T(8,128)S(1)}, u32[]{:S(2)}, u32[]{:S(2)}) collective-permute-start(f32[65,8,128]{2,1,0:T(8,128)S(1)} %get-tuple-element.60), channel_id=1, source_target_pairs={{0,15},{1,2},{2,1},{3,4},{4,3},{5,6},{6,5},{7,8},{8,7},{9,10},{10,... | collective-permute-start | bytes 798728 | tf_op jit(solution)/shard_map/ppermute | solution.py:565
  49.0 16.0 %collective-permute-start.10 = (f32[65,8,128]{2,1,0:T(8,128)S(1)}, f32[65,8,128]{2,1,0:T(8,128)S(1)}, u32[]{:S(2)}, u32[]{:S(2)}) collective-permute-start(f32[65,8,128]{2,1,0:T(8,128)S(1)} %get-tuple-element.61), channel_id=1, source_target_pairs={{0,1},{1,0},{2,3},{3,2},{4,5},{5,4},{6,7},{7,6},{8,9},{9,8},{10,11... | collective-permute-start | bytes 798728 | tf_op jit(solution)/shard_map/ppermute | solution.py:561
  52.5 4.3 %collective-permute-start.13 = (f32[16,8,128]{2,1,0:T(8,128)S(1)}, f32[16,8,128]{2,1,0:T(8,128)S(1)}, u32[]{:S(2)}, u32[]{:S(2)}) collective-permute-start(f32[16,8,128]{2,1,0:T(8,128)S(1)} %slice.4), channel_id=1, source_target_pairs={{0,16},{16,0},{32,48},{48,32},{64,80},{80,64},{96,112},{112,96},{1... | collective-permute-start | bytes 196616 | tf_op jit(solution)/shard_map/ppermute | solution.py:561
  52.5 12.7 %collective-permute-start.16 = (f32[72,8,128]{2,1,0:T(8,128)S(1)}, f32[72,8,128]{2,1,0:T(8,128)S(1)}, u32[]{:S(2)}, u32[]{:S(2)}) collective-permute-start(f32[72,8,128]{2,1,0:T(8,128)S(1)} %constant_dynamic-update-slice_fusion), channel_id=1, source_target_pairs={{0,15},{1,2},{2,1},{3,4},{4,3},{5,6},{6,5},{7,8},{8,7},{9,10},{10,... | collective-permute-start | bytes 884744 | tf_op jit(solution)/shard_map/ppermute | solution.py:565
  53.5 11.7 %collective-permute-start.15 = (f32[72,8,128]{2,1,0:T(8,128)S(1)}, f32[72,8,128]{2,1,0:T(8,128)S(1)}, u32[]{:S(2)}, u32[]{:S(2)}) collective-permute-start(f32[72,8,128]{2,1,0:T(8,128)S(1)} %constant_dynamic-update-slice_fusion), channel_id=1, source_target_pairs={{0,1},{1,0},{2,3},{3,2},{4,5},{5,4},{6,7},{7,6},{8,9},{9,8},{10,11... | collective-permute-start | bytes 884744 | tf_op jit(solution)/shard_map/ppermute | solution.py:561
  56.7 8.0 %collective-permute-start.14 = (f32[16,8,128]{2,1,0:T(8,128)S(1)}, f32[16,8,128]{2,1,0:T(8,128)S(1)}, u32[]{:S(2)}, u32[]{:S(2)}) collective-permute-start(f32[16,8,128]{2,1,0:T(8,128)S(1)} %collective-permute-done.13.b3), channel_id=1, source_target_pairs={{0,240},{16,32},{32,16},{48,64},{64,48},{80,96},{96,80},{112,128},... | collective-permute-start | bytes 196616 | tf_op jit(solution)/shard_map/ppermute | solution.py:565
  64.7 6.5 %collective-permute-start.18 = (f32[32,8,128]{2,1,0:T(8,128)S(1)}, f32[32,8,128]{2,1,0:T(8,128)S(1)}, u32[]{:S(2)}, u32[]{:S(2)}) collective-permute-start(f32[32,8,128]{2,1,0:T(8,128)S(1)} %constant_dynamic-update-slice_fusion.2), channel_id=1, source_target_pairs={{0,15},{1,2},{2,1},{3,4},{4,3},{5,6},{6,5},{7,8},{8,7},{9,10},{10,... | collective-permute-start | bytes 393224 | tf_op jit(solution)/shard_map/ppermute | solution.py:565
  64.7 6.5 %collective-permute-start.17 = (f32[32,8,128]{2,1,0:T(8,128)S(1)}, f32[32,8,128]{2,1,0:T(8,128)S(1)}, u32[]{:S(2)}, u32[]{:S(2)}) collective-permute-start(f32[32,8,128]{2,1,0:T(8,128)S(1)} %constant_dynamic-update-slice_fusion.2), channel_id=1, source_target_pairs={{0,1},{1,0},{2,3},{3,2},{4,5},{5,4},{6,7},{7,6},{8,9},{9,8},{10,11... | collective-permute-start | bytes 393224 | tf_op jit(solution)/shard_map/ppermute | solution.py:561
  74.5 4.2 %collective-permute-start.19 = (f32[3,2,16,128]{3,2,1,0:T(8,128)S(1)}, f32[3,2,16,128]{3,2,1,0:T(8,128)S(1)}, u32[]{:S(2)}, u32[]{:S(2)}) collective-permute-start(f32[3,2,16,128]{3,2,1,0:T(8,128)S(1)} %get-tuple-element.55), channel_id=1, source_target_pairs={{0,16},{16,0},{32,48},{48,32},{64,80},{80,64},{96,112},{112,96},{1... | collective-permute-start | bytes 147464 | tf_op jit(solution)/shard_map/ppermute | solution.py:561

commit v7 on v6

--- a/solution.py
+++ b/solution.py
@@ -357,7 +357,7 @@
                 to[16:24, :] = jnp.where(up, b, a)
             return carry
 
-        lax.fori_loop(0, 4 if force else 6, fill, 0, unroll=2)
+        lax.fori_loop(0, 4 if force else 6, fill, 0, unroll=True)
 
 
 def coarse_blocks(pos, eb, ob, k01, k23, r1e, r1o, rme, rmo, gk, ki, k3):
@@ -440,7 +440,7 @@
         o3[q] = room
         return carry
 
-    lax.fori_loop(1, 7, third, 0, unroll=4)
+    lax.fori_loop(1, 7, third, 0, unroll=3)
 
     def lowest(q, carry):
         rest = []
@@ -456,7 +456,7 @@
         return carry
 
     lax.fori_loop(2, 6, lowest, 0, unroll=4)
-    lax.fori_loop(5, 11, sweep(va, vb), 0, unroll=4)
+    lax.fori_loop(5, 11, sweep(va, vb), 0, unroll=3)
     lax.fori_loop(6, 10, sweep(vb, va), 0, unroll=4)
     for c in range(3):
         for k in range(4):
@@ -590,7 +590,9 @@
     )
     eb = swap_even(jnp.concatenate([b0, k23], 0), "grp")
     ob = swap_odd(jnp.concatenate([b0, eb], 0), "grp")
-    ge, go = swap_even(planes, "grp"), swap_odd(planes, "grp")
+    go = swap_odd(planes, "grp")
+    planes, eb = lax.optimization_barrier((planes, eb))
+    ge = swap_even(planes, "grp")
     after, go = lax.optimization_barrier((b0, go))
     r1e = swap_even(jnp.concatenate([after, k01, k23, pe], 0), "brick")
     r1o = swap_odd(jnp.concatenate([after, k01, k23, po], 0), "brick")

time: 81.8 us -> 82 us (level)
  the two profiles are of different devices: /device:TPU:0 before, /device:TPU:4 now
where the time goes in v7:
time: 82 us; the launch traced here: 81.9 us
  waiting for transfers between devices  43.2 us (53%)
  starting transfers between devices  23.9 us (29%)
  Pallas kernels  13.6 us (17%)
  between operations  0.91 us (1%)
    ppermute x10, waiting for transfers between devices, swap_odd(): return lax.ppermute(x, axis, ODD)  30.6 us
    ppermute x10, starting transfers between devices, swap_odd(): return lax.ppermute(x, axis, ODD)  21.4 us
    pallas_call x7, Pallas kernels, call(): pl.pallas_call(kernel, out_shape=[jax.ShapeDtypeStruct(x, F32) for x in o...  13.6 us
    ppermute x10, waiting for transfers between devices, swap_even(): return lax.ppermute(x, axis, EVEN)  12.7 us
    ppermute x10, starting transfers between devices, swap_even(): return lax.ppermute(x, axis, EVEN)  2.48 us
  transfers between devices with their start and end apart: 20, of which 10 were waited for; matrix products, arithmetic and copies ran while one was open for 0% of the time, Pallas kernels for 7%

profile of v7, /device:TPU:4, one launch (start us, length us, event | category | flops | bytes accessed | tf_op | source)
XLA Modules:
  0.0 81.9 jit_solution(7354862150436027507)
XLA Ops:
  0.6 0.0 copy-start.4
  0.6 0.0 copy-start.1
  0.7 0.0 copy-start
  0.7 0.0 copy-start.7
  0.7 0.0 copy-start.6
  0.7 0.0 copy-start.5
  0.7 0.0 copy-start.3
  0.7 0.0 copy-start.2
  0.7 0.1 pad_add_fusion.pos
  0.8 2.2 %shard_map.95 = (f32[6,4,16,256]{3,2,1,0:T(8,128)S(1)}, f32[4,16,256]{2,1,0:T(8,128)S(1)}, f32[35,16,256]{2,1,0:T(8,128)S(1)}, f32[32,16,256]{2,1,0:T(8,128)S(1)...) custom-call(s32[2]{0:T(128)S(1)} %pad_add_fusion.pos, f32[3,4,16,256]{3,2,1,0:T(8,128)} %disp.1, ...), custom_call_target="tpu_custom_call" | custom-call | tf_op jit(solution)/shard_map/pallas_call | solution.py:546
  3.0 2.0 %collective-permute-start = (f32[35,16,256]{2,1,0:T(8,128)S(1)}, f32[35,16,256]{2,1,0:T(8,128)S(1)}, u32[]{:S(2)}, u32[]{:S(2)}) collective-permute-start(f32[35,16,256]{2,1,0:T(8,128)S(1)} %get-tuple-element.35), channel_id=1, source_target_pairs={{0,16},{16,0},{32,48},{48,32},{64,80},{80,64},{96,112},{112,96},{1... | collective-permute-start | bytes 1720328 | tf_op jit(solution)/shard_map/ppermute | solution.py:561
  5.0 4.9 %collective-permute-start.1 = (f32[32,16,256]{2,1,0:T(8,128)S(1)}, f32[32,16,256]{2,1,0:T(8,128)S(1)}, u32[]{:S(2)}, u32[]{:S(2)}) collective-permute-start(f32[32,16,256]{2,1,0:T(8,128)S(1)} %get-tuple-element.36), channel_id=1, source_target_pairs={{0,240},{16,32},{32,16},{48,64},{64,48},{80,96},{96,80},{112,128},... | collective-permute-start | bytes 1572872 | tf_op jit(solution)/shard_map/ppermute | solution.py:565
  9.9 0.0 collective-permute-start.2
  9.9 4.7 %collective-permute-start.3 = (f32[40,8,128]{2,1,0:T(8,128)S(1)}, f32[40,8,128]{2,1,0:T(8,128)S(1)}, u32[]{:S(2)}, u32[]{:S(2)}) collective-permute-start(f32[40,8,128]{2,1,0:T(8,128)S(1)} %get-tuple-element.38), channel_id=1, source_target_pairs={{0,15},{1,2},{2,1},{3,4},{4,3},{5,6},{6,5},{7,8},{8,7},{9,10},{10,... | collective-permute-start | bytes 491528 | tf_op jit(solution)/shard_map/ppermute | solution.py:565
  14.5 7.5 %collective-permute-done.1.ro = f32[32,16,256]{2,1,0:T(8,128)S(1)} collective-permute-done((f32[32,16,256]{2,1,0:T(8,128)S(1)}, f32[32,16,256]{2,1,0:T(8,128)S(1)}, u32[]{:S(2)}, u32[]{:S(2)}) %collective-permute-start.1) | collective-permute-done | bytes 524320 | tf_op jit(solution)/shard_map/ppermute | solution.py:565
  22.1 0.0 collective-permute-done.re
  22.1 0.6 shard_map.96
  22.7 5.0 %collective-permute-start.6 = (f32[24,8,128]{2,1,0:T(8,128)S(1)}, f32[24,8,128]{2,1,0:T(8,128)S(1)}, u32[]{:S(2)}, u32[]{:S(2)}) collective-permute-start(f32[24,8,128]{2,1,0:T(8,128)S(1)} %get-tuple-element.45.k01), channel_id=1, source_target_pairs={{0,240},{16,32},{32,16},{48,64},{64,48},{80,96},{96,80},{112,128},... | collective-permute-start | bytes 294920 | tf_op jit(solution)/shard_map/ppermute | solution.py:565
  27.7 0.0 collective-permute-start.4
  27.7 4.7 %collective-permute-start.5 = (f32[13,8,128]{2,1,0:T(8,128)S(1)}, f32[13,8,128]{2,1,0:T(8,128)S(1)}, u32[]{:S(2)}, u32[]{:S(2)}) collective-permute-start(f32[13,8,128]{2,1,0:T(8,128)S(1)} %get-tuple-element.41), channel_id=1, source_target_pairs={{0,15},{1,2},{2,1},{3,4},{4,3},{5,6},{6,5},{7,8},{8,7},{9,10},{10,... | collective-permute-start | bytes 159752 | tf_op jit(solution)/shard_map/ppermute | solution.py:565
  32.4 0.0 collective-permute-done.2.be
  32.4 2.4 %collective-permute-done.5.co = f32[13,8,128]{2,1,0:T(8,128)S(1)} collective-permute-done((f32[13,8,128]{2,1,0:T(8,128)S(1)}, f32[13,8,128]{2,1,0:T(8,128)S(1)}, u32[]{:S(2)}, u32[]{:S(2)}) %collective-permute-start.5) | collective-permute-done | bytes 53280 | tf_op jit(solution)/shard_map/ppermute | solution.py:565
  34.8 2.7 %shard_map.97 = (f32[3,8,24,256]{3,2,1,0:T(8,128)S(1)}, f32[6,8,24,256]{3,2,1,0:T(8,128)S(1)}, f32[8,24,256]{2,1,0:T(8,128)S(1)}, f32[3,6,24,256]{3,2,1,0:T(8,12...) custom-call(s32[2]{0:T(128)S(1)} %pad_add_fusion.pos, ...), custom_call_target="tpu_custom_call" | custom-call | tf_op jit(solution)/shard_map/pallas_call | solution.py:546
  37.5 0.1 collective-permute-start.7
  37.6 0.1 collective-permute-start.9
  37.7 6.1 %collective-permute-done.7.eb = f32[32,8,128]{2,1,0:T(8,128)S(1)} collective-permute-done((f32[32,8,128]{2,1,0:T(8,128)S(1)}, f32[32,8,128]{2,1,0:T(8,128)S(1)}, u32[]{:S(2)}, u32[]{:S(2)}) %collective-permute-start.7) | collective-permute-done | bytes 131104 | tf_op jit(solution)/shard_map/ppermute | solution.py:561
  43.8 0.0 collective-permute-start.8
  43.8 0.1 collective-permute-start.12
  43.9 4.8 %collective-permute-done.9.go = f32[12,16,256]{2,1,0:T(8,128)S(1)} collective-permute-done((f32[12,16,256]{2,1,0:T(8,128)S(1)}, f32[12,16,256]{2,1,0:T(8,128)S(1)}, u32[]{:S(2)}, u32[]{:S(2)}) %collective-permute-start.9) | collective-permute-done | bytes 196640 | tf_op jit(solution)/shard_map/ppermute | solution.py:565
  48.8 0.9 %collective-permute-start.11 = (f32[65,8,128]{2,1,0:T(8,128)S(1)}, f32[65,8,128]{2,1,0:T(8,128)S(1)}, u32[]{:S(2)}, u32[]{:S(2)}) collective-permute-start(f32[65,8,128]{2,1,0:T(8,128)S(1)} %get-tuple-element.64), channel_id=1, source_target_pairs={{0,15},{1,2},{2,1},{3,4},{4,3},{5,6},{6,5},{7,8},{8,7},{9,10},{10,... | collective-permute-start | bytes 798728 | tf_op jit(solution)/shard_map/ppermute | solution.py:565
  49.7 3.3 %collective-permute-done.12.ob = f32[40,8,128]{2,1,0:T(8,128)S(1)} collective-permute-done((f32[40,8,128]{2,1,0:T(8,128)S(1)}, f32[40,8,128]{2,1,0:T(8,128)S(1)}, u32[]{:S(2)}, u32[]{:S(2)}) %collective-permute-start.12) | collective-permute-done | bytes 163872 | tf_op jit(solution)/shard_map/ppermute | solution.py:565
  53.0 0.0 collective-permute-done.8.ge
  53.0 1.1 %collective-permute-start.16 = (f32[72,8,128]{2,1,0:T(8,128)S(1)}, f32[72,8,128]{2,1,0:T(8,128)S(1)}, u32[]{:S(2)}, u32[]{:S(2)}) collective-permute-start(f32[72,8,128]{2,1,0:T(8,128)S(1)} %constant_dynamic-update-slice_fusion), channel_id=1, source_target_pairs={{0,15},{1,2},{2,1},{3,4},{4,3},{5,6},{6,5},{7,8},{8,7},{9,10},{10,... | collective-permute-start | bytes 884744 | tf_op jit(solution)/shard_map/ppermute | solution.py:565
  54.1 0.0 collective-permute-start.15
  54.1 3.1 %collective-permute-done.13.b3 = f32[16,8,128]{2,1,0:T(8,128)S(1)} collective-permute-done((f32[16,8,128]{2,1,0:T(8,128)S(1)}, f32[16,8,128]{2,1,0:T(8,128)S(1)}, u32[]{:S(2)}, u32[]{:S(2)}) %collective-permute-start.13) | collective-permute-done | bytes 65568 | tf_op jit(solution)/shard_map/ppermute | solution.py:561
  57.2 7.9 %collective-permute-done.14.b4 = f32[16,8,128]{2,1,0:T(8,128)S(1)} collective-permute-done((f32[16,8,128]{2,1,0:T(8,128)S(1)}, f32[16,8,128]{2,1,0:T(8,128)S(1)}, u32[]{:S(2)}, u32[]{:S(2)}) %collective-permute-start.14) | collective-permute-done | bytes 65568 | tf_op jit(solution)/shard_map/ppermute | solution.py:565
  65.1 0.0 collective-permute-done.11.r1o
  65.2 0.3 collective-permute-start.17
  65.4 0.0 collective-permute-done.10.r1e
  65.4 1.0 %collective-permute-done.16.rmo = f32[72,8,128]{2,1,0:T(8,128)S(1)} collective-permute-done((f32[72,8,128]{2,1,0:T(8,128)S(1)}, f32[72,8,128]{2,1,0:T(8,128)S(1)}, u32[]{:S(2)}, u32[]{:S(2)}) %collective-permute-start.16) | collective-permute-done | bytes 294944 | tf_op jit(solution)/shard_map/ppermute | solution.py:565
  66.4 0.0 collective-permute-done.15.rme
  66.4 1.4 %shard_map.99 = (f32[6,16,24,128]{3,2,1,0:T(8,128)S(1)}, f32[6,16,24,128]{3,2,1,0:T(8,128)S(1)}, f32[6,8,24,128]{3,2,1,0:T(8,128)S(1)}) custom-call(s32[2]{0:T(128)S(1)} %pad_add_fusion.pos, f32[32,8,128]{2,1,0:T(8,128)S(1)} %collective-permute-done.7.eb, f32[40,8,128]{2,1,0:T(8,128)S(1)} %collective-permute-done.12.ob, ...), custom_call_target="tpu_custom_call" | custom-call | tf_op jit(solution)/shard_map/pallas_call | solution.py:546
  67.9 3.7 %collective-permute-done.18.r2o = f32[32,8,128]{2,1,0:T(8,128)S(1)} collective-permute-done((f32[32,8,128]{2,1,0:T(8,128)S(1)}, f32[32,8,128]{2,1,0:T(8,128)S(1)}, u32[]{:S(2)}, u32[]{:S(2)}) %collective-permute-start.18) | collective-permute-done | bytes 131104 | tf_op jit(solution)/shard_map/ppermute | solution.py:565
  71.6 3.1 %shard_map.100 = (f32[3,4,16,128]{3,2,1,0:T(8,128)S(1)}, f32[3,2,16,128]{3,2,1,0:T(8,128)S(1)}) custom-call(s32[2]{0:T(128)S(1)} %pad_add_fusion.pos, f32[8,8,128]{2,1,0:T(8,128)S(1)} %get-tuple-element.50.b0, f32[32,8,128]{2,1,0:T(8,128)S(1)} %collective-permute-done.7.eb, f32[40,8,128]{2,1,0:T(8,128)S(1)} %collective-permute-done.12.ob, ...), custom_call_target="tpu_custom_call" | custom-call | tf_op jit(solution)/shard_map/pallas_call | solution.py:546
  74.7 0.1 collective-permute-start.19
  74.8 0.7 shard_map.98
  75.5 3.4 %collective-permute-done.19.other = f32[3,2,16,128]{3,2,1,0:T(8,128)S(1)} collective-permute-done((f32[3,2,16,128]{3,2,1,0:T(8,128)S(1)}, f32[3,2,16,128]{3,2,1,0:T(8,128)S(1)}, u32[]{:S(2)}, u32[]{:S(2)}) %collective-permute-start.19) | collective-permute-done | bytes 49184 | tf_op jit(solution)/shard_map/ppermute | solution.py:561
  78.9 3.0 %shard_map.101 = (f32[3,4,16,256]{3,2,1,0:T(8,128)}, f32[3,4,16,256]{3,2,1,0:T(8,128)}) custom-call(s32[2]{0:T(128)S(1)} %pad_add_fusion.pos, f32[3,10,24,256]{3,2,1,0:T(8,128)S(1)} %get-tuple-element.53.held, f32[3,4,16,128]{3,2,1,0:T(8,128)S(1)} %get-tuple-element.58.mid2, f32[3,2,16,128]{3,2,1,0:T(8,128)S(1)} %collective-permute-done.19.other, ...), custom_call_target="tpu_custom_call" | custom-call | tf_op jit(solution)/shard_map/pallas_call | solution.py:546
  (24 shorter events, 0.1 us)
Async XLA Ops:
  0.6 34.1 %copy-start.4 = (s32[4,16,256]{2,1,0:T(8,128)S(1)}, s32[4,16,256]{2,1,0:T(8,128)}, u32[]{:S(2)}) copy-start(s32[4,16,256]{2,1,0:T(8,128)} %clip.3) | copy-start | bytes 196612
  0.6 34.1 %copy-start.1 = (f32[3,4,16,256]{3,2,1,0:T(8,128)S(1)}, f32[3,4,16,256]{3,2,1,0:T(8,128)}, u32[]{:S(2)}) copy-start(f32[3,4,16,256]{3,2,1,0:T(8,128)} %cross.3) | copy-start | bytes 589828
  0.7 34.1 %copy-start = (f32[3,4,16,256]{3,2,1,0:T(8,128)S(1)}, f32[3,4,16,256]{3,2,1,0:T(8,128)}, u32[]{:S(2)}) copy-start(f32[3,4,16,256]{3,2,1,0:T(8,128)} %main.3) | copy-start | bytes 589828
  0.7 34.1 %copy-start.7 = (s32[4,16,256]{2,1,0:T(8,128)S(1)}, s32[4,16,256]{2,1,0:T(8,128)}, u32[]{:S(2)}) copy-start(s32[4,16,256]{2,1,0:T(8,128)} %touch.1) | copy-start | bytes 196612
  0.7 34.1 %copy-start.6 = (f32[4,16,256]{2,1,0:T(8,128)S(1)}, f32[4,16,256]{2,1,0:T(8,128)}, u32[]{:S(2)}) copy-start(f32[4,16,256]{2,1,0:T(8,128)} %clear.1) | copy-start | bytes 196612
  0.7 34.1 %copy-start.5 = (f32[4,16,256]{2,1,0:T(8,128)S(1)}, f32[4,16,256]{2,1,0:T(8,128)}, u32[]{:S(2)}) copy-start(f32[4,16,256]{2,1,0:T(8,128)} %heat.1) | copy-start | bytes 196612
  0.7 34.1 %copy-start.3 = (f32[3,4,16,256]{3,2,1,0:T(8,128)S(1)}, f32[3,4,16,256]{3,2,1,0:T(8,128)}, u32[]{:S(2)}) copy-start(f32[3,4,16,256]{3,2,1,0:T(8,128)} %trac.1) | copy-start | bytes 589828
  0.7 34.1 %copy-start.2 = (f32[3,4,16,256]{3,2,1,0:T(8,128)S(1)}, f32[3,4,16,256]{3,2,1,0:T(8,128)}, u32[]{:S(2)}) copy-start(f32[3,4,16,256]{3,2,1,0:T(8,128)} %disp.1) | copy-start | bytes 589828
  3.0 19.1 %collective-permute-start = (f32[35,16,256]{2,1,0:T(8,128)S(1)}, f32[35,16,256]{2,1,0:T(8,128)S(1)}, u32[]{:S(2)}, u32[]{:S(2)}) collective-permute-start(f32[35,16,256]{2,1,0:T(8,128)S(1)} %get-tuple-element.35), channel_id=1, source_target_pairs={{0,16},{16,0},{32,48},{48,32},{64,80},{80,64},{96,112},{112,96},{1... | collective-permute-start | bytes 1720328 | tf_op jit(solution)/shard_map/ppermute | solution.py:561
  5.0 17.1 %collective-permute-start.1 = (f32[32,16,256]{2,1,0:T(8,128)S(1)}, f32[32,16,256]{2,1,0:T(8,128)S(1)}, u32[]{:S(2)}, u32[]{:S(2)}) collective-permute-start(f32[32,16,256]{2,1,0:T(8,128)S(1)} %get-tuple-element.36), channel_id=1, source_target_pairs={{0,240},{16,32},{32,16},{48,64},{64,48},{80,96},{96,80},{112,128},... | collective-permute-start | bytes 1572872 | tf_op jit(solution)/shard_map/ppermute | solution.py:565
  9.9 22.5 %collective-permute-start.2 = (f32[40,8,128]{2,1,0:T(8,128)S(1)}, f32[40,8,128]{2,1,0:T(8,128)S(1)}, u32[]{:S(2)}, u32[]{:S(2)}) collective-permute-start(f32[40,8,128]{2,1,0:T(8,128)S(1)} %get-tuple-element.37), channel_id=1, source_target_pairs={{0,1},{1,0},{2,3},{3,2},{4,5},{5,4},{6,7},{7,6},{8,9},{9,8},{10,11... | collective-permute-start | bytes 491528 | tf_op jit(solution)/shard_map/ppermute | solution.py:561
  9.9 22.5 %collective-permute-start.3 = (f32[40,8,128]{2,1,0:T(8,128)S(1)}, f32[40,8,128]{2,1,0:T(8,128)S(1)}, u32[]{:S(2)}, u32[]{:S(2)}) collective-permute-start(f32[40,8,128]{2,1,0:T(8,128)S(1)} %get-tuple-element.38), channel_id=1, source_target_pairs={{0,15},{1,2},{2,1},{3,4},{4,3},{5,6},{6,5},{7,8},{8,7},{9,10},{10,... | collective-permute-start | bytes 491528 | tf_op jit(solution)/shard_map/ppermute | solution.py:565
  22.7 14.8 %collective-permute-start.6 = (f32[24,8,128]{2,1,0:T(8,128)S(1)}, f32[24,8,128]{2,1,0:T(8,128)S(1)}, u32[]{:S(2)}, u32[]{:S(2)}) collective-permute-start(f32[24,8,128]{2,1,0:T(8,128)S(1)} %get-tuple-element.45.k01), channel_id=1, source_target_pairs={{0,240},{16,32},{32,16},{48,64},{64,48},{80,96},{96,80},{112,128},... | collective-permute-start | bytes 294920 | tf_op jit(solution)/shard_map/ppermute | solution.py:565
  27.7 4.7 %collective-permute-start.4 = (f32[13,8,128]{2,1,0:T(8,128)S(1)}, f32[13,8,128]{2,1,0:T(8,128)S(1)}, u32[]{:S(2)}, u32[]{:S(2)}) collective-permute-start(f32[13,8,128]{2,1,0:T(8,128)S(1)} %get-tuple-element.40), channel_id=1, source_target_pairs={{0,1},{1,0},{2,3},{3,2},{4,5},{5,4},{6,7},{7,6},{8,9},{9,8},{10,11... | collective-permute-start | bytes 159752 | tf_op jit(solution)/shard_map/ppermute | solution.py:561
  27.7 7.0 %collective-permute-start.5 = (f32[13,8,128]{2,1,0:T(8,128)S(1)}, f32[13,8,128]{2,1,0:T(8,128)S(1)}, u32[]{:S(2)}, u32[]{:S(2)}) collective-permute-start(f32[13,8,128]{2,1,0:T(8,128)S(1)} %get-tuple-element.41), channel_id=1, source_target_pairs={{0,15},{1,2},{2,1},{3,4},{4,3},{5,6},{6,5},{7,8},{8,7},{9,10},{10,... | collective-permute-start | bytes 159752 | tf_op jit(solution)/shard_map/ppermute | solution.py:565
  37.5 6.3 %collective-permute-start.7 = (f32[32,8,128]{2,1,0:T(8,128)S(1)}, f32[32,8,128]{2,1,0:T(8,128)S(1)}, u32[]{:S(2)}, u32[]{:S(2)}) collective-permute-start(f32[32,8,128]{2,1,0:T(8,128)S(1)} %pad_maximum_fusion.4), channel_id=1, source_target_pairs={{0,16},{16,0},{32,48},{48,32},{64,80},{80,64},{96,112},{112,96},{1... | collective-permute-start | bytes 393224 | tf_op jit(solution)/shard_map/ppermute | solution.py:561
  37.6 11.1 %collective-permute-start.9 = (f32[12,16,256]{2,1,0:T(8,128)S(1)}, f32[12,16,256]{2,1,0:T(8,128)S(1)}, u32[]{:S(2)}, u32[]{:S(2)}) collective-permute-start(f32[12,16,256]{2,1,0:T(8,128)S(1)} %get-tuple-element.47), channel_id=1, source_target_pairs={{0,240},{16,32},{32,16},{48,64},{64,48},{80,96},{96,80},{112,128},... | collective-permute-start | bytes 589832 | tf_op jit(solution)/shard_map/ppermute | solution.py:565
  43.8 9.2 %collective-permute-start.8 = (f32[12,16,256]{2,1,0:T(8,128)S(1)}, f32[12,16,256]{2,1,0:T(8,128)S(1)}, u32[]{:S(2)}, u32[]{:S(2)}) collective-permute-start(f32[12,16,256]{2,1,0:T(8,128)S(1)} %get-tuple-element.47), channel_id=1, source_target_pairs={{0,16},{16,0},{32,48},{48,32},{64,80},{80,64},{96,112},{112,96},{1... | collective-permute-start | bytes 589832 | tf_op jit(solution)/shard_map/ppermute | solution.py:561
  43.8 9.1 %collective-permute-start.12 = (f32[40,8,128]{2,1,0:T(8,128)S(1)}, f32[40,8,128]{2,1,0:T(8,128)S(1)}, u32[]{:S(2)}, u32[]{:S(2)}) collective-permute-start(f32[40,8,128]{2,1,0:T(8,128)S(1)} %pad_maximum_fusion.3), channel_id=1, source_target_pairs={{0,240},{16,32},{32,16},{48,64},{64,48},{80,96},{96,80},{112,128},... | collective-permute-start | bytes 491528 | tf_op jit(solution)/shard_map/ppermute | solution.py:565
  48.8 16.4 %collective-permute-start.11 = (f32[65,8,128]{2,1,0:T(8,128)S(1)}, f32[65,8,128]{2,1,0:T(8,128)S(1)}, u32[]{:S(2)}, u32[]{:S(2)}) collective-permute-start(f32[65,8,128]{2,1,0:T(8,128)S(1)} %get-tuple-element.64), channel_id=1, source_target_pairs={{0,15},{1,2},{2,1},{3,4},{4,3},{5,6},{6,5},{7,8},{8,7},{9,10},{10,... | collective-permute-start | bytes 798728 | tf_op jit(solution)/shard_map/ppermute | solution.py:565
  49.7 15.7 %collective-permute-start.10 = (f32[65,8,128]{2,1,0:T(8,128)S(1)}, f32[65,8,128]{2,1,0:T(8,128)S(1)}, u32[]{:S(2)}, u32[]{:S(2)}) collective-permute-start(f32[65,8,128]{2,1,0:T(8,128)S(1)} %get-tuple-element.65), channel_id=1, source_target_pairs={{0,1},{1,0},{2,3},{3,2},{4,5},{5,4},{6,7},{7,6},{8,9},{9,8},{10,11... | collective-permute-start | bytes 798728 | tf_op jit(solution)/shard_map/ppermute | solution.py:561
  53.0 4.3 %collective-permute-start.13 = (f32[16,8,128]{2,1,0:T(8,128)S(1)}, f32[16,8,128]{2,1,0:T(8,128)S(1)}, u32[]{:S(2)}, u32[]{:S(2)}) collective-permute-start(f32[16,8,128]{2,1,0:T(8,128)S(1)} %slice.4), channel_id=1, source_target_pairs={{0,16},{16,0},{32,48},{48,32},{64,80},{80,64},{96,112},{112,96},{1... | collective-permute-start | bytes 196616 | tf_op jit(solution)/shard_map/ppermute | solution.py:561
  53.0 13.4 %collective-permute-start.16 = (f32[72,8,128]{2,1,0:T(8,128)S(1)}, f32[72,8,128]{2,1,0:T(8,128)S(1)}, u32[]{:S(2)}, u32[]{:S(2)}) collective-permute-start(f32[72,8,128]{2,1,0:T(8,128)S(1)} %constant_dynamic-update-slice_fusion), channel_id=1, source_target_pairs={{0,15},{1,2},{2,1},{3,4},{4,3},{5,6},{6,5},{7,8},{8,7},{9,10},{10,... | collective-permute-start | bytes 884744 | tf_op jit(solution)/shard_map/ppermute | solution.py:565
  54.1 12.3 %collective-permute-start.15 = (f32[72,8,128]{2,1,0:T(8,128)S(1)}, f32[72,8,128]{2,1,0:T(8,128)S(1)}, u32[]{:S(2)}, u32[]{:S(2)}) collective-permute-start(f32[72,8,128]{2,1,0:T(8,128)S(1)} %constant_dynamic-update-slice_fusion), channel_id=1, source_target_pairs={{0,1},{1,0},{2,3},{3,2},{4,5},{5,4},{6,7},{7,6},{8,9},{9,8},{10,11... | collective-permute-start | bytes 884744 | tf_op jit(solution)/shard_map/ppermute | solution.py:561
  57.2 7.9 %collective-permute-start.14 = (f32[16,8,128]{2,1,0:T(8,128)S(1)}, f32[16,8,128]{2,1,0:T(8,128)S(1)}, u32[]{:S(2)}, u32[]{:S(2)}) collective-permute-start(f32[16,8,128]{2,1,0:T(8,128)S(1)} %collective-permute-done.13.b3), channel_id=1, source_target_pairs={{0,240},{16,32},{32,16},{48,64},{64,48},{80,96},{96,80},{112,128},... | collective-permute-start | bytes 196616 | tf_op jit(solution)/shard_map/ppermute | solution.py:565
  65.1 6.5 %collective-permute-start.18 = (f32[32,8,128]{2,1,0:T(8,128)S(1)}, f32[32,8,128]{2,1,0:T(8,128)S(1)}, u32[]{:S(2)}, u32[]{:S(2)}) collective-permute-start(f32[32,8,128]{2,1,0:T(8,128)S(1)} %constant_dynamic-update-slice_fusion.2), channel_id=1, source_target_pairs={{0,15},{1,2},{2,1},{3,4},{4,3},{5,6},{6,5},{7,8},{8,7},{9,10},{10,... | collective-permute-start | bytes 393224 | tf_op jit(solution)/shard_map/ppermute | solution.py:565
  65.2 6.5 %collective-permute-start.17 = (f32[32,8,128]{2,1,0:T(8,128)S(1)}, f32[32,8,128]{2,1,0:T(8,128)S(1)}, u32[]{:S(2)}, u32[]{:S(2)}) collective-permute-start(f32[32,8,128]{2,1,0:T(8,128)S(1)} %constant_dynamic-update-slice_fusion.2), channel_id=1, source_target_pairs={{0,1},{1,0},{2,3},{3,2},{4,5},{5,4},{6,7},{7,6},{8,9},{9,8},{10,11... | collective-permute-start | bytes 393224 | tf_op jit(solution)/shard_map/ppermute | solution.py:561
  74.7 4.2 %collective-permute-start.19 = (f32[3,2,16,128]{3,2,1,0:T(8,128)S(1)}, f32[3,2,16,128]{3,2,1,0:T(8,128)S(1)}, u32[]{:S(2)}, u32[]{:S(2)}) collective-permute-start(f32[3,2,16,128]{3,2,1,0:T(8,128)S(1)} %get-tuple-element.59), channel_id=1, source_target_pairs={{0,16},{16,0},{32,48},{48,32},{64,80},{80,64},{96,112},{112,96},{1... | collective-permute-start | bytes 147464 | tf_op jit(solution)/shard_map/ppermute | solution.py:561

commit v8 on v6

--- a/solution.py
+++ b/solution.py
@@ -357,7 +357,7 @@
                 to[16:24, :] = jnp.where(up, b, a)
             return carry
 
-        lax.fori_loop(0, 4 if force else 6, fill, 0, unroll=2)
+        lax.fori_loop(0, 4 if force else 6, fill, 0, unroll=True)
 
 
 def coarse_blocks(pos, eb, ob, k01, k23, r1e, r1o, rme, rmo, gk, ki, k3):

time: 81.8 us -> 81.7 us (level)
  no operation moved by 1% of the time
where the time goes in v8:
time: 81.7 us; the launch traced here: 81.6 us
  waiting for transfers between devices  41.7 us (51%)
  starting transfers between devices  25 us (31%)
  Pallas kernels  13.7 us (17%)
  between operations  0.89 us (1%)
    ppermute x10, waiting for transfers between devices, swap_odd(): return lax.ppermute(x, axis, ODD)  30.7 us
    ppermute x10, starting transfers between devices, swap_odd(): return lax.ppermute(x, axis, ODD)  22.6 us
    pallas_call x7, Pallas kernels, call(): pl.pallas_call(kernel, out_shape=[jax.ShapeDtypeStruct(x, F32) for x in o...  13.7 us
    ppermute x10, waiting for transfers between devices, swap_even(): return lax.ppermute(x, axis, EVEN)  11 us
    ppermute x10, starting transfers between devices, swap_even(): return lax.ppermute(x, axis, EVEN)  2.38 us
  transfers between devices with their start and end apart: 20, of which 10 were waited for; matrix products, arithmetic and copies ran while one was open for 0% of the time, Pallas kernels for 7%

profile of v8, /device:TPU:0, one launch (start us, length us, event | category | flops | bytes accessed | tf_op | source)
XLA Modules:
  0.0 81.6 jit_solution(17465182162580149221)
XLA Ops:
  0.6 0.0 copy-start.4
  0.6 0.0 copy-start.1
  0.7 0.0 copy-start
  0.7 0.0 copy-start.7
  0.7 0.0 copy-start.6
  0.7 0.0 copy-start.5
  0.7 0.0 copy-start.3
  0.7 0.0 copy-start.2
  0.7 0.1 pad_add_fusion.pos
  0.8 2.2 %shard_map.95 = (f32[6,4,16,256]{3,2,1,0:T(8,128)S(1)}, f32[4,16,256]{2,1,0:T(8,128)S(1)}, f32[35,16,256]{2,1,0:T(8,128)S(1)}, f32[32,16,256]{2,1,0:T(8,128)S(1)...) custom-call(s32[2]{0:T(128)S(1)} %pad_add_fusion.pos, f32[3,4,16,256]{3,2,1,0:T(8,128)} %disp.1, ...), custom_call_target="tpu_custom_call" | custom-call | tf_op jit(solution)/shard_map/pallas_call | solution.py:546
  3.0 0.3 collective-permute-start
  3.2 7.4 %collective-permute-start.1 = (f32[32,16,256]{2,1,0:T(8,128)S(1)}, f32[32,16,256]{2,1,0:T(8,128)S(1)}, u32[]{:S(2)}, u32[]{:S(2)}) collective-permute-start(f32[32,16,256]{2,1,0:T(8,128)S(1)} %get-tuple-element.34), channel_id=1, source_target_pairs={{0,240},{16,32},{32,16},{48,64},{64,48},{80,96},{96,80},{112,128},... | collective-permute-start | bytes 1572872 | tf_op jit(solution)/shard_map/ppermute | solution.py:565
  10.7 0.0 collective-permute-start.2
  10.7 3.2 %collective-permute-start.3 = (f32[40,8,128]{2,1,0:T(8,128)S(1)}, f32[40,8,128]{2,1,0:T(8,128)S(1)}, u32[]{:S(2)}, u32[]{:S(2)}) collective-permute-start(f32[40,8,128]{2,1,0:T(8,128)S(1)} %get-tuple-element.36), channel_id=1, source_target_pairs={{0,15},{1,2},{2,1},{3,4},{4,3},{5,6},{6,5},{7,8},{8,7},{9,10},{10,... | collective-permute-start | bytes 491528 | tf_op jit(solution)/shard_map/ppermute | solution.py:565
  13.8 8.6 %collective-permute-done.1.ro = f32[32,16,256]{2,1,0:T(8,128)S(1)} collective-permute-done((f32[32,16,256]{2,1,0:T(8,128)S(1)}, f32[32,16,256]{2,1,0:T(8,128)S(1)}, u32[]{:S(2)}, u32[]{:S(2)}) %collective-permute-start.1) | collective-permute-done | bytes 524320 | tf_op jit(solution)/shard_map/ppermute | solution.py:565
  22.4 0.0 collective-permute-done.re
  22.4 0.6 shard_map.96
  23.0 5.4 %collective-permute-start.6 = (f32[24,8,128]{2,1,0:T(8,128)S(1)}, f32[24,8,128]{2,1,0:T(8,128)S(1)}, u32[]{:S(2)}, u32[]{:S(2)}) collective-permute-start(f32[24,8,128]{2,1,0:T(8,128)S(1)} %get-tuple-element.42.k01), channel_id=1, source_target_pairs={{0,240},{16,32},{32,16},{48,64},{64,48},{80,96},{96,80},{112,128},... | collective-permute-start | bytes 294920 | tf_op jit(solution)/shard_map/ppermute | solution.py:565
  28.5 3.2 %collective-permute-start.5 = (f32[13,8,128]{2,1,0:T(8,128)S(1)}, f32[13,8,128]{2,1,0:T(8,128)S(1)}, u32[]{:S(2)}, u32[]{:S(2)}) collective-permute-start(f32[13,8,128]{2,1,0:T(8,128)S(1)} %get-tuple-element.39), channel_id=1, source_target_pairs={{0,15},{1,2},{2,1},{3,4},{4,3},{5,6},{6,5},{7,8},{8,7},{9,10},{10,... | collective-permute-start | bytes 159752 | tf_op jit(solution)/shard_map/ppermute | solution.py:565
  31.6 0.0 collective-permute-done.2.be
  31.6 0.0 collective-permute-done.3.bo
  31.6 0.0 collective-permute-done.4.ce
  31.6 2.5 %collective-permute-done.5.co = f32[13,8,128]{2,1,0:T(8,128)S(1)} collective-permute-done((f32[13,8,128]{2,1,0:T(8,128)S(1)}, f32[13,8,128]{2,1,0:T(8,128)S(1)}, u32[]{:S(2)}, u32[]{:S(2)}) %collective-permute-start.5) | collective-permute-done | bytes 53280 | tf_op jit(solution)/shard_map/ppermute | solution.py:565
  34.2 2.7 %shard_map.97 = (f32[3,8,24,256]{3,2,1,0:T(8,128)S(1)}, f32[6,8,24,256]{3,2,1,0:T(8,128)S(1)}, f32[8,24,256]{2,1,0:T(8,128)S(1)}, f32[3,6,24,256]{3,2,1,0:T(8,12...) custom-call(s32[2]{0:T(128)S(1)} %pad_add_fusion.pos, ...), custom_call_target="tpu_custom_call" | custom-call | tf_op jit(solution)/shard_map/pallas_call | solution.py:546
  36.9 0.1 collective-permute-start.7
  37.0 0.4 collective-permute-start.9
  37.4 1.6 %collective-permute-start.8 = (f32[12,16,256]{2,1,0:T(8,128)S(1)}, f32[12,16,256]{2,1,0:T(8,128)S(1)}, u32[]{:S(2)}, u32[]{:S(2)}) collective-permute-start(f32[12,16,256]{2,1,0:T(8,128)S(1)} %get-tuple-element.43), channel_id=1, source_target_pairs={{0,16},{16,0},{32,48},{48,32},{64,80},{80,64},{96,112},{112,96},{1... | collective-permute-start | bytes 589832 | tf_op jit(solution)/shard_map/ppermute | solution.py:561
  39.0 4.3 %collective-permute-done.7.eb = f32[32,8,128]{2,1,0:T(8,128)S(1)} collective-permute-done((f32[32,8,128]{2,1,0:T(8,128)S(1)}, f32[32,8,128]{2,1,0:T(8,128)S(1)}, u32[]{:S(2)}, u32[]{:S(2)}) %collective-permute-start.7) | collective-permute-done | bytes 131104 | tf_op jit(solution)/shard_map/ppermute | solution.py:561
  43.3 0.1 collective-permute-start.12
  43.4 3.5 %collective-permute-done.9.go = f32[12,16,256]{2,1,0:T(8,128)S(1)} collective-permute-done((f32[12,16,256]{2,1,0:T(8,128)S(1)}, f32[12,16,256]{2,1,0:T(8,128)S(1)}, u32[]{:S(2)}, u32[]{:S(2)}) %collective-permute-start.9) | collective-permute-done | bytes 196640 | tf_op jit(solution)/shard_map/ppermute | solution.py:565
  47.0 0.0 collective-permute-done.8.ge
  47.0 2.0 %collective-permute-start.11 = (f32[65,8,128]{2,1,0:T(8,128)S(1)}, f32[65,8,128]{2,1,0:T(8,128)S(1)}, u32[]{:S(2)}, u32[]{:S(2)}) collective-permute-start(f32[65,8,128]{2,1,0:T(8,128)S(1)} %get-tuple-element.60), channel_id=1, source_target_pairs={{0,15},{1,2},{2,1},{3,4},{4,3},{5,6},{6,5},{7,8},{8,7},{9,10},{10,... | collective-permute-start | bytes 798728 | tf_op jit(solution)/shard_map/ppermute | solution.py:565
  49.0 0.0 collective-permute-start.10
  49.0 3.5 %collective-permute-done.12.ob = f32[40,8,128]{2,1,0:T(8,128)S(1)} collective-permute-done((f32[40,8,128]{2,1,0:T(8,128)S(1)}, f32[40,8,128]{2,1,0:T(8,128)S(1)}, u32[]{:S(2)}, u32[]{:S(2)}) %collective-permute-start.12) | collective-permute-done | bytes 163872 | tf_op jit(solution)/shard_map/ppermute | solution.py:565
  52.5 1.0 %collective-permute-start.16 = (f32[72,8,128]{2,1,0:T(8,128)S(1)}, f32[72,8,128]{2,1,0:T(8,128)S(1)}, u32[]{:S(2)}, u32[]{:S(2)}) collective-permute-start(f32[72,8,128]{2,1,0:T(8,128)S(1)} %constant_dynamic-update-slice_fusion), channel_id=1, source_target_pairs={{0,15},{1,2},{2,1},{3,4},{4,3},{5,6},{6,5},{7,8},{8,7},{9,10},{10,... | collective-permute-start | bytes 884744 | tf_op jit(solution)/shard_map/ppermute | solution.py:565
  53.5 0.0 collective-permute-start.15
  53.5 3.3 %collective-permute-done.13.b3 = f32[16,8,128]{2,1,0:T(8,128)S(1)} collective-permute-done((f32[16,8,128]{2,1,0:T(8,128)S(1)}, f32[16,8,128]{2,1,0:T(8,128)S(1)}, u32[]{:S(2)}, u32[]{:S(2)}) %collective-permute-start.13) | collective-permute-done | bytes 65568 | tf_op jit(solution)/shard_map/ppermute | solution.py:561
  56.7 0.0 collective-permute-start.14
  56.7 8.0 %collective-permute-done.14.b4 = f32[16,8,128]{2,1,0:T(8,128)S(1)} collective-permute-done((f32[16,8,128]{2,1,0:T(8,128)S(1)}, f32[16,8,128]{2,1,0:T(8,128)S(1)}, u32[]{:S(2)}, u32[]{:S(2)}) %collective-permute-start.14) | collective-permute-done | bytes 65568 | tf_op jit(solution)/shard_map/ppermute | solution.py:565
  64.7 0.3 collective-permute-start.17
  65.0 0.1 collective-permute-done.16.rmo
  65.2 1.4 %shard_map.99 = (f32[6,16,24,128]{3,2,1,0:T(8,128)S(1)}, f32[6,16,24,128]{3,2,1,0:T(8,128)S(1)}, f32[6,8,24,128]{3,2,1,0:T(8,128)S(1)}) custom-call(s32[2]{0:T(128)S(1)} %pad_add_fusion.pos, f32[32,8,128]{2,1,0:T(8,128)S(1)} %collective-permute-done.7.eb, f32[40,8,128]{2,1,0:T(8,128)S(1)} %collective-permute-done.12.ob, ...), custom_call_target="tpu_custom_call" | custom-call | tf_op jit(solution)/shard_map/pallas_call | solution.py:546
  66.6 4.6 %collective-permute-done.18.r2o = f32[32,8,128]{2,1,0:T(8,128)S(1)} collective-permute-done((f32[32,8,128]{2,1,0:T(8,128)S(1)}, f32[32,8,128]{2,1,0:T(8,128)S(1)}, u32[]{:S(2)}, u32[]{:S(2)}) %collective-permute-start.18) | collective-permute-done | bytes 131104 | tf_op jit(solution)/shard_map/ppermute | solution.py:565
  71.2 3.1 %shard_map.100 = (f32[3,4,16,128]{3,2,1,0:T(8,128)S(1)}, f32[3,2,16,128]{3,2,1,0:T(8,128)S(1)}) custom-call(s32[2]{0:T(128)S(1)} %pad_add_fusion.pos, f32[8,8,128]{2,1,0:T(8,128)S(1)} %get-tuple-element.46.b0, f32[32,8,128]{2,1,0:T(8,128)S(1)} %collective-permute-done.7.eb, f32[40,8,128]{2,1,0:T(8,128)S(1)} %collective-permute-done.12.ob, ...), custom_call_target="tpu_custom_call" | custom-call | tf_op jit(solution)/shard_map/pallas_call | solution.py:546
  74.4 0.1 collective-permute-start.19
  74.5 0.7 shard_map.98
  75.1 3.4 %collective-permute-done.19.other = f32[3,2,16,128]{3,2,1,0:T(8,128)S(1)} collective-permute-done((f32[3,2,16,128]{3,2,1,0:T(8,128)S(1)}, f32[3,2,16,128]{3,2,1,0:T(8,128)S(1)}, u32[]{:S(2)}, u32[]{:S(2)}) %collective-permute-start.19) | collective-permute-done | bytes 49184 | tf_op jit(solution)/shard_map/ppermute | solution.py:561
  78.5 3.0 %shard_map.101 = (f32[3,4,16,256]{3,2,1,0:T(8,128)}, f32[3,4,16,256]{3,2,1,0:T(8,128)}) custom-call(s32[2]{0:T(128)S(1)} %pad_add_fusion.pos, f32[3,10,24,256]{3,2,1,0:T(8,128)S(1)} %get-tuple-element.49.held, f32[3,4,16,128]{3,2,1,0:T(8,128)S(1)} %get-tuple-element.54.mid2, f32[3,2,16,128]{3,2,1,0:T(8,128)S(1)} %collective-permute-done.19.other, ...), custom_call_target="tpu_custom_call" | custom-call | tf_op jit(solution)/shard_map/pallas_call | solution.py:546
  (24 shorter events, 0.1 us)
Async XLA Ops:
  0.6 33.5 %copy-start.4 = (s32[4,16,256]{2,1,0:T(8,128)S(1)}, s32[4,16,256]{2,1,0:T(8,128)}, u32[]{:S(2)}) copy-start(s32[4,16,256]{2,1,0:T(8,128)} %clip.3) | copy-start | bytes 196612
  0.6 33.5 %copy-start.1 = (f32[3,4,16,256]{3,2,1,0:T(8,128)S(1)}, f32[3,4,16,256]{3,2,1,0:T(8,128)}, u32[]{:S(2)}) copy-start(f32[3,4,16,256]{3,2,1,0:T(8,128)} %cross.3) | copy-start | bytes 589828
  0.7 33.5 %copy-start = (f32[3,4,16,256]{3,2,1,0:T(8,128)S(1)}, f32[3,4,16,256]{3,2,1,0:T(8,128)}, u32[]{:S(2)}) copy-start(f32[3,4,16,256]{3,2,1,0:T(8,128)} %main.3) | copy-start | bytes 589828
  0.7 33.5 %copy-start.7 = (s32[4,16,256]{2,1,0:T(8,128)S(1)}, s32[4,16,256]{2,1,0:T(8,128)}, u32[]{:S(2)}) copy-start(s32[4,16,256]{2,1,0:T(8,128)} %touch.1) | copy-start | bytes 196612
  0.7 33.5 %copy-start.6 = (f32[4,16,256]{2,1,0:T(8,128)S(1)}, f32[4,16,256]{2,1,0:T(8,128)}, u32[]{:S(2)}) copy-start(f32[4,16,256]{2,1,0:T(8,128)} %clear.1) | copy-start | bytes 196612
  0.7 33.5 %copy-start.5 = (f32[4,16,256]{2,1,0:T(8,128)S(1)}, f32[4,16,256]{2,1,0:T(8,128)}, u32[]{:S(2)}) copy-start(f32[4,16,256]{2,1,0:T(8,128)} %heat.1) | copy-start | bytes 196612
  0.7 33.5 %copy-start.3 = (f32[3,4,16,256]{3,2,1,0:T(8,128)S(1)}, f32[3,4,16,256]{3,2,1,0:T(8,128)}, u32[]{:S(2)}) copy-start(f32[3,4,16,256]{3,2,1,0:T(8,128)} %trac.1) | copy-start | bytes 589828
  0.7 33.5 %copy-start.2 = (f32[3,4,16,256]{3,2,1,0:T(8,128)S(1)}, f32[3,4,16,256]{3,2,1,0:T(8,128)}, u32[]{:S(2)}) copy-start(f32[3,4,16,256]{3,2,1,0:T(8,128)} %disp.1) | copy-start | bytes 589828
  3.0 19.4 %collective-permute-start = (f32[35,16,256]{2,1,0:T(8,128)S(1)}, f32[35,16,256]{2,1,0:T(8,128)S(1)}, u32[]{:S(2)}, u32[]{:S(2)}) collective-permute-start(f32[35,16,256]{2,1,0:T(8,128)S(1)} %get-tuple-element.33), channel_id=1, source_target_pairs={{0,16},{16,0},{32,48},{48,32},{64,80},{80,64},{96,112},{112,96},{1... | collective-permute-start | bytes 1720328 | tf_op jit(solution)/shard_map/ppermute | solution.py:561
  3.2 19.1 %collective-permute-start.1 = (f32[32,16,256]{2,1,0:T(8,128)S(1)}, f32[32,16,256]{2,1,0:T(8,128)S(1)}, u32[]{:S(2)}, u32[]{:S(2)}) collective-permute-start(f32[32,16,256]{2,1,0:T(8,128)S(1)} %get-tuple-element.34), channel_id=1, source_target_pairs={{0,240},{16,32},{32,16},{48,64},{64,48},{80,96},{96,80},{112,128},... | collective-permute-start | bytes 1572872 | tf_op jit(solution)/shard_map/ppermute | solution.py:565
  10.7 21.0 %collective-permute-start.2 = (f32[40,8,128]{2,1,0:T(8,128)S(1)}, f32[40,8,128]{2,1,0:T(8,128)S(1)}, u32[]{:S(2)}, u32[]{:S(2)}) collective-permute-start(f32[40,8,128]{2,1,0:T(8,128)S(1)} %get-tuple-element.35), channel_id=1, source_target_pairs={{0,1},{1,0},{2,3},{3,2},{4,5},{5,4},{6,7},{7,6},{8,9},{9,8},{10,11... | collective-permute-start | bytes 491528 | tf_op jit(solution)/shard_map/ppermute | solution.py:561
  10.7 21.0 %collective-permute-start.3 = (f32[40,8,128]{2,1,0:T(8,128)S(1)}, f32[40,8,128]{2,1,0:T(8,128)S(1)}, u32[]{:S(2)}, u32[]{:S(2)}) collective-permute-start(f32[40,8,128]{2,1,0:T(8,128)S(1)} %get-tuple-element.36), channel_id=1, source_target_pairs={{0,15},{1,2},{2,1},{3,4},{4,3},{5,6},{6,5},{7,8},{8,7},{9,10},{10,... | collective-permute-start | bytes 491528 | tf_op jit(solution)/shard_map/ppermute | solution.py:565
  23.0 13.9 %collective-permute-start.6 = (f32[24,8,128]{2,1,0:T(8,128)S(1)}, f32[24,8,128]{2,1,0:T(8,128)S(1)}, u32[]{:S(2)}, u32[]{:S(2)}) collective-permute-start(f32[24,8,128]{2,1,0:T(8,128)S(1)} %get-tuple-element.42.k01), channel_id=1, source_target_pairs={{0,240},{16,32},{32,16},{48,64},{64,48},{80,96},{96,80},{112,128},... | collective-permute-start | bytes 294920 | tf_op jit(solution)/shard_map/ppermute | solution.py:565
  28.5 3.2 %collective-permute-start.4 = (f32[13,8,128]{2,1,0:T(8,128)S(1)}, f32[13,8,128]{2,1,0:T(8,128)S(1)}, u32[]{:S(2)}, u32[]{:S(2)}) collective-permute-start(f32[13,8,128]{2,1,0:T(8,128)S(1)} %get-tuple-element.38), channel_id=1, source_target_pairs={{0,1},{1,0},{2,3},{3,2},{4,5},{5,4},{6,7},{7,6},{8,9},{9,8},{10,11... | collective-permute-start | bytes 159752 | tf_op jit(solution)/shard_map/ppermute | solution.py:561
  28.5 5.7 %collective-permute-start.5 = (f32[13,8,128]{2,1,0:T(8,128)S(1)}, f32[13,8,128]{2,1,0:T(8,128)S(1)}, u32[]{:S(2)}, u32[]{:S(2)}) collective-permute-start(f32[13,8,128]{2,1,0:T(8,128)S(1)} %get-tuple-element.39), channel_id=1, source_target_pairs={{0,15},{1,2},{2,1},{3,4},{4,3},{5,6},{6,5},{7,8},{8,7},{9,10},{10,... | collective-permute-start | bytes 159752 | tf_op jit(solution)/shard_map/ppermute | solution.py:565
  36.9 6.4 %collective-permute-start.7 = (f32[32,8,128]{2,1,0:T(8,128)S(1)}, f32[32,8,128]{2,1,0:T(8,128)S(1)}, u32[]{:S(2)}, u32[]{:S(2)}) collective-permute-start(f32[32,8,128]{2,1,0:T(8,128)S(1)} %pad_maximum_fusion.4), channel_id=1, source_target_pairs={{0,16},{16,0},{32,48},{48,32},{64,80},{80,64},{96,112},{112,96},{1... | collective-permute-start | bytes 393224 | tf_op jit(solution)/shard_map/ppermute | solution.py:561
  37.0 9.9 %collective-permute-start.9 = (f32[12,16,256]{2,1,0:T(8,128)S(1)}, f32[12,16,256]{2,1,0:T(8,128)S(1)}, u32[]{:S(2)}, u32[]{:S(2)}) collective-permute-start(f32[12,16,256]{2,1,0:T(8,128)S(1)} %get-tuple-element.43), channel_id=1, source_target_pairs={{0,240},{16,32},{32,16},{48,64},{64,48},{80,96},{96,80},{112,128},... | collective-permute-start | bytes 589832 | tf_op jit(solution)/shard_map/ppermute | solution.py:565
  37.4 9.6 %collective-permute-start.8 = (f32[12,16,256]{2,1,0:T(8,128)S(1)}, f32[12,16,256]{2,1,0:T(8,128)S(1)}, u32[]{:S(2)}, u32[]{:S(2)}) collective-permute-start(f32[12,16,256]{2,1,0:T(8,128)S(1)} %get-tuple-element.43), channel_id=1, source_target_pairs={{0,16},{16,0},{32,48},{48,32},{64,80},{80,64},{96,112},{112,96},{1... | collective-permute-start | bytes 589832 | tf_op jit(solution)/shard_map/ppermute | solution.py:561
  43.3 9.1 %collective-permute-start.12 = (f32[40,8,128]{2,1,0:T(8,128)S(1)}, f32[40,8,128]{2,1,0:T(8,128)S(1)}, u32[]{:S(2)}, u32[]{:S(2)}) collective-permute-start(f32[40,8,128]{2,1,0:T(8,128)S(1)} %pad_maximum_fusion.3), channel_id=1, source_target_pairs={{0,240},{16,32},{32,16},{48,64},{64,48},{80,96},{96,80},{112,128},... | collective-permute-start | bytes 491528 | tf_op jit(solution)/shard_map/ppermute | solution.py:565
  47.0 17.7 %collective-permute-start.11 = (f32[65,8,128]{2,1,0:T(8,128)S(1)}, f32[65,8,128]{2,1,0:T(8,128)S(1)}, u32[]{:S(2)}, u32[]{:S(2)}) collective-permute-start(f32[65,8,128]{2,1,0:T(8,128)S(1)} %get-tuple-element.60), channel_id=1, source_target_pairs={{0,15},{1,2},{2,1},{3,4},{4,3},{5,6},{6,5},{7,8},{8,7},{9,10},{10,... | collective-permute-start | bytes 798728 | tf_op jit(solution)/shard_map/ppermute | solution.py:565
  49.0 16.0 %collective-permute-start.10 = (f32[65,8,128]{2,1,0:T(8,128)S(1)}, f32[65,8,128]{2,1,0:T(8,128)S(1)}, u32[]{:S(2)}, u32[]{:S(2)}) collective-permute-start(f32[65,8,128]{2,1,0:T(8,128)S(1)} %get-tuple-element.61), channel_id=1, source_target_pairs={{0,1},{1,0},{2,3},{3,2},{4,5},{5,4},{6,7},{7,6},{8,9},{9,8},{10,11... | collective-permute-start | bytes 798728 | tf_op jit(solution)/shard_map/ppermute | solution.py:561
  52.5 4.3 %collective-permute-start.13 = (f32[16,8,128]{2,1,0:T(8,128)S(1)}, f32[16,8,128]{2,1,0:T(8,128)S(1)}, u32[]{:S(2)}, u32[]{:S(2)}) collective-permute-start(f32[16,8,128]{2,1,0:T(8,128)S(1)} %slice.4), channel_id=1, source_target_pairs={{0,16},{16,0},{32,48},{48,32},{64,80},{80,64},{96,112},{112,96},{1... | collective-permute-start | bytes 196616 | tf_op jit(solution)/shard_map/ppermute | solution.py:561
  52.5 12.7 %collective-permute-start.16 = (f32[72,8,128]{2,1,0:T(8,128)S(1)}, f32[72,8,128]{2,1,0:T(8,128)S(1)}, u32[]{:S(2)}, u32[]{:S(2)}) collective-permute-start(f32[72,8,128]{2,1,0:T(8,128)S(1)} %constant_dynamic-update-slice_fusion), channel_id=1, source_target_pairs={{0,15},{1,2},{2,1},{3,4},{4,3},{5,6},{6,5},{7,8},{8,7},{9,10},{10,... | collective-permute-start | bytes 884744 | tf_op jit(solution)/shard_map/ppermute | solution.py:565
  53.5 11.7 %collective-permute-start.15 = (f32[72,8,128]{2,1,0:T(8,128)S(1)}, f32[72,8,128]{2,1,0:T(8,128)S(1)}, u32[]{:S(2)}, u32[]{:S(2)}) collective-permute-start(f32[72,8,128]{2,1,0:T(8,128)S(1)} %constant_dynamic-update-slice_fusion), channel_id=1, source_target_pairs={{0,1},{1,0},{2,3},{3,2},{4,5},{5,4},{6,7},{7,6},{8,9},{9,8},{10,11... | collective-permute-start | bytes 884744 | tf_op jit(solution)/shard_map/ppermute | solution.py:561
  56.7 8.0 %collective-permute-start.14 = (f32[16,8,128]{2,1,0:T(8,128)S(1)}, f32[16,8,128]{2,1,0:T(8,128)S(1)}, u32[]{:S(2)}, u32[]{:S(2)}) collective-permute-start(f32[16,8,128]{2,1,0:T(8,128)S(1)} %collective-permute-done.13.b3), channel_id=1, source_target_pairs={{0,240},{16,32},{32,16},{48,64},{64,48},{80,96},{96,80},{112,128},... | collective-permute-start | bytes 196616 | tf_op jit(solution)/shard_map/ppermute | solution.py:565
  64.7 6.5 %collective-permute-start.18 = (f32[32,8,128]{2,1,0:T(8,128)S(1)}, f32[32,8,128]{2,1,0:T(8,128)S(1)}, u32[]{:S(2)}, u32[]{:S(2)}) collective-permute-start(f32[32,8,128]{2,1,0:T(8,128)S(1)} %constant_dynamic-update-slice_fusion.2), channel_id=1, source_target_pairs={{0,15},{1,2},{2,1},{3,4},{4,3},{5,6},{6,5},{7,8},{8,7},{9,10},{10,... | collective-permute-start | bytes 393224 | tf_op jit(solution)/shard_map/ppermute | solution.py:565
  64.7 6.5 %collective-permute-start.17 = (f32[32,8,128]{2,1,0:T(8,128)S(1)}, f32[32,8,128]{2,1,0:T(8,128)S(1)}, u32[]{:S(2)}, u32[]{:S(2)}) collective-permute-start(f32[32,8,128]{2,1,0:T(8,128)S(1)} %constant_dynamic-update-slice_fusion.2), channel_id=1, source_target_pairs={{0,1},{1,0},{2,3},{3,2},{4,5},{5,4},{6,7},{7,6},{8,9},{9,8},{10,11... | collective-permute-start | bytes 393224 | tf_op jit(solution)/shard_map/ppermute | solution.py:561
  74.4 4.2 %collective-permute-start.19 = (f32[3,2,16,128]{3,2,1,0:T(8,128)S(1)}, f32[3,2,16,128]{3,2,1,0:T(8,128)S(1)}, u32[]{:S(2)}, u32[]{:S(2)}) collective-permute-start(f32[3,2,16,128]{3,2,1,0:T(8,128)S(1)} %get-tuple-element.55), channel_id=1, source_target_pairs={{0,16},{16,0},{32,48},{48,32},{64,80},{80,64},{96,112},{112,96},{1... | collective-permute-start | bytes 147464 | tf_op jit(solution)/shard_map/ppermute | solution.py:561
